TPU v7x, 128 devices: a whole 4x4x4 slice. The times are simulated.
128 devices in a mesh: track: 8 (over z, core), cross: 16 (over y, x).
Axes of the slice: x: 4, y: 4, z: 4, core: 2. Of those that a mesh axis runs over, the one named last changes fastest.
Arguments:
- direction: float32 [3, 128, 1024, 256], P(None, 'track', 'cross'), may hold values from -6 to 6
- wind: float32 [3, 128, 1024, 256], P(None, 'track', 'cross'), may hold values from -5 to 5
- wind_gradient: float32 [9, 128, 1024, 256], P(None, 'track', 'cross'), may hold values from -3 to 3
- viscosity: float32 [128, 1024, 256], P('track', 'cross'), may hold values from 0.1 to 0.5
- sample_owner: int32 [8, 16, 8192, 1], P('track', 'cross'), may hold values from 0 to 127; in each aligned block of 8192 rows (0 to 8191, 8192 to 16383, ..., all dimensions but the last counted through in order) at most 128 rows name the same one
- sample_cell: int32 [8, 16, 8192], P('track', 'cross'), may hold values from 0 to 262143
- sample_gate: int32 [8, 16, 8192], P('track', 'cross'), may hold values from 0 to 1023
- sight: float32 [3, 128, 1024], P(None, ('track', 'cross')), may hold values from -1.5 to 1.5
- gate_counts: int32 [128, 8], P(('track', 'cross')), may hold values from 1 to 128, 768 in all within a row
- precision: float32 [128, 128, 128], P(('track', 'cross')), as said below
Outputs:
- hessian_product: float32 [3, 128, 1024, 256], P(None, 'track', 'cross')
- weighted_obs: float32 [128, 1024], P(('track', 'cross'))
Inputs may be any that keep to these rules, and one draw needn't show every extreme that they name: `sample_owner`: among the 8192 samples of one device no lidar is named more than 128 times, a bound that some block reaches. `gate_counts`: each lidar's counts sum to 768, and the largest is 128. `precision`: each matrix is symmetric with a diagonal that exceeds its row's other entries in sum of magnitudes.
All inputs are finite; a program needn't handle non-finite values.
Results may differ from a plain program's by a relative error of at most 0.0003.
Values sent between devices are 32-bit elements; how exact they have to be, the bound alone decides.
No kernel may reach another device: no remote copies, remote signals or barrier semaphores. Data moves between devices by JAX's collectives and lax.ppermute only.
A program may use at most 384 MiB of HBM per device.

v0:
```python
import jax
import jax.numpy as jnp
from jax import lax
from jax.sharding import PartitionSpec as P

time_step = 0.2
highest = lax.Precision.HIGHEST


def with_halo(cells, sides, width):
    for axis, dim in sides:
        count = lax.axis_size(axis)
        ends = count - 1
        head = lax.slice_in_dim(cells, 0, width, axis=dim)
        tail = lax.slice_in_dim(cells, cells.shape[dim] - width, cells.shape[dim], axis=dim)
        cells = jnp.concatenate(
            [
                lax.ppermute(tail, axis, [(i, (i + 1) % count) for i in range(ends)]),
                cells,
                lax.ppermute(head, axis, [((i + 1) % count, i) for i in range(ends)]),
            ],
            axis=dim,
        )
    return cells


def pad_depth(field):
    return jnp.pad(field, ((0, 0), (0, 0), (0, 0), (1, 1)))


def along_x(padded):
    return (padded[:, 2:, 1:-1] - padded[:, :-2, 1:-1]) * 0.5


def along_y(padded):
    return (padded[:, 1:-1, 2:] - padded[:, 1:-1, :-2]) * 0.5


def along_z(field):
    deep = pad_depth(field)
    return (deep[..., 2:] - deep[..., :-2]) * 0.5


def near_sum(padded, field):
    deep = pad_depth(field)
    total = padded[:, 2:, 1:-1] + padded[:, :-2, 1:-1] + padded[:, 1:-1, 2:] + padded[:, 1:-1, :-2]
    return total + deep[..., 2:] + deep[..., :-2]


def indicator(index, width, dtype):
    return (index[:, None] == jnp.arange(width, dtype=jnp.int32)[None, :]).astype(dtype)


def owner_ranks(owner, owning_ranks):
    count_all = owner.shape[0]
    group = 128
    nblocks = count_all // group
    marks = indicator(owner, owning_ranks, jnp.bfloat16).reshape(nblocks, group, owning_ranks)
    steps = jnp.arange(group, dtype=jnp.int32)
    lower = (steps[:, None] > steps[None, :]).astype(jnp.bfloat16)
    within = jnp.einsum("st,bto->bso", lower, marks, preferred_element_type=jnp.float32)
    block_counts = jnp.sum(marks.astype(jnp.float32), axis=1)
    order_blocks = jnp.arange(nblocks, dtype=jnp.int32)
    earlier = (order_blocks[:, None] > order_blocks[None, :]).astype(jnp.float32)
    offsets = jnp.dot(earlier, block_counts, precision=highest, preferred_element_type=jnp.float32)
    ranks = jnp.sum(marks.astype(jnp.float32) * (within + offsets[:, None, :]), axis=-1)
    return ranks.reshape(count_all).astype(jnp.int32)


def body(
    direction,
    wind,
    wind_gradient,
    viscosity,
    sample_owner,
    sample_cell,
    sample_gate,
    sight,
    gate_counts,
    precision,
):
    n_track = lax.axis_size("track")
    n_cross = lax.axis_size("cross")
    owning_ranks = n_track * n_cross
    s_dev = sample_cell.shape[2]
    slot_capacity = max(4, 2 * s_dev // owning_ranks)
    obs = sight.shape[2]
    beams = gate_counts.shape[1]
    gates_each = precision.shape[1]
    padded = with_halo(direction, (("track", 1), ("cross", 2)), 1)
    adv = wind[0] * along_x(padded) + wind[1] * along_y(padded) + wind[2] * along_z(direction)
    gq = jnp.stack(
        [
            wind_gradient[3 * i] * direction[0]
            + wind_gradient[3 * i + 1] * direction[1]
            + wind_gradient[3 * i + 2] * direction[2]
            for i in range(3)
        ]
    )
    tangent = direction + time_step * (
        -adv - gq + viscosity * (near_sum(padded, direction) - 6.0 * direction)
    )
    owner = sample_owner.reshape(-1)
    cells = sample_cell.reshape(-1)
    gates = sample_gate.reshape(-1)
    ranks = owner_ranks(owner, owning_ranks)
    slot_index = owner * slot_capacity + ranks
    slot_count = owning_ranks * slot_capacity
    picked_values = tangent.reshape(3, -1)[:, cells]
    items = jnp.concatenate([picked_values, (gates + 1).astype(jnp.float32)[None, :]], axis=0)
    sent = (
        jnp.zeros((4, slot_count), jnp.float32)
        .at[:, slot_index]
        .add(items)
        .reshape(4, owning_ranks, slot_capacity)
    )
    received_values = lax.all_to_all(
        sent, ("track", "cross"), split_axis=1, concat_axis=1, tiled=True
    )
    value_slots = received_values[:3].reshape(3, slot_count)
    gate_slots = jnp.maximum(received_values[3].reshape(slot_count).astype(jnp.int32) - 1, 0)
    picked = sight[:, 0, :][:, gate_slots]
    proj = jnp.sum(picked * value_slots, axis=0)
    observed = jnp.zeros((obs,), jnp.float32).at[gate_slots].add(proj)
    live = (jnp.arange(gates_each, dtype=jnp.int32)[None, :] < gate_counts[0][:, None]).astype(
        jnp.float32
    )
    masked = live * observed.reshape(beams, gates_each)
    weighted = (
        jnp.dot(masked, precision[0], precision=highest, preferred_element_type=jnp.float32) * live
    )
    weighted_flat = weighted.reshape(obs)
    returned_value_rows = (picked * weighted_flat[gate_slots][None, :]).reshape(
        3, owning_ranks, slot_capacity
    )
    returned = lax.all_to_all(
        returned_value_rows, ("track", "cross"), split_axis=1, concat_axis=1, tiled=True
    )
    sample_terms = returned.reshape(3, slot_count)[:, slot_index]
    pulled = (
        jnp.zeros((3, direction.shape[1] * direction.shape[2] * direction.shape[3]), jnp.float32)
        .at[:, cells]
        .add(sample_terms)
    )
    pulled = pulled.reshape(direction.shape)
    shift_x = wind[0] * pulled
    shift_y = wind[1] * pulled
    shift_z = wind[2] * pulled
    mixed = viscosity * pulled
    gtr = jnp.stack(
        [
            wind_gradient[j] * pulled[0]
            + wind_gradient[3 + j] * pulled[1]
            + wind_gradient[6 + j] * pulled[2]
            for j in range(3)
        ]
    )
    stacked = jnp.concatenate([shift_x, shift_y, mixed], axis=0)
    outer = with_halo(stacked, (("track", 1), ("cross", 2)), 1)
    moved = along_x(outer[0:3]) + along_y(outer[3:6]) + along_z(shift_z)
    spread = near_sum(outer[6:9], mixed) - 6.0 * mixed
    terms = moved + spread
    result = pulled + time_step * (terms - gtr)
    return (result, weighted_flat.reshape(1, obs))


def solution(mesh):
    placed = (
        P(None, "track", "cross", None),
        P(None, "track", "cross", None),
        P(None, "track", "cross", None),
        P("track", "cross", None),
        P("track", "cross", None, None),
        P("track", "cross", None),
        P("track", "cross", None),
        P(None, ("track", "cross"), None),
        P(("track", "cross"), None),
        P(("track", "cross"), None, None),
    )
    return jax.shard_map(
        body,
        mesh=mesh,
        in_specs=placed,
        out_specs=(P(None, "track", "cross", None), P(("track", "cross"), None)),
        check_vma=False,
    )
```

profile of v0, /device:TPU:0, one launch (start us, length us, event | category | flops | bytes accessed | tf_op | source)
XLA Modules:
  0.0 1077.8 jit_solution(13842871747099539996)
XLA Ops:
  0.6 1.1 fusion.44
  1.7 1.3 collective-permute-start.1
  3.1 1.4 collective-permute-start
  4.5 6.0 multiply_add_fusion.5
  11.2 0.7 convert_reduce_fusion
  12.1 1.7 fusion.3
  14.2 1.6 copy-done.5
  16.3 1.3 collective-permute-start.2
  17.6 5.2 collective-permute-start.3
  22.7 1.2 collective-permute-done.3
  23.9 6.7 fusion.27
  30.6 64.6 %copy.30 = f32[3,16,64,256]{0,3,2,1:T(8,128)} copy(f32[3,16,64,256]{3,2,1,0:T(8,128)} %fusion.27) | data formatting | bytes 6291456 | tf_op jit(solution)/shard_map/add | solution.py:100
  95.2 118.9 %gather_fusion = f32[8192,3]{1,0:T(8,128)} fusion(f32[3,262144]{0,1:T(8,128)} %bitcast.12, s32[8192]{0:T(1024)S(1)} %broadcast_clamp_fusion.3), kind=kCustom, calls=%fused_computation | custom fusion | bytes 229376 | tf_op jit(solution)/shard_map/gather | solution.py:109
  214.1 2.8 copy.31
  217.0 0.8 maximum_bitcast_fusion
  217.8 2.6 copy.32
  220.4 48.0 %scatter_custom_fusion = f32[4,16384]{0,1:T(8,128)} fusion(s32[8192]{0:T(1024)S(1)} %bitcast.76, f32[8192,4]{1,0:T(8,128)} %copy.32, f32[]{:T(128)} %constant.10.clone.1), kind=kCustom, calls=%fused_computation.26 | custom fusion | flops 32768 | bytes 262656 | tf_op jit(solution)/shard_map/scatter-add | solution.py:114
  268.5 5.9 copy.33
  274.4 17.3 %all-to-all-start = ((f32[4,128,128]{2,0,1:T(4,128)}), f32[4,128,128]{2,0,1:T(4,128)S(1)}, u32[]{:S(2)}, u32[]{:S(2)}) async-start(f32[4,128,128]{2,0,1:T(4,128)} %copy.33), calls=%async_computation | async-start | bytes 524288 | tf_op jit(solution)/shard_map/all_to_all | solution.py:117
  291.7 1.8 slice_bitcast_fusion.2
  293.7 5.9 sort
  299.6 2.9 all-to-all-done
  302.7 54.8 %gather_fusion.1 = f32[16384,3]{1,0:T(8,128)} fusion(f32[3,1024]{0,1:T(8,128)S(1)} %bitcast.65, s32[16384]{0:T(1024)S(1)} %broadcast_clamp_fusion), kind=kCustom, calls=%fused_computation.1 | custom fusion | bytes 458752 | tf_op jit(solution)/shard_map/gather | solution.py:122
  357.4 5.5 copy.36
  363.1 113.4 %scatter_custom_fusion.1 = f32[1024]{0:T(1024)S(1)} fusion(s32[16384]{0:T(1024)S(1)} %maximum_bitcast_fusion.1, f32[16384]{0:T(1024)S(1)} %bitcast.79, f32[]{:T(128)} %constant.10.clone.1), kind=kCustom, calls=%fused_computation.120 | custom fusion | flops 16384 | bytes 4100 | tf_op jit(solution)/shard_map/scatter-add | solution.py:124
  476.8 65.3 %gather_fusion.2 = f32[16384]{0:T(1024)S(1)} fusion(f32[1024]{0:T(1024)S(1)} %bitcast.62, s32[16384]{0:T(1024)S(1)} %broadcast_clamp_fusion), kind=kCustom, calls=%fused_computation.2 | custom fusion | bytes 196608 | tf_op jit(solution)/shard_map/gather | solution.py:133
  542.1 0.8 broadcast_multiply_fusion.7
  542.9 7.0 all-to-all-start.1
  549.9 10.9 %all-to-all-done.1 = f32[3,128,128]{2,0,1:T(4,128)S(1)} async-done(((f32[3,128,128]{2,0,1:T(4,128)}), f32[3,128,128]{2,0,1:T(4,128)S(1)}, u32[]{:S(2)}, u32[]{:S(2)}) %all-to-all-start.1) | async-done | bytes 196640 | tf_op jit(solution)/shard_map/all_to_all | solution.py:136
  560.7 4.8 copy.37
  565.6 31.2 %gather_fusion.3 = f32[8192,3]{1,0:T(8,128)} fusion(f32[3,16384]{0,1:T(8,128)} %bitcast.66, s32[8192]{0:T(1024)S(1)} %broadcast_clamp_fusion.2), kind=kCustom, calls=%fused_computation.3 | custom fusion | bytes 229376 | tf_op jit(solution)/shard_map/gather | solution.py:139
  596.8 158.2 %scatter_custom_fusion.2 = f32[3,262144]{0,1:T(8,128)} fusion(s32[8192]{0:T(1024)S(1)} %get-tuple-element.2, f32[]{:T(128)} %constant.10.clone.1, f32[8192,3]{1,0:T(8,128)} %gather_fusion.3, s32[8192]{0:T(1024)S(1)} %broadcast_clamp_fusion.1), kind=kCustom, calls=%fused_computation.11 | custom fusion | flops 24576 | bytes 3146240 | tf_op jit(solution)/shard_map/scatter-add | solution.py:143
  755.0 77.2 %copy.42 = f32[3,16,64,256]{3,2,1,0:T(8,128)} copy(f32[3,16,64,256]{0,3,2,1:T(8,128)} %bitcast.29) | data formatting | bytes 6291456 | tf_op jit(solution)/shard_map/reshape | solution.py:145
  832.3 6.7 broadcast_multiply_fusion.2
  838.9 1.2 pad_maximum_fusion.20
  840.2 0.8 copy-done.3
  840.9 1.0 copy-done.4
  841.9 1.3 collective-permute-start.4
  843.2 3.9 collective-permute-start.5
  847.1 186.4 %slice_reduce_fusion.2 = (f32[262144]{0:T(1024)}, f32[262144]{0:T(1024)}, f32[262144]{0:T(1024)}) fusion(f32[3,262144]{0,1:T(8,128)} %scatter_custom_fusion.2), kind=kLoop, calls=%fused_computation.10 | loop fusion | bytes 6291456 | tf_op jit(solution)/shard_map/slice | solution.py:152
  1033.6 2.5 squeeze.12
  1036.0 2.5 squeeze.13
  1038.6 2.5 squeeze.14
  1041.1 1.9 pad_maximum_fusion.27
  1043.0 1.3 collective-permute-start.6
  1044.3 4.8 collective-permute-start.7
  1049.1 6.6 multiply_add_fusion.2
  1055.7 21.9 %fusion.17 = f32[3,16,64,256]{3,2,1,0:T(8,128)} fusion(f32[3,16,64,256]{3,2,1,0:T(8,128)} %copy.42, f32[3,16,64,256]{3,2,1,0:T(8,128)} %get-tuple-element.20, f32[3,16,64,256]{3,2,1,0:T(8,128)} %copy-done.3, f32[9,18,1,256]{3,2,1,0:T(1,128)S(1)} %collective-permute-done.7, f32[9,1,64,256]{3,2,1,0:T(8,128)} %collective-permute-done.4, ...), kind=kLoop, calls=%fused_computation.34 | loop fusion | flops 40108032 | bytes 23531520 | tf_op jit(solution)/shard_map/add | solution.py:163
  (56 shorter events, 2.4 us)
Async XLA Ops:
  0.6 475.9 %copy-start = (f32[1,128,128]{2,1,0:T(8,128)S(1)}, f32[1,128,128]{2,1,0:T(8,128)}, u32[]{:S(2)}) copy-start(f32[1,128,128]{2,1,0:T(8,128)} %param.19) | copy-start | bytes 196612
  1.7 12.4 %collective-permute-start.1 = (f32[3,1,64,256]{3,2,1,0:T(8,128)S(1)}, f32[3,1,64,256]{3,2,1,0:T(8,128)S(1)}, u32[]{:S(2)}, u32[]{:S(2)}) collective-permute-start(f32[3,1,64,256]{3,2,1,0:T(8,128)S(1)} %get-tuple-element.30), channel_id=1, source_target_pairs={{0,16},{16,32},{32,48},{48,64},{64,80},{80,96},{96,112},{1,17},{17... | collective-permute-start | bytes 589832 | tf_op jit(solution)/shard_map/ppermute | solution.py:18
  3.0 7.5 copy-start.12
  3.1 7.5 copy-start.13
  3.1 8.2 copy-start.11
  3.1 13.1 %collective-permute-start = (f32[3,1,64,256]{3,2,1,0:T(8,128)S(1)}, f32[3,1,64,256]{3,2,1,0:T(8,128)S(1)}, u32[]{:S(2)}, u32[]{:S(2)}) collective-permute-start(f32[3,1,64,256]{3,2,1,0:T(8,128)S(1)} %get-tuple-element.29), channel_id=1, source_target_pairs={{16,0},{32,16},{48,32},{64,48},{80,64},{96,80},{112,96},{17,1},{33... | collective-permute-start | bytes 589832 | tf_op jit(solution)/shard_map/ppermute | solution.py:20
  10.5 3.3 copy-start.6
  13.9 1.9 copy-start.5
  15.8 8.1 copy-start.7
  16.3 6.5 collective-permute-start.2
  17.6 6.4 collective-permute-start.3
  274.4 28.1 %all-to-all-start = ((f32[4,128,128]{2,0,1:T(4,128)}), f32[4,128,128]{2,0,1:T(4,128)S(1)}, u32[]{:S(2)}, u32[]{:S(2)}) async-start(f32[4,128,128]{2,0,1:T(4,128)} %copy.33), calls=%async_computation | async-start | bytes 524288 | tf_op jit(solution)/shard_map/all_to_all | solution.py:117
  291.7 1.8 copy-start.14
  357.4 119.2 %copy-start.15 = (s32[1,8]{1,0:T(1,128)S(1)}, s32[1,8]{1,0:T(1,128)}, u32[]{:S(2)}) copy-start(s32[1,8]{1,0:T(1,128)} %param.18) | copy-start | bytes 100
  476.8 65.3 %copy-start.2 = (f32[8,128]{1,0:T(8,128)}, f32[8,128]{1,0:T(8,128)S(1)}, u32[]{:S(2)}) copy-start(f32[8,128]{1,0:T(8,128)S(1)} %convolution_select_fusion) | copy-start | bytes 12292
  542.9 17.9 %all-to-all-start.1 = ((f32[3,128,128]{2,0,1:T(4,128)}), f32[3,128,128]{2,0,1:T(4,128)S(1)}, u32[]{:S(2)}, u32[]{:S(2)}) async-start(f32[3,128,128]{2,0,1:T(4,128)} %broadcast_multiply_fusion.7), calls=%async_computation.1 | async-start | bytes 524288 | tf_op jit(solution)/shard_map/all_to_all | solution.py:136
  838.9 2.0 copy-start.3
  838.9 3.0 copy-start.4
  841.9 199.1 %collective-permute-start.4 = (f32[9,1,64,256]{3,2,1,0:T(8,128)}, f32[9,1,64,256]{3,2,1,0:T(8,128)}, u32[]{:S(2)}, u32[]{:S(2)}) collective-permute-start(f32[9,1,64,256]{3,2,1,0:T(8,128)} %get-tuple-element.16), channel_id=1, source_target_pairs={{16,0},{32,16},{48,32},{64,48},{80,64},{96,80},{112,96},{17,1},{33... | collective-permute-start | bytes 1769480 | tf_op jit(solution)/shard_map/ppermute | solution.py:20
  843.2 197.9 %collective-permute-start.5 = (f32[9,1,64,256]{3,2,1,0:T(8,128)}, f32[9,1,64,256]{3,2,1,0:T(8,128)}, u32[]{:S(2)}, u32[]{:S(2)}) collective-permute-start(f32[9,1,64,256]{3,2,1,0:T(8,128)} %get-tuple-element.15), channel_id=1, source_target_pairs={{0,16},{16,32},{32,48},{48,64},{64,80},{80,96},{96,112},{1,17},{17... | collective-permute-start | bytes 1769480 | tf_op jit(solution)/shard_map/ppermute | solution.py:18
  1041.1 8.0 copy-start.8
  1041.1 8.0 copy-start.9
  1041.1 8.0 copy-start.10
  1043.0 12.7 %collective-permute-start.6 = (f32[9,18,1,256]{3,2,1,0:T(1,128)S(1)}, f32[9,18,1,256]{3,2,1,0:T(1,128)S(1)}, u32[]{:S(2)}, u32[]{:S(2)}) collective-permute-start(f32[9,18,1,256]{3,2,1,0:T(1,128)S(1)} %get-tuple-element.13), channel_id=1, source_target_pairs={{1,0},{2,1},{3,2},{4,3},{5,4},{6,5},{7,6},{8,7},{9,8},{10,9},{11,1... | collective-permute-start | bytes 497672 | tf_op jit(solution)/shard_map/ppermute | solution.py:20
  1044.3 11.4 %collective-permute-start.7 = (f32[9,18,1,256]{3,2,1,0:T(1,128)S(1)}, f32[9,18,1,256]{3,2,1,0:T(1,128)S(1)}, u32[]{:S(2)}, u32[]{:S(2)}) collective-permute-start(f32[9,18,1,256]{3,2,1,0:T(1,128)S(1)} %get-tuple-element.14), channel_id=1, source_target_pairs={{0,1},{1,2},{2,3},{3,4},{4,5},{5,6},{6,7},{7,8},{8,9},{9,10},{10,1... | collective-permute-start | bytes 497672 | tf_op jit(solution)/shard_map/ppermute | solution.py:18
  1055.7 21.9 %copy-start.1 = (f32[1,128,128]{2,1,0:T(8,128)S(1)}, f32[1,128,128]{2,1,0:T(8,128)}, u32[]{:S(2)}) copy-start(f32[1,128,128]{2,1,0:T(8,128)} %param.19) | copy-start | bytes 196612
where the time goes:
time: 1090 us; the launch traced here: 1080 us
  local copies, waits for them, and re-layouts  635 us (58%)
  other arithmetic  380 us (35%)
  starting transfers between devices  44.7 us (4%)
  waiting for transfers between devices  15 us (1%)
    slice x1, local copies, waits for them, and re-layouts, body(): pulled[0]  186 us
    scatter-add x3, other arithmetic, body(): pulled = jnp.zeros((3, direction.shape[1] * direction.shape[2] * directio...  164 us
    gather x2, local copies, waits for them, and re-layouts, body(): picked_values = tangent.reshape(3, -1)[:, cells]  122 us
    scatter-add x1, other arithmetic, body(): observed = jnp.zeros((obs,), jnp.float32).at[gate_slots].add(proj)  113 us
    reshape x1, local copies, waits for them, and re-layouts, body(): pulled = pulled.reshape(direction.shape)  77.2 us
    gather x1, local copies, waits for them, and re-layouts, body(): weighted_flat[gate_slots][None, :]  65.3 us
    add x1, local copies, waits for them, and re-layouts, body(): direction + time_step * (-adv - gq + viscosity * (near_sum(padded, direct...  64.6 us
    gather x2, local copies, waits for them, and re-layouts, body(): picked = sight[:, 0, :][:, gate_slots]  60.3 us
  transfers between devices with their start and end apart: 10, of which 3 were waited for; matrix products, arithmetic and copies ran while one was open for 20% of the time, Pallas kernels for 0%

commit v1 on v0

v1 whole, which is shorter than its diff:
```python
import functools

import jax
import jax.numpy as jnp
from jax import lax
from jax.experimental import pallas as pl
from jax.experimental.pallas import tpu as pltpu
from jax.sharding import PartitionSpec as P

time_step = 0.2
highest = lax.Precision.HIGHEST
tile = 256
lanes = 128
f32 = jnp.float32
bf16 = jnp.bfloat16
i32 = jnp.int32


def split(value):
    head = value.astype(bf16)
    return head, (value - head.astype(f32)).astype(bf16)


def rows_equal(count, row):
    iota = lax.broadcasted_iota(i32, (count, row.shape[1]), 0)
    return iota == row


def pick(mask, value):
    return jnp.sum(jnp.where(mask, value, 0.0), axis=0, keepdims=True)


def ones_at(mask):
    return jnp.where(mask, 1.0, 0.0).astype(bf16)


def dot_nt(a, b):
    return lax.dot_general(a, b, (((1,), (1,)), ((), ())), preferred_element_type=f32)


def dot_nn(a, b):
    return jnp.dot(a, b, preferred_element_type=f32)


def walk_tiles(first_ref, pointer, limit, tiles, visit):
    def first(p):
        return first_ref[jnp.minimum(p, tiles - 1) * tile]

    def go_on(carry):
        p, go = carry
        return go & (p < tiles) & (first(p) < limit)

    def step(carry):
        p, _ = carry
        visit(p)
        done = first_ref[p * tile + tile - 1] < limit
        return jnp.where(done, p + 1, p), done

    p, _ = lax.while_loop(go_on, step, (pointer[0], jnp.bool_(True)))
    pointer[0] = p


def sample_kernel(
    cell_s,
    field_ref,
    xlo_ref,
    xhi_ref,
    ylo_ref,
    yhi_ref,
    wind_ref,
    grad_ref,
    visc_ref,
    cell_ref,
    og_ref,
    slots_ref,
    rank_ref,
    plane_ref,
    value_ref,
    offset_ref,
    upper_ref,
    total_ref,
    pointer,
    *,
    obs,
):
    x = pl.program_id(0)
    nx = pl.num_programs(0)
    cy, nz = field_ref.shape[2], field_ref.shape[3]
    tiles = cell_ref.shape[0]
    owners = slots_ref.shape[0]
    per_step = -(-tiles // field_ref.shape[1])

    @pl.when(x == 0)
    def _():
        pointer[0] = 0
        value_ref[...] = jnp.zeros_like(value_ref)
        offset_ref[...] = jnp.zeros_like(offset_ref)
        a = lax.broadcasted_iota(i32, (tile, 2 * tile), 0)
        b = lax.broadcasted_iota(i32, (tile, 2 * tile), 1)
        upper_ref[...] = ones_at((a < b) | (b >= tile))

    y_at = lax.broadcasted_iota(i32, (cy, nz), 0)
    z_at = lax.broadcasted_iota(i32, (cy, nz), 1)
    visc = visc_ref[0]
    here = [field_ref[c, x] for c in range(3)]
    below = jnp.maximum(x - 1, 0)
    above = jnp.minimum(x + 1, nx - 1)
    for c in range(3):
        f = here[c]
        down = jnp.where(x == 0, xlo_ref[c], field_ref[c, below])
        up = jnp.where(x == nx - 1, xhi_ref[c], field_ref[c, above])
        left = jnp.where(y_at == 0, ylo_ref[c, pl.ds(x, 1), :], pltpu.roll(f, 1, 0))
        right = jnp.where(y_at == cy - 1, yhi_ref[c, pl.ds(x, 1), :], pltpu.roll(f, cy - 1, 0))
        under = jnp.where(z_at == 0, 0.0, pltpu.roll(f, 1, 1))
        over = jnp.where(z_at == nz - 1, 0.0, pltpu.roll(f, nz - 1, 1))
        adv = 0.5 * (
            wind_ref[0, 0] * (up - down) + wind_ref[1, 0] * (right - left) + wind_ref[2, 0] * (over - under)
        )
        gq = (
            grad_ref[3 * c, 0] * here[0]
            + grad_ref[3 * c + 1, 0] * here[1]
            + grad_ref[3 * c + 2, 0] * here[2]
        )
        near = up + down + right + left + over + under
        tangent = f + time_step * (visc * (near - 6.0 * f) - adv - gq)
        head, rest = split(tangent)
        plane_ref[c * cy : (c + 1) * cy, :nz] = head
        plane_ref[c * cy : (c + 1) * cy, nz:] = rest

    for k in range(per_step):
        t = x * per_step + k

        @pl.when(t < tiles)
        def _():
            mask = rows_equal(owners, og_ref[pl.ds(t, 1), :] // obs)
            counts = dot_nn(ones_at(mask), upper_ref[...])
            rank = pick(mask, counts[:, :tile] + offset_ref[...])
            rank_ref[pl.ds(t, 1), :] = rank.astype(i32)
            offset_ref[...] += counts[:, tile:]

    def visit(p):
        cells = cell_ref[pl.ds(p, 1), :]
        zs = ones_at(rows_equal(nz, cells % nz))
        line = cells // nz
        mask = rows_equal(cy, line - x * cy)
        found = dot_nn(plane_ref[...], jnp.concatenate([zs, zs], axis=0))
        for c in range(3):
            value_ref[c, pl.ds(p, 1), :] += pick(mask, found[c * cy : (c + 1) * cy])

    walk_tiles(cell_s, pointer, (x + 1) * cy * nz, tiles, visit)

    @pl.when(x == nx - 1)
    def _():
        total_ref[...] = jnp.zeros_like(total_ref)

        def add_tile(t, carry):
            og = og_ref[pl.ds(t, 1), :]
            mask = rows_equal(owners, og // obs)
            gate = og % obs
            ranks = ones_at(rows_equal(lanes, rank_ref[pl.ds(t, 1), :]))
            parts = []
            for c in range(3):
                head, rest = split(value_ref[c, pl.ds(t, 1), :])
                parts.append((head.astype(f32), rest.astype(f32)))
            low = gate % lanes
            parts.append(((gate - low).astype(f32), low.astype(f32)))
            left = jnp.concatenate(
                [
                    jnp.concatenate([jnp.where(mask, a, 0.0).astype(bf16), jnp.where(mask, b, 0.0).astype(bf16)], axis=1)
                    for a, b in parts
                ],
                axis=0,
            )
            total_ref[...] += dot_nt(left, jnp.concatenate([ranks, ranks], axis=1))
            return carry

        lax.fori_loop(0, tiles, add_tile, 0)
        for c in range(4):
            slots_ref[:, c, :] = total_ref[c * owners : (c + 1) * owners]


def owner_kernel(counts_s, got_ref, sight_ref, precision_ref, back_ref, weighted_ref, gate_ref):
    sources = got_ref.shape[0]
    group = 8
    wide = group * lanes
    beams = counts_s.shape[1]

    def gathered(i):
        return jnp.concatenate([got_ref[i * group + j] for j in range(group)], axis=1)

    def beam_mask(gate):
        return rows_equal(beams, gate // lanes)

    def collect(i, acc):
        rows = gathered(i)
        gate = rows[3:4].astype(i32)
        gates = ones_at(rows_equal(lanes, gate % lanes))
        gate_ref[i] = gates
        mask = beam_mask(gate)
        parts = []
        for k in range(3):
            head, rest = split(rows[k : k + 1])
            parts.append(jnp.where(mask, head.astype(f32), 0.0))
            parts.append(jnp.where(mask, rest.astype(f32), 0.0))
        left = jnp.concatenate(parts, axis=0).astype(bf16)
        return acc + dot_nt(left, gates)

    acc = lax.fori_loop(0, sources // group, collect, jnp.zeros((6 * beams, lanes), f32))
    sights = [
        jnp.concatenate([sight_ref[k, :, b * lanes : (b + 1) * lanes] for b in range(beams)], axis=0)
        for k in range(3)
    ]
    observed = jnp.zeros((beams, lanes), f32)
    for k in range(3):
        at = 2 * k * beams
        observed += sights[k] * (acc[at : at + beams] + acc[at + beams : at + 2 * beams])
    beam_at = lax.broadcasted_iota(i32, (beams, lanes), 0)
    gate_at = lax.broadcasted_iota(i32, (beams, lanes), 1)
    limit = jnp.zeros((beams, lanes), i32)
    for b in range(beams):
        limit = jnp.where(beam_at == b, counts_s[0, b], limit)
    live = jnp.where(gate_at < limit, 1.0, 0.0)
    weighted = live * jnp.dot(live * observed, precision_ref[0], precision=highest, preferred_element_type=f32)
    for b in range(beams):
        weighted_ref[:, b * lanes : (b + 1) * lanes] = weighted[b : b + 1]
    spread = jnp.concatenate([s * weighted for s in sights], axis=0)
    head = spread.astype(bf16).astype(f32)
    table = jnp.concatenate([head, spread - head], axis=1).astype(bf16)

    def give(i, carry):
        gate = gathered(i)[3:4].astype(i32)
        mask = beam_mask(gate)
        gates = gate_ref[i]
        found = dot_nn(table, jnp.concatenate([gates, gates], axis=0))
        rows = jnp.concatenate(
            [pick(mask, found[k * beams : (k + 1) * beams]) for k in range(3)] + [jnp.zeros((1, wide), f32)], axis=0
        )
        for j in range(group):
            back_ref[i * group + j] = rows[:, j * lanes : (j + 1) * lanes]
        return carry

    lax.fori_loop(0, sources // group, give, 0)


def adjoint_kernel(
    cell_s,
    back_ref,
    cell_ref,
    og_ref,
    rank_ref,
    wind_ref,
    grad_ref,
    visc_ref,
    out_ref,
    xlo_ref,
    xhi_ref,
    ylo_ref,
    yhi_ref,
    table_ref,
    value_ref,
    plane_ref,
    carry_ref,
    passed_ref,
    pointer,
    *,
    obs,
):
    x = pl.program_id(0)
    nx = pl.num_programs(0) - 1
    cy, nz = out_ref.shape[2], out_ref.shape[3]
    tiles = cell_ref.shape[0]
    owners = back_ref.shape[0]

    @pl.when(x == 0)
    def _():
        pointer[0] = 0
        for c in range(3):
            head, rest = split(back_ref[:, c, :])
            table_ref[c * owners : (c + 1) * owners, :lanes] = head
            table_ref[c * owners : (c + 1) * owners, lanes:] = rest
        carry_ref[...] = jnp.zeros_like(carry_ref)
        passed_ref[...] = jnp.zeros_like(passed_ref)

        def restore(t, carry):
            mask = rows_equal(owners, og_ref[pl.ds(t, 1), :] // obs)
            ranks = ones_at(rows_equal(lanes, rank_ref[pl.ds(t, 1), :]))
            found = dot_nn(table_ref[...], jnp.concatenate([ranks, ranks], axis=0))
            for c in range(3):
                value_ref[c, pl.ds(t, 1), :] = pick(mask, found[c * owners : (c + 1) * owners])
            return carry

        lax.fori_loop(0, tiles, restore, 0)

    @pl.when(x < nx)
    def _():
        plane_ref[...] = jnp.zeros_like(plane_ref)

        def visit(p):
            cells = cell_ref[pl.ds(p, 1), :]
            zs = ones_at(rows_equal(nz, cells % nz))
            mask = rows_equal(cy, cells // nz - x * cy)
            heads, rests = [], []
            for c in range(3):
                head, rest = split(value_ref[c, pl.ds(p, 1), :])
                heads.append(jnp.where(mask, head.astype(f32), 0.0).astype(bf16))
                rests.append(jnp.where(mask, rest.astype(f32), 0.0).astype(bf16))
            left = jnp.concatenate([jnp.concatenate(heads, axis=0), jnp.concatenate(rests, axis=0)], axis=1)
            plane_ref[...] += dot_nt(left, jnp.concatenate([zs, zs], axis=1))

        walk_tiles(cell_s, pointer, (x + 1) * cy * nz, tiles, visit)

        y_at = lax.broadcasted_iota(i32, (cy, nz), 0)
        z_at = lax.broadcasted_iota(i32, (cy, nz), 1)
        visc = visc_ref[0]
        pulled = [plane_ref[c * cy : (c + 1) * cy] for c in range(3)]
        for c in range(3):
            p = pulled[c]
            mixed = visc * p
            sx = 0.5 * wind_ref[0, 0] * p
            sy = 0.5 * wind_ref[1, 0] * p
            sz = 0.5 * wind_ref[2, 0] * p
            to_down = mixed + sx
            to_up = mixed - sx
            to_left = mixed + sy
            to_right = mixed - sy
            to_under = mixed + sz
            to_over = mixed - sz
            gtr = grad_ref[c, 0] * pulled[0] + grad_ref[3 + c, 0] * pulled[1] + grad_ref[6 + c, 0] * pulled[2]
            around = (
                jnp.where(y_at == cy - 1, 0.0, pltpu.roll(to_left, cy - 1, 0))
                + jnp.where(y_at == 0, 0.0, pltpu.roll(to_right, 1, 0))
                + jnp.where(z_at == nz - 1, 0.0, pltpu.roll(to_under, nz - 1, 1))
                + jnp.where(z_at == 0, 0.0, pltpu.roll(to_over, 1, 1))
            )
            own = p + time_step * (around - gtr - 6.0 * mixed)
            out_ref[c, 0] = carry_ref[c] + time_step * to_down
            carry_ref[c] = own + passed_ref[c]
            passed_ref[c] = time_step * to_up
            ylo_ref[c, pl.ds(x, 1), :] = time_step * to_left[0:1]
            yhi_ref[c, pl.ds(x, 1), :] = time_step * to_right[cy - 1 : cy]

            @pl.when(x == 0)
            def _():
                xlo_ref[c] = time_step * to_down

            @pl.when(x == nx - 1)
            def _():
                xhi_ref[c] = time_step * to_up

    @pl.when(x == nx)
    def _():
        out_ref[:, 0] = carry_ref[...]


def edge_kernel(
    given_ref, xlo_ref, xhi_ref, ylo_ref, yhi_ref, out_ref, low_ref, high_ref, left_ref, right_ref, sems
):
    del given_ref
    nx, cy = out_ref.shape[1], out_ref.shape[2]
    inner = nx - 2
    places = [
        (out_ref.at[:, 0], low_ref),
        (out_ref.at[:, nx - 1], high_ref),
        (out_ref.at[:, pl.ds(1, inner), pl.ds(0, 8)], left_ref),
        (out_ref.at[:, pl.ds(1, inner), pl.ds(cy - 8, 8)], right_ref),
    ]
    reads = [pltpu.make_async_copy(a, b, sems.at[i]) for i, (a, b) in enumerate(places)]
    for read in reads:
        read.start()
    writes = [pltpu.make_async_copy(b, a, sems.at[4 + i]) for i, (a, b) in enumerate(places)]
    for i, (x, ref, halo) in enumerate(((0, low_ref, xlo_ref), (nx - 1, high_ref, xhi_ref))):
        reads[i].wait()
        ref[...] += halo[...]
        ref[:, 0:1, :] += ylo_ref[:, x : x + 1, :]
        ref[:, cy - 1 : cy, :] += yhi_ref[:, x : x + 1, :]
        writes[i].start()
    reads[2].wait()
    for k in range(inner):
        left_ref[:, k, 0:1, :] += ylo_ref[:, k + 1 : k + 2, :]
    writes[2].start()
    reads[3].wait()
    for k in range(inner):
        right_ref[:, k, 7:8, :] += yhi_ref[:, k + 1 : k + 2, :]
    writes[3].start()
    for write in writes:
        write.wait()


def shifted(value, axis, by):
    count = lax.axis_size(axis)
    return lax.ppermute(value, axis, [(i, i + by) for i in range(count) if 0 <= i + by < count])


def whole(shape):
    return pl.BlockSpec(shape, lambda *_: (0,) * len(shape))


def body(
    direction,
    wind,
    wind_gradient,
    viscosity,
    sample_owner,
    sample_cell,
    sample_gate,
    sight,
    gate_counts,
    precision,
):
    _, cx, cy, nz = direction.shape
    owners = lax.axis_size("track") * lax.axis_size("cross")
    obs = sight.shape[2]
    samples = sample_cell.shape[2]
    tiles = samples // tile
    names = ("track", "cross")
    big = pltpu.CompilerParams(dimension_semantics=("arbitrary",), vmem_limit_bytes=48 << 20)

    xlo = shifted(direction[:, cx - 1], "track", 1)
    xhi = shifted(direction[:, 0], "track", -1)
    ylo = shifted(direction[:, :, cy - 1], "cross", 1)
    yhi = shifted(direction[:, :, 0], "cross", -1)
    cells, og = lax.sort(
        (sample_cell.reshape(-1), sample_owner.reshape(-1) * obs + sample_gate.reshape(-1)), num_keys=1, is_stable=False
    )
    cell_rows = cells.reshape(tiles, tile)
    og_rows = og.reshape(tiles, tile)

    def plane(count, last):
        return pl.BlockSpec((count, 1, cy, nz), lambda x, *_: (0, jnp.minimum(x, last), 0, 0))

    def visc_plane(last):
        return pl.BlockSpec((1, cy, nz), lambda x, *_: (jnp.minimum(x, last), 0, 0))

    rows = whole((tiles, tile))
    slots, rank_rows = pl.pallas_call(
        functools.partial(sample_kernel, obs=obs),
        name="sample",
        grid_spec=pltpu.PrefetchScalarGridSpec(
            num_scalar_prefetch=1,
            grid=(cx,),
            in_specs=[
                whole((3, cx, cy, nz)),
                whole((3, cy, nz)),
                whole((3, cy, nz)),
                whole((3, cx, nz)),
                whole((3, cx, nz)),
                plane(3, cx - 1),
                plane(9, cx - 1),
                visc_plane(cx - 1),
                rows,
                rows,
            ],
            out_specs=[whole((owners, 4, lanes)), rows],
            scratch_shapes=[
                pltpu.VMEM((3 * cy, 2 * nz), bf16),
                pltpu.VMEM((3, tiles, tile), f32),
                pltpu.VMEM((owners, tile), f32),
                pltpu.VMEM((tile, 2 * tile), bf16),
                pltpu.VMEM((4 * owners, lanes), f32),
                pltpu.SMEM((1,), i32),
            ],
        ),
        out_shape=[
            jax.ShapeDtypeStruct((owners, 4, lanes), f32),
            jax.ShapeDtypeStruct((tiles, tile), i32),
        ],
        compiler_params=big,
    )(cells, direction, xlo, xhi, ylo, yhi, wind, wind_gradient, viscosity, cell_rows, og_rows)

    got = lax.all_to_all(slots, names, split_axis=0, concat_axis=0, tiled=True)
    back, weighted = pl.pallas_call(
        owner_kernel,
        name="owner",
        in_specs=[
            pl.BlockSpec(memory_space=pltpu.SMEM),
            pl.BlockSpec(memory_space=pltpu.VMEM),
            pl.BlockSpec(memory_space=pltpu.VMEM),
            pl.BlockSpec(memory_space=pltpu.VMEM),
        ],
        out_specs=[pl.BlockSpec(memory_space=pltpu.VMEM), pl.BlockSpec(memory_space=pltpu.VMEM)],
        scratch_shapes=[pltpu.VMEM((owners // 8, lanes, 8 * lanes), bf16)],
        out_shape=[
            jax.ShapeDtypeStruct((owners, 4, lanes), f32),
            jax.ShapeDtypeStruct((1, obs), f32),
        ],
        compiler_params=pltpu.CompilerParams(vmem_limit_bytes=48 << 20),
    )(gate_counts, got, sight, precision)
    returned = lax.all_to_all(back, names, split_axis=0, concat_axis=0, tiled=True)

    result, sent_xlo, sent_xhi, sent_ylo, sent_yhi = pl.pallas_call(
        functools.partial(adjoint_kernel, obs=obs),
        name="adjoint",
        grid_spec=pltpu.PrefetchScalarGridSpec(
            num_scalar_prefetch=1,
            grid=(cx + 1,),
            in_specs=[
                whole((owners, 4, lanes)),
                rows,
                rows,
                rows,
                plane(3, cx - 1),
                plane(9, cx - 1),
                visc_plane(cx - 1),
            ],
            out_specs=[
                pl.BlockSpec((3, 1, cy, nz), lambda x, *_: (0, jnp.maximum(x - 1, 0), 0, 0)),
                whole((3, cy, nz)),
                whole((3, cy, nz)),
                whole((3, cx, nz)),
                whole((3, cx, nz)),
            ],
            scratch_shapes=[
                pltpu.VMEM((3 * owners, 2 * lanes), bf16),
                pltpu.VMEM((3, tiles, tile), f32),
                pltpu.VMEM((3 * cy, nz), f32),
                pltpu.VMEM((3, cy, nz), f32),
                pltpu.VMEM((3, cy, nz), f32),
                pltpu.SMEM((1,), i32),
            ],
        ),
        out_shape=[
            jax.ShapeDtypeStruct((3, cx, cy, nz), f32),
            jax.ShapeDtypeStruct((3, cy, nz), f32),
            jax.ShapeDtypeStruct((3, cy, nz), f32),
            jax.ShapeDtypeStruct((3, cx, nz), f32),
            jax.ShapeDtypeStruct((3, cx, nz), f32),
        ],
        compiler_params=big,
    )(cells, returned, cell_rows, og_rows, rank_rows, wind, wind_gradient, viscosity)

    from_low = shifted(sent_xhi, "track", 1)
    from_high = shifted(sent_xlo, "track", -1)
    from_left = shifted(sent_yhi, "cross", 1)
    from_right = shifted(sent_ylo, "cross", -1)
    vmem = pl.BlockSpec(memory_space=pltpu.VMEM)
    hbm = pl.BlockSpec(memory_space=pl.ANY)
    result = pl.pallas_call(
        edge_kernel,
        name="edges",
        in_specs=[hbm, vmem, vmem, vmem, vmem],
        out_specs=hbm,
        scratch_shapes=[
            pltpu.VMEM((3, cy, nz), f32),
            pltpu.VMEM((3, cy, nz), f32),
            pltpu.VMEM((3, cx - 2, 8, nz), f32),
            pltpu.VMEM((3, cx - 2, 8, nz), f32),
            pltpu.SemaphoreType.DMA((8,)),
        ],
        out_shape=jax.ShapeDtypeStruct((3, cx, cy, nz), f32),
        input_output_aliases={0: 0},
        compiler_params=pltpu.CompilerParams(vmem_limit_bytes=48 << 20),
    )(result, from_low, from_high, from_left, from_right)
    return (result, weighted)


def solution(mesh):
    placed = (
        P(None, "track", "cross", None),
        P(None, "track", "cross", None),
        P(None, "track", "cross", None),
        P("track", "cross", None),
        P("track", "cross", None, None),
        P("track", "cross", None),
        P("track", "cross", None),
        P(None, ("track", "cross"), None),
        P(("track", "cross"), None),
        P(("track", "cross"), None, None),
    )
    return jax.shard_map(
        body,
        mesh=mesh,
        in_specs=placed,
        out_specs=(P(None, "track", "cross", None), P(("track", "cross"), None)),
        check_vma=False,
    )
```

time: 1090 us -> 154 us (0.14)
  the two profiles are of different devices: /device:TPU:0 before, /device:TPU:38 now
where the time goes in v1:
time: 154 us
  Pallas kernels  76.5 us (50%)
  blocking collectives  34.8 us (23%)
  starting transfers between devices  21.9 us (14%)
  other arithmetic  7.99 us (5%)
  waiting for transfers between devices  6.17 us (4%)
  local copies, waits for them, and re-layouts  5.41 us (4%)
    pallas_call x1, Pallas kernels, body(): pl.pallas_call(functools.partial(sample_kernel, obs=obs), name='sample',...  35 us
    pallas_call x1, Pallas kernels, body(): pl.pallas_call(functools.partial(adjoint_kernel, obs=obs), name='adjoint'...  30.9 us
    ppermute x8, starting transfers between devices, shifted(): lax.ppermute(value, axis, [(i, i + by) for i in range(count) if 0 <= i +...  21.9 us
    all_to_all x1, blocking collectives, body(): got = lax.all_to_all(slots, names, split_axis=0, concat_axis=0, tiled=True)  19.6 us
    all_to_all x1, blocking collectives, body(): lax.all_to_all(back, names, split_axis=0, concat_axis=0, tiled=True)  15.3 us
    pallas_call x1, Pallas kernels, body(): pl.pallas_call(owner_kernel, name='owner', in_specs=[pl.BlockSpec(memory_...  8.46 us
    sort x1, other arithmetic, body(): lax.sort((sample_cell.reshape(-1), sample_owner.reshape(-1) * obs + sampl...  6.44 us
    ppermute x8, waiting for transfers between devices, shifted(): lax.ppermute(value, axis, [(i, i + by) for i in range(count) if 0 <= i +...  6.17 us
  transfers between devices with their start and end apart: 8, of which 1 were waited for; matrix products, arithmetic and copies ran while one was open for 6% of the time, Pallas kernels for 0%

profile of v1, /device:TPU:38, one launch (start us, length us, event | category | flops | bytes accessed | tf_op | source)
XLA Modules:
  0.0 153.7 jit_solution(7024839470518910490)
XLA Ops:
  0.6 1.2 fusion
  1.8 3.4 %collective-permute-start.2 = (f32[3,16,256]{2,1,0:T(8,128)S(1)}, f32[3,16,256]{2,1,0:T(8,128)S(1)}, u32[]{:S(2)}, u32[]{:S(2)}) collective-permute-start(f32[3,16,256]{2,1,0:T(8,128)S(1)} %bitcast.18), channel_id=1, source_target_pairs={{0,1},{1,2},{2,3},{3,4},{4,5},{5,6},{6,7},{7,8},{8,9},{9,10},{10,1... | collective-permute-start | bytes 147464 | tf_op jit(solution)/shard_map/ppermute | solution.py:391
  5.3 2.4 %collective-permute-start.3 = (f32[3,16,256]{2,1,0:T(8,128)S(1)}, f32[3,16,256]{2,1,0:T(8,128)S(1)}, u32[]{:S(2)}, u32[]{:S(2)}) collective-permute-start(f32[3,16,256]{2,1,0:T(8,128)S(1)} %bitcast.19), channel_id=1, source_target_pairs={{1,0},{2,1},{3,2},{4,3},{5,4},{6,5},{7,6},{8,7},{9,8},{10,9},{11,1... | collective-permute-start | bytes 147464 | tf_op jit(solution)/shard_map/ppermute | solution.py:391
  7.7 1.1 slice_bitcast_fusion
  8.8 1.9 %collective-permute-start.1 = (f32[3,64,256]{2,1,0:T(8,128)S(1)}, f32[3,64,256]{2,1,0:T(8,128)S(1)}, u32[]{:S(2)}, u32[]{:S(2)}) collective-permute-start(f32[3,64,256]{2,1,0:T(8,128)S(1)} %get-tuple-element.26), channel_id=1, source_target_pairs={{16,0},{32,16},{48,32},{64,48},{80,64},{96,80},{112,96},{17,1},{33... | collective-permute-start | bytes 589832 | tf_op jit(solution)/shard_map/ppermute | solution.py:391
  10.7 2.4 %collective-permute-start = (f32[3,64,256]{2,1,0:T(8,128)S(1)}, f32[3,64,256]{2,1,0:T(8,128)S(1)}, u32[]{:S(2)}, u32[]{:S(2)}) collective-permute-start(f32[3,64,256]{2,1,0:T(8,128)S(1)} %get-tuple-element.27), channel_id=1, source_target_pairs={{0,16},{16,32},{32,48},{48,64},{64,80},{80,96},{96,112},{1,17},{17... | collective-permute-start | bytes 589832 | tf_op jit(solution)/shard_map/ppermute | solution.py:391
  13.1 0.8 broadcast_multiply_fusion
  13.9 0.8 add.3
  14.7 6.4 %sort.15 = (s32[8192]{0:T(1024)S(1)}, s32[8192]{0:T(1024)S(1)}) sort(s32[8192]{0:T(1024)} %bitcast.21, s32[8192]{0:T(1024)S(1)} %add.3), dimensions={0}, to_apply=%region_0.0 | sort | flops 106496 | bytes 131072 | tf_op jit(solution)/shard_map/sort | solution.py:422
  21.1 0.0 copy-start.5
  21.1 0.0 copy-start.6
  21.1 0.0 copy-start.4
  21.2 0.0 collective-permute-done.2.ylo_ref
  21.2 0.0 collective-permute-done.3.yhi_ref
  21.2 0.0 collective-permute-done.1.xhi_ref
  21.2 0.0 collective-permute-done.xlo_ref
  21.2 0.0 copy-start.1
  21.2 1.9 %copy-done.1 = f32[3,16,64,256]{3,2,1,0:T(8,128)S(1)} copy-done((f32[3,16,64,256]{3,2,1,0:T(8,128)S(1)}, f32[3,16,64,256]{3,2,1,0:T(8,128)}, u32[]{:S(2)}) %copy-start.1) | copy-done | bytes 3145752
  23.1 0.0 copy-start.2
  23.1 1.2 copy-done.2
  24.3 0.0 copy-start
  24.3 0.0 copy-start.3
  24.3 35.0 %sample.1 = (f32[128,4,128]{2,1,0:T(4,128)S(1)}, s32[32,256]{1,0:T(8,128)S(1)}) custom-call(s32[8192]{0:T(1024)S(1)} %get-tuple-element.13.cell_s, f32[3,16,64,256]{3,2,1,0:T(8,128)S(1)} %copy-done.1, f32[3,64,256]{2,1,0:T(8,128)S(1)} %collective-permute-done.xlo_ref, f32[3,64,256]{2,1,0:T(8,128)S(1)} %collective-permute-done.1.xhi_ref, ...), custom_call_target="tpu_custom_call" | custom-call | tf_op jit(solution)/shard_map/sample/pallas_call | solution.py:435
  59.4 19.6 %all_to_all.10.got_ref = f32[128,4,128]{2,1,0:T(4,128)S(1)} all-to-all(f32[128,4,128]{2,1,0:T(4,128)S(1)} %get-tuple-element.15), channel_id=1, replica_groups=mesh['track'=8,'cross'=16] {'track','cross'}, dimensions={0} | all-to-all | bytes 524288 | tf_op jit(solution)/shard_map/all_to_all | solution.py:470
  78.9 0.0 copy-done.5
  78.9 0.0 copy-done.6
  79.0 0.0 copy-done.4
  79.0 8.5 %owner.1 = (f32[128,4,128]{2,1,0:T(4,128)S(1)}, f32[1,1024]{1,0:T(1,128)}) custom-call(s32[1,8]{1,0:T(1,128)S(1)} %copy-done.6, f32[128,4,128]{2,1,0:T(4,128)S(1)} %all_to_all.10.got_ref, f32[3,1,1024]{2,1,0:T(1,128)S(1)} %copy-done.5, f32[1,128,128]{2,1,0:T(8,128)S(1)} %copy-done.4), custom_call_target="tpu_custom_call" | custom-call | tf_op jit(solution)/shard_map/owner/pallas_call | solution.py:471
  87.4 15.3 %all_to_all.11.back_ref = f32[128,4,128]{2,1,0:T(4,128)S(1)} all-to-all(f32[128,4,128]{2,1,0:T(4,128)S(1)} %get-tuple-element.16), channel_id=1, replica_groups=mesh['track'=8,'cross'=16] {'track','cross'}, dimensions={0} | all-to-all | bytes 524288 | tf_op jit(solution)/shard_map/all_to_all | solution.py:488
  102.7 0.0 copy-done
  102.7 0.0 copy-done.3
  102.7 30.9 %adjoint.1 = (f32[3,16,64,256]{3,2,1,0:T(8,128)}, f32[3,64,256]{2,1,0:T(8,128)S(1)}, f32[3,64,256]{2,1,0:T(8,128)S(1)}, f32[3,16,256]{2,1,0:T(8,128)S(1)}, f32[3,16,256]{2,1,0:T(8,128)S(1)}) custom-call(s32[8192]{0:T(1024)S(1)} %get-tuple-element.13.cell_s, f32[128,4,128]{2,1,0:T(4,128)S(1)} %all_to_all.11.back_ref, s32[32,256]{1,0:T(8,128)S(1)} %reshape.21.cell_ref, ...), custom_call_target="tpu_custom_call" | custom-call | tf_op jit(solution)/shard_map/adjoint/pallas_call | solution.py:490
  133.6 1.9 %collective-permute-start.4 = (f32[3,64,256]{2,1,0:T(8,128)S(1)}, f32[3,64,256]{2,1,0:T(8,128)S(1)}, u32[]{:S(2)}, u32[]{:S(2)}) collective-permute-start(f32[3,64,256]{2,1,0:T(8,128)S(1)} %get-tuple-element.19), channel_id=1, source_target_pairs={{0,16},{16,32},{32,48},{48,64},{64,80},{80,96},{96,112},{1,17},{17... | collective-permute-start | bytes 589832 | tf_op jit(solution)/shard_map/ppermute | solution.py:391
  135.5 3.6 %collective-permute-start.5 = (f32[3,64,256]{2,1,0:T(8,128)S(1)}, f32[3,64,256]{2,1,0:T(8,128)S(1)}, u32[]{:S(2)}, u32[]{:S(2)}) collective-permute-start(f32[3,64,256]{2,1,0:T(8,128)S(1)} %get-tuple-element.20), channel_id=1, source_target_pairs={{16,0},{32,16},{48,32},{64,48},{80,64},{96,80},{112,96},{17,1},{33... | collective-permute-start | bytes 589832 | tf_op jit(solution)/shard_map/ppermute | solution.py:391
  139.2 4.3 %collective-permute-start.6 = (f32[3,16,256]{2,1,0:T(8,128)S(1)}, f32[3,16,256]{2,1,0:T(8,128)S(1)}, u32[]{:S(2)}, u32[]{:S(2)}) collective-permute-start(f32[3,16,256]{2,1,0:T(8,128)S(1)} %get-tuple-element.21), channel_id=1, source_target_pairs={{0,1},{1,2},{2,3},{3,4},{4,5},{5,6},{6,7},{7,8},{8,9},{9,10},{10,1... | collective-permute-start | bytes 147464 | tf_op jit(solution)/shard_map/ppermute | solution.py:391
  143.4 1.9 %collective-permute-start.7 = (f32[3,16,256]{2,1,0:T(8,128)S(1)}, f32[3,16,256]{2,1,0:T(8,128)S(1)}, u32[]{:S(2)}, u32[]{:S(2)}) collective-permute-start(f32[3,16,256]{2,1,0:T(8,128)S(1)} %get-tuple-element.22), channel_id=1, source_target_pairs={{1,0},{2,1},{3,2},{4,3},{5,4},{6,5},{7,6},{8,7},{9,8},{10,9},{11,1... | collective-permute-start | bytes 147464 | tf_op jit(solution)/shard_map/ppermute | solution.py:391
  145.3 0.0 collective-permute-done.6.ylo_ref
  145.4 6.2 %collective-permute-done.7.yhi_ref = f32[3,16,256]{2,1,0:T(8,128)S(1)} collective-permute-done((f32[3,16,256]{2,1,0:T(8,128)S(1)}, f32[3,16,256]{2,1,0:T(8,128)S(1)}, u32[]{:S(2)}, u32[]{:S(2)}) %collective-permute-start.7) | collective-permute-done | bytes 49184 | tf_op jit(solution)/shard_map/ppermute | solution.py:391
  151.5 0.0 collective-permute-done.4.xlo_ref
  151.5 0.0 collective-permute-done.5.xhi_ref
  151.5 2.1 %edges.1 = f32[3,16,64,256]{3,2,1,0:T(8,128)} custom-call(f32[3,16,64,256]{3,2,1,0:T(8,128)} %get-tuple-element.18.given_ref, f32[3,64,256]{2,1,0:T(8,128)S(1)} %collective-permute-done.4.xlo_ref, f32[3,64,256]{2,1,0:T(8,128)S(1)} %collective-permute-done.5.xhi_ref, ...), custom_call_target="tpu_custom_call", output_to_operand_aliasing={{}: (0, {})} | custom-call | tf_op jit(solution)/shard_map/edges/pallas_call | solution.py:537
  (4 shorter events, 0.0 us)
Async XLA Ops:
  1.8 19.3 %collective-permute-start.2 = (f32[3,16,256]{2,1,0:T(8,128)S(1)}, f32[3,16,256]{2,1,0:T(8,128)S(1)}, u32[]{:S(2)}, u32[]{:S(2)}) collective-permute-start(f32[3,16,256]{2,1,0:T(8,128)S(1)} %bitcast.18), channel_id=1, source_target_pairs={{0,1},{1,2},{2,3},{3,4},{4,5},{5,6},{6,7},{7,8},{8,9},{9,10},{10,1... | collective-permute-start | bytes 147464 | tf_op jit(solution)/shard_map/ppermute | solution.py:391
  5.3 15.9 %collective-permute-start.3 = (f32[3,16,256]{2,1,0:T(8,128)S(1)}, f32[3,16,256]{2,1,0:T(8,128)S(1)}, u32[]{:S(2)}, u32[]{:S(2)}) collective-permute-start(f32[3,16,256]{2,1,0:T(8,128)S(1)} %bitcast.19), channel_id=1, source_target_pairs={{1,0},{2,1},{3,2},{4,3},{5,4},{6,5},{7,6},{8,7},{9,8},{10,9},{11,1... | collective-permute-start | bytes 147464 | tf_op jit(solution)/shard_map/ppermute | solution.py:391
  8.8 12.4 %collective-permute-start.1 = (f32[3,64,256]{2,1,0:T(8,128)S(1)}, f32[3,64,256]{2,1,0:T(8,128)S(1)}, u32[]{:S(2)}, u32[]{:S(2)}) collective-permute-start(f32[3,64,256]{2,1,0:T(8,128)S(1)} %get-tuple-element.26), channel_id=1, source_target_pairs={{16,0},{32,16},{48,32},{64,48},{80,64},{96,80},{112,96},{17,1},{33... | collective-permute-start | bytes 589832 | tf_op jit(solution)/shard_map/ppermute | solution.py:391
  10.7 10.5 %collective-permute-start = (f32[3,64,256]{2,1,0:T(8,128)S(1)}, f32[3,64,256]{2,1,0:T(8,128)S(1)}, u32[]{:S(2)}, u32[]{:S(2)}) collective-permute-start(f32[3,64,256]{2,1,0:T(8,128)S(1)} %get-tuple-element.27), channel_id=1, source_target_pairs={{0,16},{16,32},{32,48},{48,64},{64,80},{80,96},{96,112},{1,17},{17... | collective-permute-start | bytes 589832 | tf_op jit(solution)/shard_map/ppermute | solution.py:391
  21.1 57.8 %copy-start.5 = (f32[3,1,1024]{2,1,0:T(1,128)S(1)}, f32[3,1,1024]{2,1,0:T(1,128)}, u32[]{:S(2)}) copy-start(f32[3,1,1024]{2,1,0:T(1,128)} %sight_ref.1) | copy-start | bytes 36868
  21.1 57.8 %copy-start.6 = (s32[1,8]{1,0:T(1,128)S(1)}, s32[1,8]{1,0:T(1,128)}, u32[]{:S(2)}) copy-start(s32[1,8]{1,0:T(1,128)} %counts_s.1) | copy-start | bytes 100
  21.1 57.8 %copy-start.4 = (f32[1,128,128]{2,1,0:T(8,128)S(1)}, f32[1,128,128]{2,1,0:T(8,128)}, u32[]{:S(2)}) copy-start(f32[1,128,128]{2,1,0:T(8,128)} %precision_ref.1) | copy-start | bytes 196612
  21.2 1.9 %copy-start.1 = (f32[3,16,64,256]{3,2,1,0:T(8,128)S(1)}, f32[3,16,64,256]{3,2,1,0:T(8,128)}, u32[]{:S(2)}) copy-start(f32[3,16,64,256]{3,2,1,0:T(8,128)} %field_ref.1) | copy-start | bytes 9437188
  23.1 1.2 copy-start.2
  24.3 78.3 %copy-start = (f32[3,16,64,256]{3,2,1,0:T(8,128)S(1)}, f32[3,16,64,256]{3,2,1,0:T(8,128)}, u32[]{:S(2)}) copy-start(f32[3,16,64,256]{3,2,1,0:T(8,128)} %wind_ref.3) | copy-start | bytes 9437188
  24.3 78.3 %copy-start.3 = (f32[16,64,256]{2,1,0:T(8,128)S(1)}, f32[16,64,256]{2,1,0:T(8,128)}, u32[]{:S(2)}) copy-start(f32[16,64,256]{2,1,0:T(8,128)} %visc_ref.3) | copy-start | bytes 3145732
  133.6 17.9 %collective-permute-start.4 = (f32[3,64,256]{2,1,0:T(8,128)S(1)}, f32[3,64,256]{2,1,0:T(8,128)S(1)}, u32[]{:S(2)}, u32[]{:S(2)}) collective-permute-start(f32[3,64,256]{2,1,0:T(8,128)S(1)} %get-tuple-element.19), channel_id=1, source_target_pairs={{0,16},{16,32},{32,48},{48,64},{64,80},{80,96},{96,112},{1,17},{17... | collective-permute-start | bytes 589832 | tf_op jit(solution)/shard_map/ppermute | solution.py:391
  135.5 16.0 %collective-permute-start.5 = (f32[3,64,256]{2,1,0:T(8,128)S(1)}, f32[3,64,256]{2,1,0:T(8,128)S(1)}, u32[]{:S(2)}, u32[]{:S(2)}) collective-permute-start(f32[3,64,256]{2,1,0:T(8,128)S(1)} %get-tuple-element.20), channel_id=1, source_target_pairs={{16,0},{32,16},{48,32},{64,48},{80,64},{96,80},{112,96},{17,1},{33... | collective-permute-start | bytes 589832 | tf_op jit(solution)/shard_map/ppermute | solution.py:391
  139.2 6.2 %collective-permute-start.6 = (f32[3,16,256]{2,1,0:T(8,128)S(1)}, f32[3,16,256]{2,1,0:T(8,128)S(1)}, u32[]{:S(2)}, u32[]{:S(2)}) collective-permute-start(f32[3,16,256]{2,1,0:T(8,128)S(1)} %get-tuple-element.21), channel_id=1, source_target_pairs={{0,1},{1,2},{2,3},{3,4},{4,5},{5,6},{6,7},{7,8},{8,9},{9,10},{10,1... | collective-permute-start | bytes 147464 | tf_op jit(solution)/shard_map/ppermute | solution.py:391
  143.4 8.1 %collective-permute-start.7 = (f32[3,16,256]{2,1,0:T(8,128)S(1)}, f32[3,16,256]{2,1,0:T(8,128)S(1)}, u32[]{:S(2)}, u32[]{:S(2)}) collective-permute-start(f32[3,16,256]{2,1,0:T(8,128)S(1)} %get-tuple-element.22), channel_id=1, source_target_pairs={{1,0},{2,1},{3,2},{4,3},{5,4},{6,5},{7,6},{8,7},{9,8},{10,9},{11,1... | collective-permute-start | bytes 147464 | tf_op jit(solution)/shard_map/ppermute | solution.py:391

commit v2 on v0

v2 whole, which is shorter than its diff:
```python
import functools

import jax
import jax.numpy as jnp
from jax import lax
from jax.experimental import pallas as pl
from jax.experimental.pallas import tpu as pltpu
from jax.sharding import PartitionSpec as P

time_step = 0.2
highest = lax.Precision.HIGHEST
tile = 256
lanes = 128
span = 64
strip = 16
batch = 4
row_bits = 8
f32 = jnp.float32
bf16 = jnp.bfloat16
i32 = jnp.int32


def split(value):
    head = value.astype(bf16)
    return head, (value - head.astype(f32)).astype(bf16)


def rows_equal(count, row):
    iota = lax.broadcasted_iota(i32, (count, row.shape[1]), 0)
    return iota == row


def pick(mask, value):
    return jnp.sum(jnp.where(mask, value, 0.0), axis=0, keepdims=True)


def onehot(count, row):
    iota = lax.broadcasted_iota(i32, (count, row.shape[1]), 0).astype(bf16)
    return jnp.where(iota == row.astype(f32).astype(bf16), jnp.ones((), bf16), jnp.zeros((), bf16))


def ones_at(mask):
    return jnp.where(mask, 1.0, 0.0).astype(bf16)


def dot_nt(a, b):
    return lax.dot_general(a, b, (((1,), (1,)), ((), ())), preferred_element_type=f32)


def dot_nn(a, b):
    return jnp.dot(a, b, preferred_element_type=f32)


def window(cell_s, t, rows):
    first = cell_s[t, 0] >> row_bits
    last = cell_s[t, tile - 1] >> row_bits
    base = jnp.minimum((first >> 4) << 4, rows - span)
    return pl.multiple_of(base, 16), last - base - span + 1


def each_tile(cell_s, tiles, rows, visit, more):
    def first(t, most):
        base, over = window(cell_s, t, rows)
        visit(t, base)
        return jnp.maximum(most, over)

    most = lax.fori_loop(0, tiles, first, i32(0), unroll=8)

    @pl.when(most > 0)
    def _():
        def rest(t, carry):
            base, over = window(cell_s, t, rows)

            def step(k, carry):
                least = base + k * span
                more(t, pl.multiple_of(jnp.minimum(least, rows - span), 16), least)
                return carry

            lax.fori_loop(1, 1 + (over + span - 1) // span, step, 0)
            return carry

        lax.fori_loop(0, tiles, rest, 0)


def slot_parts(slot):
    return slot // (2 * lanes), slot % (2 * lanes)


def sample_kernel(
    cell_s,
    field_hbm,
    xlo_ref,
    xhi_ref,
    ylo_ref,
    yhi_ref,
    wind_hbm,
    grad_hbm,
    visc_hbm,
    cell_ref,
    og_ref,
    slots_ref,
    slot_ref,
    field_ref,
    wind_ref,
    grad_ref,
    visc_ref,
    plane_ref,
    value_ref,
    offset_ref,
    upper_ref,
    total_ref,
    sems,
    *,
    obs,
):
    nx, cy, nz = visc_ref.shape
    tiles = cell_ref.shape[0]
    owners = 2 * slots_ref.shape[0]
    rows = nx * cy

    def copies(k):
        part = pl.ds(k * batch, batch)
        return [
            pltpu.make_async_copy(field_hbm.at[:, part], field_ref.at[:, pl.ds(k * batch + 1, batch)], sems.at[0, k]),
            pltpu.make_async_copy(wind_hbm.at[:, part], wind_ref.at[:, part], sems.at[1, k]),
            pltpu.make_async_copy(grad_hbm.at[:, part], grad_ref.at[:, part], sems.at[2, k]),
            pltpu.make_async_copy(visc_hbm.at[part], visc_ref.at[part], sems.at[3, k]),
        ]

    batches = nx // batch
    for k in range(batches):
        for copy in copies(k):
            copy.start()

    along, across = lax.axis_index("track"), lax.axis_index("cross")
    field_ref[:, 0] = jnp.where(along == 0, 0.0, xlo_ref[...])
    field_ref[:, nx + 1] = jnp.where(along == lax.axis_size("track") - 1, 0.0, xhi_ref[...])
    left_edge = across == 0
    right_edge = across == lax.axis_size("cross") - 1

    offset_ref[...] = jnp.zeros_like(offset_ref)
    a = lax.broadcasted_iota(i32, (tile, tile), 0)
    b = lax.broadcasted_iota(i32, (tile, tile), 1)
    upper_ref[...] = ones_at(a <= b)

    def rank(t, carry):
        own = og_ref[pl.ds(t, 1), :] // obs
        mask = rows_equal(owners, own)
        counts = dot_nn(ones_at(mask), upper_ref[...])
        offset = offset_ref[...]
        ranks = pick(mask, counts + jnp.concatenate([offset] * (tile // lanes), axis=1))
        slot_ref[pl.ds(t, 1), :] = own * lanes + ranks.astype(i32) - 1
        offset_ref[...] = offset + jnp.broadcast_to(counts[:, tile - 1 : tile], offset.shape)
        return carry

    lax.fori_loop(0, tiles, rank, 0, unroll=8)

    y_at = lax.broadcasted_iota(i32, (strip, nz), 0)
    z_at = lax.broadcasted_iota(i32, (strip, nz), 1)

    def advance(x, carry):
        for y in range(0, cy, strip):
            part = pl.ds(y, strip)
            visc = time_step * visc_ref[x, part]
            wind = [(-0.5 * time_step) * wind_ref[a, x, part] for a in range(3)]
            here = [field_ref[c, x + 1, part] for c in range(3)]
            for c in range(3):
                f = here[c]
                down = field_ref[c, x, part]
                up = field_ref[c, x + 2, part]
                if y == 0:
                    before = jnp.where(left_edge, 0.0, ylo_ref[c, pl.ds(x, 1), :])
                else:
                    before = field_ref[c, x + 1, y - 1 : y]
                if y + strip == cy:
                    after = jnp.where(right_edge, 0.0, yhi_ref[c, pl.ds(x, 1), :])
                else:
                    after = field_ref[c, x + 1, y + strip : y + strip + 1]
                left = jnp.where(y_at == 0, before, pltpu.roll(f, 1, 0))
                right = jnp.where(y_at == strip - 1, after, pltpu.roll(f, strip - 1, 0))
                under = jnp.where(z_at == 0, 0.0, pltpu.roll(f, 1, 1))
                over = jnp.where(z_at == nz - 1, 0.0, pltpu.roll(f, nz - 1, 1))
                near = (up + down) + (right + left) + (over + under)
                tangent = f + visc * (near - 6.0 * f)
                tangent += wind[0] * (up - down) + wind[1] * (right - left) + wind[2] * (over - under)
                gq = (
                    grad_ref[3 * c, x, part] * here[0]
                    + grad_ref[3 * c + 1, x, part] * here[1]
                    + grad_ref[3 * c + 2, x, part] * here[2]
                )
                head, rest = split(tangent - time_step * gq)
                at = pl.multiple_of(x * cy + y, strip)
                plane_ref[c, pl.ds(at, strip), :nz] = head
                plane_ref[c, pl.ds(at, strip), nz:] = rest
        return carry

    copies(0)[0].wait()
    for k in range(batches):
        for copy in copies(k)[1:]:
            copy.wait()
        if k + 1 < batches:
            copies(k + 1)[0].wait()
        lax.fori_loop(k * batch, (k + 1) * batch, advance, 0)

    def find(t, begin, least):
        cells = cell_ref[pl.ds(t, 1), :]
        zs = onehot(nz, cells % nz)
        line = cells // nz
        mask = rows_equal(span, jnp.where(line >= least, line - begin, -1))
        block = jnp.concatenate(
            [plane_ref[c, pl.ds(begin, span), h * nz : (h + 1) * nz] for h in range(2) for c in range(3)], axis=0
        )
        found = dot_nn(block, zs)
        found = found[: 3 * span] + found[3 * span :]
        return [pick(mask, found[c * span : (c + 1) * span]) for c in range(3)]

    def gather(t, begin):
        for c, value in enumerate(find(t, begin, 0)):
            value_ref[c, pl.ds(t, 1), :] = value

    def gather_more(t, begin, least):
        for c, value in enumerate(find(t, begin, least)):
            value_ref[c, pl.ds(t, 1), :] += value

    each_tile(cell_s, tiles, rows, gather, gather_more)

    total_ref[...] = jnp.zeros_like(total_ref)
    half = owners // 2

    def add_tile(t, carry):
        line, column = slot_parts(slot_ref[pl.ds(t, 1), :])
        gate = og_ref[pl.ds(t, 1), :] % obs
        mask = rows_equal(half, line)
        columns = onehot(2 * lanes, column)
        low = gate % lanes
        parts = []
        for c in range(3):
            head, rest = split(value_ref[c, pl.ds(t, 1), :])
            parts.append((head.astype(f32), rest.astype(f32)))
        parts.append(((gate - low).astype(f32), low.astype(f32)))
        left = jnp.concatenate(
            [
                jnp.concatenate([jnp.where(mask, a, 0.0).astype(bf16), jnp.where(mask, b, 0.0).astype(bf16)], axis=1)
                for a, b in parts
            ],
            axis=0,
        )
        total_ref[...] += dot_nt(left, jnp.concatenate([columns, columns], axis=1))
        return carry

    lax.fori_loop(0, tiles, add_tile, 0, unroll=8)
    for c in range(4):
        for h in range(2):
            slots_ref[:, h, c, :] = total_ref[c * half : (c + 1) * half, h * lanes : (h + 1) * lanes]


def owner_kernel(counts_s, got_ref, sight_ref, precision_ref, back_ref, weighted_ref, gate_ref):
    sources = got_ref.shape[0]
    group = 8
    wide = group * lanes
    beams = counts_s.shape[1]

    def gathered(i):
        return jnp.concatenate([got_ref[i * group + j] for j in range(group)], axis=1)

    def beam_mask(gate):
        return rows_equal(beams, gate // lanes)

    def collect(i, acc):
        rows = gathered(i)
        gate = rows[3:4].astype(i32)
        gates = ones_at(rows_equal(lanes, gate % lanes))
        gate_ref[i] = gates
        mask = beam_mask(gate)
        parts = []
        for k in range(3):
            head, rest = split(rows[k : k + 1])
            parts.append(jnp.where(mask, head.astype(f32), 0.0))
            parts.append(jnp.where(mask, rest.astype(f32), 0.0))
        left = jnp.concatenate(parts, axis=0).astype(bf16)
        return acc + dot_nt(left, gates)

    acc = lax.fori_loop(0, sources // group, collect, jnp.zeros((6 * beams, lanes), f32), unroll=4)
    sights = [
        jnp.concatenate([sight_ref[k, :, b * lanes : (b + 1) * lanes] for b in range(beams)], axis=0)
        for k in range(3)
    ]
    observed = jnp.zeros((beams, lanes), f32)
    for k in range(3):
        at = 2 * k * beams
        observed += sights[k] * (acc[at : at + beams] + acc[at + beams : at + 2 * beams])
    beam_at = lax.broadcasted_iota(i32, (beams, lanes), 0)
    gate_at = lax.broadcasted_iota(i32, (beams, lanes), 1)
    limit = jnp.zeros((beams, lanes), i32)
    for b in range(beams):
        limit = jnp.where(beam_at == b, counts_s[0, b], limit)
    live = jnp.where(gate_at < limit, 1.0, 0.0)
    weighted = live * jnp.dot(live * observed, precision_ref[0], precision=highest, preferred_element_type=f32)
    for b in range(beams):
        weighted_ref[:, b * lanes : (b + 1) * lanes] = weighted[b : b + 1]
    spread = jnp.concatenate([s * weighted for s in sights], axis=0)
    head = spread.astype(bf16).astype(f32)
    table = jnp.concatenate([head, spread - head], axis=1).astype(bf16)

    def give(i, carry):
        gate = gathered(i)[3:4].astype(i32)
        mask = beam_mask(gate)
        gates = gate_ref[i]
        found = dot_nn(table, jnp.concatenate([gates, gates], axis=0))
        rows = jnp.concatenate(
            [pick(mask, found[k * beams : (k + 1) * beams]) for k in range(3)] + [jnp.zeros((1, wide), f32)], axis=0
        )
        for j in range(group):
            back_ref[i * group + j] = rows[:, j * lanes : (j + 1) * lanes]
        return carry

    lax.fori_loop(0, sources // group, give, 0, unroll=4)


def adjoint_kernel(
    cell_s,
    back_ref,
    cell_ref,
    slot_ref,
    wind_hbm,
    grad_hbm,
    visc_hbm,
    out_hbm,
    xlo_ref,
    xhi_ref,
    ylo_ref,
    yhi_ref,
    wind_ref,
    grad_ref,
    visc_ref,
    table_ref,
    value_ref,
    plane_ref,
    out_ref,
    sems,
):
    nx, cy, nz = visc_ref.shape
    tiles = cell_ref.shape[0]
    half = back_ref.shape[0]
    rows = nx * cy

    copies = [
        pltpu.make_async_copy(wind_hbm, wind_ref, sems.at[0, 0]),
        pltpu.make_async_copy(grad_hbm, grad_ref, sems.at[1, 0]),
        pltpu.make_async_copy(visc_hbm, visc_ref, sems.at[2, 0]),
    ]

    def write(x):
        return pltpu.make_async_copy(out_ref.at[:, x + 1], out_hbm.at[:, x], sems.at[3, x])

    for copy in copies:
        copy.start()
    for c in range(3):
        for h in range(2):
            head, rest = split(back_ref[:, h, c, :])
            table_ref[c * half : (c + 1) * half, h * lanes : (h + 1) * lanes] = head
            table_ref[c * half : (c + 1) * half, (2 + h) * lanes : (3 + h) * lanes] = rest
    plane_ref[...] = jnp.zeros_like(plane_ref)

    def restore(t, carry):
        line, column = slot_parts(slot_ref[pl.ds(t, 1), :])
        mask = rows_equal(half, line)
        columns = onehot(2 * lanes, column)
        found = dot_nn(table_ref[...], jnp.concatenate([columns, columns], axis=0))
        for c in range(3):
            value_ref[c, pl.ds(t, 1), :] = pick(mask, found[c * half : (c + 1) * half])
        return carry

    lax.fori_loop(0, tiles, restore, 0, unroll=8)

    def put(t, begin, least):
        cells = cell_ref[pl.ds(t, 1), :]
        zs = onehot(nz, cells % nz)
        line = cells // nz
        mask = rows_equal(span, jnp.where(line >= least, line - begin, -1))
        heads, rests = [], []
        for c in range(3):
            head, rest = split(value_ref[c, pl.ds(t, 1), :])
            heads.append(jnp.where(mask, head.astype(f32), 0.0).astype(bf16))
            rests.append(jnp.where(mask, rest.astype(f32), 0.0).astype(bf16))
        left = jnp.concatenate([jnp.concatenate(heads, axis=0), jnp.concatenate(rests, axis=0)], axis=1)
        added = dot_nt(left, jnp.concatenate([zs, zs], axis=1))
        for c in range(3):
            plane_ref[c, pl.ds(begin, span), :] += added[c * span : (c + 1) * span]

    each_tile(cell_s, tiles, rows, lambda t, base: put(t, base, 0), put)

    y_at = lax.broadcasted_iota(i32, (strip, nz), 0)
    z_at = lax.broadcasted_iota(i32, (strip, nz), 1)
    strips = cy // strip

    def advance(x, carry):
        def give(k):
            part = pl.ds(k * strip, strip)
            at = pl.multiple_of(x * cy + k * strip, strip)
            pulled = [plane_ref[c, pl.ds(at, strip), :] for c in range(3)]
            visc = time_step * visc_ref[x, part]
            wind = (0.5 * time_step) * wind_ref[1, x, part]
            mixed = [visc * p for p in pulled]
            moved = [wind * p for p in pulled]
            return pulled, mixed, [m + w for m, w in zip(mixed, moved)], [m - w for m, w in zip(mixed, moved)]

        later = give(0)
        before = [0.0] * 3
        for k in range(strips):
            pulled, mixed, to_left, to_right = later
            part = pl.ds(k * strip, strip)
            after = [0.0] * 3
            if k + 1 < strips:
                later = give(k + 1)
                after = [v[0:1] for v in later[2]]
            wind_x = (0.5 * time_step) * wind_ref[0, x, part]
            wind_z = (0.5 * time_step) * wind_ref[2, x, part]
            for c in range(3):
                p = pulled[c]
                sx = wind_x * p
                sz = wind_z * p
                gtr = (
                    grad_ref[c, x, part] * pulled[0]
                    + grad_ref[3 + c, x, part] * pulled[1]
                    + grad_ref[6 + c, x, part] * pulled[2]
                )
                around = (
                    jnp.where(y_at == strip - 1, after[c], pltpu.roll(to_left[c], strip - 1, 0))
                    + jnp.where(y_at == 0, before[c], pltpu.roll(to_right[c], 1, 0))
                ) + (
                    jnp.where(z_at == nz - 1, 0.0, pltpu.roll(mixed[c] + sz, nz - 1, 1))
                    + jnp.where(z_at == 0, 0.0, pltpu.roll(mixed[c] - sz, 1, 1))
                )
                own = (p - 6.0 * mixed[c]) + (around - time_step * gtr)
                out_ref[c, x, part] += mixed[c] + sx
                out_ref[c, x + 1, part] += own
                out_ref[c, x + 2, part] = mixed[c] - sx
            if k == 0:
                for c in range(3):
                    ylo_ref[c, pl.ds(x, 1), :] = to_left[c][0:1]
            if k + 1 == strips:
                for c in range(3):
                    yhi_ref[c, pl.ds(x, 1), :] = to_right[c][strip - 1 : strip]
            before = [v[strip - 1 : strip] for v in to_right]

        @pl.when(x > 0)
        def _():
            write(x - 1).start()

        return carry

    for copy in copies:
        copy.wait()
    out_ref[:, 0:2] = jnp.zeros((3, 2, cy, nz), f32)
    lax.fori_loop(0, nx, advance, 0)
    xlo_ref[...] = out_ref[:, 0]
    xhi_ref[...] = out_ref[:, nx + 1]
    write(nx - 1).start()

    def end(x, carry):
        write(x).wait()
        return carry

    lax.fori_loop(0, nx, end, 0)


def edge_kernel(
    given_ref, xlo_ref, xhi_ref, ylo_ref, yhi_ref, out_ref, low_ref, high_ref, left_ref, right_ref, sems
):
    del given_ref
    along, across = lax.axis_index("track"), lax.axis_index("cross")
    last_along, last_across = lax.axis_size("track") - 1, lax.axis_size("cross") - 1
    ylo = jnp.where(across == 0, 0.0, ylo_ref[...])
    yhi = jnp.where(across == last_across, 0.0, yhi_ref[...])
    nx, cy = out_ref.shape[1], out_ref.shape[2]
    inner = nx - 2
    places = [
        (out_ref.at[:, 0], low_ref),
        (out_ref.at[:, nx - 1], high_ref),
        (out_ref.at[:, pl.ds(1, inner), pl.ds(0, 8)], left_ref),
        (out_ref.at[:, pl.ds(1, inner), pl.ds(cy - 8, 8)], right_ref),
    ]
    reads = [pltpu.make_async_copy(a, b, sems.at[i]) for i, (a, b) in enumerate(places)]
    for read in reads:
        read.start()
    writes = [pltpu.make_async_copy(b, a, sems.at[4 + i]) for i, (a, b) in enumerate(places)]
    for i, (x, ref, halo, edge) in enumerate(
        ((0, low_ref, xlo_ref, along == 0), (nx - 1, high_ref, xhi_ref, along == last_along))
    ):
        reads[i].wait()
        ref[...] += jnp.where(edge, 0.0, halo[...])
        ref[:, 0:1, :] += ylo[:, x : x + 1, :]
        ref[:, cy - 1 : cy, :] += yhi[:, x : x + 1, :]
        writes[i].start()
    reads[2].wait()
    for k in range(inner):
        left_ref[:, k, 0:1, :] += ylo[:, k + 1 : k + 2, :]
    writes[2].start()
    reads[3].wait()
    for k in range(inner):
        right_ref[:, k, 7:8, :] += yhi[:, k + 1 : k + 2, :]
    writes[3].start()
    for write in writes:
        write.wait()


def shifted(value, axis, by):
    count = lax.axis_size(axis)
    return lax.ppermute(value, axis, [(i, (i + by) % count) for i in range(count)])


vmem = pl.BlockSpec(memory_space=pltpu.VMEM)
smem = pl.BlockSpec(memory_space=pltpu.SMEM)
hbm = pl.BlockSpec(memory_space=pltpu.HBM)


def room(mib):
    return pltpu.CompilerParams(vmem_limit_bytes=mib << 20)


def call_sample(direction, halo, wind, wind_gradient, viscosity, cells, og, owners, obs):
    _, cx, cy, nz = direction.shape
    tiles = cells.shape[0]
    return pl.pallas_call(
        functools.partial(sample_kernel, obs=obs),
        name="sample",
        in_specs=[smem, hbm, vmem, vmem, vmem, vmem, hbm, hbm, hbm, vmem, vmem],
        out_specs=[vmem, vmem],
        scratch_shapes=[
            pltpu.VMEM((3, cx + 2, cy, nz), f32),
            pltpu.VMEM((3, cx, cy, nz), f32),
            pltpu.VMEM((9, cx, cy, nz), f32),
            pltpu.VMEM((cx, cy, nz), f32),
            pltpu.VMEM((3, cx * cy, 2 * nz), bf16),
            pltpu.VMEM((3, tiles, tile), f32),
            pltpu.VMEM((owners, lanes), f32),
            pltpu.VMEM((tile, tile), bf16),
            pltpu.VMEM((2 * owners, 2 * lanes), f32),
            pltpu.SemaphoreType.DMA((4, cx)),
        ],
        out_shape=[
            jax.ShapeDtypeStruct((owners // 2, 2, 4, lanes), f32),
            jax.ShapeDtypeStruct((tiles, tile), i32),
        ],
        compiler_params=room(40),
    )(cells, direction, *halo, wind, wind_gradient, viscosity, cells, og)


def call_owner(gate_counts, got, sight, precision):
    owners = got.shape[0]
    return pl.pallas_call(
        owner_kernel,
        name="owner",
        in_specs=[smem, vmem, vmem, vmem],
        out_specs=[vmem, vmem],
        scratch_shapes=[pltpu.VMEM((owners // 8, lanes, 8 * lanes), bf16)],
        out_shape=[
            jax.ShapeDtypeStruct((owners, 4, lanes), f32),
            jax.ShapeDtypeStruct((1, sight.shape[2]), f32),
        ],
        compiler_params=room(24),
    )(gate_counts, got, sight, precision)


def call_adjoint(returned, cells, slot, wind, wind_gradient, viscosity):
    _, cx, cy, nz = wind.shape
    tiles = cells.shape[0]
    half = returned.shape[0]
    return pl.pallas_call(
        adjoint_kernel,
        name="adjoint",
        in_specs=[smem, vmem, vmem, vmem, hbm, hbm, hbm],
        out_specs=[hbm, vmem, vmem, vmem, vmem],
        scratch_shapes=[
            pltpu.VMEM((3, cx, cy, nz), f32),
            pltpu.VMEM((9, cx, cy, nz), f32),
            pltpu.VMEM((cx, cy, nz), f32),
            pltpu.VMEM((3 * half, 4 * lanes), bf16),
            pltpu.VMEM((3, tiles, tile), f32),
            pltpu.VMEM((3, cx * cy, nz), f32),
            pltpu.VMEM((3, cx + 2, cy, nz), f32),
            pltpu.SemaphoreType.DMA((4, cx)),
        ],
        out_shape=[
            jax.ShapeDtypeStruct((3, cx, cy, nz), f32),
            jax.ShapeDtypeStruct((3, cy, nz), f32),
            jax.ShapeDtypeStruct((3, cy, nz), f32),
            jax.ShapeDtypeStruct((3, cx, nz), f32),
            jax.ShapeDtypeStruct((3, cx, nz), f32),
        ],
        compiler_params=room(40),
    )(cells, returned, cells, slot, wind, wind_gradient, viscosity)


def call_edges(result, halo):
    _, cx, cy, nz = result.shape
    return pl.pallas_call(
        edge_kernel,
        name="edges",
        in_specs=[hbm, vmem, vmem, vmem, vmem],
        out_specs=hbm,
        scratch_shapes=[
            pltpu.VMEM((3, cy, nz), f32),
            pltpu.VMEM((3, cy, nz), f32),
            pltpu.VMEM((3, cx - 2, 8, nz), f32),
            pltpu.VMEM((3, cx - 2, 8, nz), f32),
            pltpu.SemaphoreType.DMA((8,)),
        ],
        out_shape=jax.ShapeDtypeStruct(result.shape, f32),
        input_output_aliases={0: 0},
        compiler_params=room(24),
    )(result, *halo)


def body(
    direction,
    wind,
    wind_gradient,
    viscosity,
    sample_owner,
    sample_cell,
    sample_gate,
    sight,
    gate_counts,
    precision,
):
    _, cx, cy, nz = direction.shape
    owners = lax.axis_size("track") * lax.axis_size("cross")
    obs = sight.shape[2]
    names = ("track", "cross")
    halo = (
        shifted(direction[:, cx - 1], "track", 1),
        shifted(direction[:, 0], "track", -1),
        shifted(direction[:, :, cy - 1], "cross", 1),
        shifted(direction[:, :, 0], "cross", -1),
    )
    cells, og = lax.sort(
        (sample_cell.reshape(-1), sample_owner.reshape(-1) * obs + sample_gate.reshape(-1)), num_keys=1, is_stable=False
    )
    cells = cells.reshape(-1, tile)
    og = og.reshape(-1, tile)
    slots, slot = call_sample(direction, halo, wind, wind_gradient, viscosity, cells, og, owners, obs)
    got = lax.all_to_all(slots.reshape(owners, 4, lanes), names, split_axis=0, concat_axis=0, tiled=True)
    back, weighted = call_owner(gate_counts, got, sight, precision)
    returned = lax.all_to_all(back, names, split_axis=0, concat_axis=0, tiled=True)
    returned = returned.reshape(owners // 2, 2, 4, lanes)
    result, xlo, xhi, ylo, yhi = call_adjoint(returned, cells, slot, wind, wind_gradient, viscosity)
    result = call_edges(
        result,
        (
            shifted(xhi, "track", 1),
            shifted(xlo, "track", -1),
            shifted(yhi, "cross", 1),
            shifted(ylo, "cross", -1),
        ),
    )
    return (result, weighted)


def solution(mesh):
    placed = (
        P(None, "track", "cross", None),
        P(None, "track", "cross", None),
        P(None, "track", "cross", None),
        P("track", "cross", None),
        P("track", "cross", None, None),
        P("track", "cross", None),
        P("track", "cross", None),
        P(None, ("track", "cross"), None),
        P(("track", "cross"), None),
        P(("track", "cross"), None, None),
    )
    return jax.shard_map(
        body,
        mesh=mesh,
        in_specs=placed,
        out_specs=(P(None, "track", "cross", None), P(("track", "cross"), None)),
        check_vma=False,
    )
```

time: 1090 us -> 105 us (0.10); the launches traced: 1080 us -> 105 us
  local copies, waits for them, and re-layouts: 635 us -> 8.24 us
  other arithmetic: 380 us -> 7.99 us
  Pallas kernels: 0 us -> 36.1 us
  blocking collectives: 0 us -> 32.4 us
  starting transfers between devices: 44.7 us -> 17 us
  waiting for transfers between devices: 15 us -> 2.08 us
    scatter-add x5 -> x0, other arithmetic: 326 us -> none  [the longest x3 164 us: body(): pulled = jnp.zeros((3, direction.shape[1] * direction.shape[2] * directio...]
    gather x6 -> x0, local copies, waits for them, and re-layouts: 279 us -> none  [the longest x2 122 us: body(): picked_values = tangent.reshape(3, -1)[:, cells]]
    slice x4 -> x1, local copies, waits for them, and re-layouts: 188 us -> 1.19 us  [body(): direction[:, :, 0]]
    reshape x2, local copies, waits for them, and re-layouts: 83.1 us -> 0.02 us  [the longest x1 0.01 us: body(): cells = cells.reshape(-1, tile)]
    add x1 -> x0, local copies, waits for them, and re-layouts: 64.6 us -> none  [body(): direction + time_step * (-adv - gq + viscosity * (near_sum(padded, direct...]
    add x4 -> x1, other arithmetic: 41.2 us -> 0.77 us  [body(): sample_owner.reshape(-1) * obs + sample_gate.reshape(-1)]
    pallas_call x0 -> x4, Pallas kernels: none -> 36.1 us  [the longest x1 14.4 us: call_sample(): pl.pallas_call(functools.partial(sample_kernel, obs=obs), name='sample',...]
    all_to_all x0 -> x2, blocking collectives: none -> 32.4 us  [the longest x1 17.1 us: body(): lax.all_to_all(slots.reshape(owners, 4, lanes), names, split_axis=0, conc...]
  transfers between devices with their start and end apart: 10 -> 8, of which waited for: 3 -> 1; matrix products, arithmetic and copies ran while one was open for 20% -> 9% of each run, Pallas kernels for 0% -> 0%
where the time goes in v2:
time: 105 us
  Pallas kernels  36.1 us (34%)
  blocking collectives  32.4 us (31%)
  starting transfers between devices  17 us (16%)
  local copies, waits for them, and re-layouts  8.24 us (8%)
  other arithmetic  7.99 us (8%)
  waiting for transfers between devices  2.08 us (2%)
    all_to_all x1, blocking collectives, body(): lax.all_to_all(slots.reshape(owners, 4, lanes), names, split_axis=0, conc...  17.1 us
    ppermute x8, starting transfers between devices, shifted(): lax.ppermute(value, axis, [(i, (i + by) % count) for i in range(count)])  17 us
    all_to_all x1, blocking collectives, body(): lax.all_to_all(back, names, split_axis=0, concat_axis=0, tiled=True)  15.3 us
    pallas_call x1, Pallas kernels, call_sample(): pl.pallas_call(functools.partial(sample_kernel, obs=obs), name='sample',...  14.4 us
    pallas_call x1, Pallas kernels, call_adjoint(): pl.pallas_call(adjoint_kernel, name='adjoint', in_specs=[smem, vmem, vmem...  14 us
    sort x1, other arithmetic, body(): lax.sort((sample_cell.reshape(-1), sample_owner.reshape(-1) * obs + sampl...  6.44 us
    unnamed x20, local copies, waits for them, and re-layouts  5.98 us
    pallas_call x1, Pallas kernels, call_owner(): pl.pallas_call(owner_kernel, name='owner', in_specs=[smem, vmem, vmem, vm...  5.5 us
  transfers between devices with their start and end apart: 8, of which 1 were waited for; matrix products, arithmetic and copies ran while one was open for 9% of the time, Pallas kernels for 0%

profile of v2, /device:TPU:0, one launch (start us, length us, event | category | flops | bytes accessed | tf_op | source)
XLA Modules:
  0.0 104.5 jit_solution(16716667485570198391)
XLA Ops:
  0.6 1.2 %fusion = (f32[3,16,1,256]{3,2,1,0:T(1,128)S(1)}, f32[3,16,1,256]{3,2,1,0:T(1,128)S(1)}) fusion(f32[3,16,64,256]{3,2,1,0:T(8,128)} %field_hbm.1), kind=kLoop, calls=%fused_computation.5 | loop fusion | bytes 196608 | tf_op jit(solution)/shard_map/slice | solution.py:636
  1.8 1.6 %collective-permute-start.2 = (f32[3,16,256]{2,1,0:T(8,128)S(1)}, f32[3,16,256]{2,1,0:T(8,128)S(1)}, u32[]{:S(2)}, u32[]{:S(2)}) collective-permute-start(f32[3,16,256]{2,1,0:T(8,128)S(1)} %bitcast.24), channel_id=1, source_target_pairs={{0,1},{1,2},{2,3},{3,4},{4,5},{5,6},{6,7},{7,8},{8,9},{9,10},{10,1... | collective-permute-start | bytes 147464 | tf_op jit(solution)/shard_map/ppermute | solution.py:510
  3.5 3.8 %collective-permute-start.3 = (f32[3,16,256]{2,1,0:T(8,128)S(1)}, f32[3,16,256]{2,1,0:T(8,128)S(1)}, u32[]{:S(2)}, u32[]{:S(2)}) collective-permute-start(f32[3,16,256]{2,1,0:T(8,128)S(1)} %bitcast.25), channel_id=1, source_target_pairs={{0,15},{1,0},{2,1},{3,2},{4,3},{5,4},{6,5},{7,6},{8,7},{9,8},{10,9... | collective-permute-start | bytes 147464 | tf_op jit(solution)/shard_map/ppermute | solution.py:510
  7.3 1.0 %slice_bitcast_fusion = (f32[3,64,256]{2,1,0:T(8,128)S(1)}, f32[3,64,256]{2,1,0:T(8,128)S(1)}) fusion(f32[3,16,64,256]{3,2,1,0:T(8,128)} %field_hbm.1), kind=kLoop, calls=%fused_computation | loop fusion | bytes 786432 | tf_op jit(solution)/shard_map/squeeze | solution.py:634
  8.3 3.2 %collective-permute-start.1 = (f32[3,64,256]{2,1,0:T(8,128)S(1)}, f32[3,64,256]{2,1,0:T(8,128)S(1)}, u32[]{:S(2)}, u32[]{:S(2)}) collective-permute-start(f32[3,64,256]{2,1,0:T(8,128)S(1)} %get-tuple-element.26), channel_id=1, source_target_pairs={{0,112},{16,0},{32,16},{48,32},{64,48},{80,64},{96,80},{112,96},{1... | collective-permute-start | bytes 589832 | tf_op jit(solution)/shard_map/ppermute | solution.py:510
  11.6 0.0 collective-permute-start
  11.6 0.8 broadcast_multiply_fusion
  12.3 0.8 add.3
  13.1 6.4 %sort.15 = (s32[8192]{0:T(1024)S(1)}, s32[8192]{0:T(1024)S(1)}) sort(s32[8192]{0:T(1024)} %bitcast.27, s32[8192]{0:T(1024)S(1)} %add.3), dimensions={0}, to_apply=%region_0.0 | sort | flops 106496 | bytes 131072 | tf_op jit(solution)/shard_map/sort | solution.py:638
  19.5 0.0 copy-start.3
  19.6 0.0 copy-start.5
  19.6 0.0 slice-start
  19.6 0.0 slice-start.1
  19.6 0.0 slice-start.2
  19.6 0.0 collective-permute-done.2.ylo_ref
  19.7 0.0 collective-permute-done.3.yhi_ref
  19.7 0.0 collective-permute-done.1.xhi_ref
  19.7 0.0 collective-permute-done.xlo_ref
  19.7 0.0 copy-start
  19.7 2.0 %copy-done = f32[3,16,64,256]{3,2,1,0:T(8,128)S(1)} copy-done((f32[3,16,64,256]{3,2,1,0:T(8,128)S(1)}, f32[3,16,64,256]{3,2,1,0:T(8,128)}, u32[]{:S(2)}) %copy-start) | copy-done | bytes 3145752
  21.7 0.0 copy-start.1
  21.7 2.7 %copy-done.1 = f32[3,16,64,256]{3,2,1,0:T(8,128)S(1)} copy-done((f32[3,16,64,256]{3,2,1,0:T(8,128)S(1)}, f32[3,16,64,256]{3,2,1,0:T(8,128)}, u32[]{:S(2)}) %copy-start.1) | copy-done | bytes 3145752
  24.4 0.0 copy-start.2
  24.4 1.2 %copy-done.2 = f32[16,64,256]{2,1,0:T(8,128)S(1)} copy-done((f32[16,64,256]{2,1,0:T(8,128)S(1)}, f32[16,64,256]{2,1,0:T(8,128)}, u32[]{:S(2)}) %copy-start.2) | copy-done | bytes 1048600
  25.6 0.0 copy-start.4
  25.6 14.4 %sample.1 = (f32[64,2,4,128]{3,2,1,0:T(4,128)S(1)}, s32[32,256]{1,0:T(8,128)S(1)}) custom-call(s32[32,256]{1,0:T(8,128)S(1)} %reshape.27.cell_s.cell_ref, f32[3,16,64,256]{3,2,1,0:T(8,128)S(1)} %copy-done.1, f32[3,64,256]{2,1,0:T(8,128)S(1)} %collective-permute-done.xlo_ref, f32[3,64,256]{2,1,0:T(8,128)S(1)} %collective-permute-done.1.xhi_ref, ...), custom_call_target="tpu_custom_call" | custom-call | tf_op jit(solution)/shard_map/sample/pallas_call | solution.py:525
  40.0 17.1 %all_to_all.10.got_ref = f32[128,4,128]{2,1,0:T(4,128)S(1)} all-to-all(f32[128,4,128]{2,1,0:T(4,128)S(1)} %bitcast.22), channel_id=1, replica_groups=mesh['track'=8,'cross'=16] {'track','cross'}, dimensions={0} | all-to-all | bytes 524288 | tf_op jit(solution)/shard_map/all_to_all | solution.py:644
  57.2 0.0 copy-done.3
  57.2 0.0 copy-done.5
  57.2 0.0 copy-done.4
  57.2 5.5 %owner.1 = (f32[128,4,128]{2,1,0:T(4,128)S(1)}, f32[1,1024]{1,0:T(1,128)}) custom-call(s32[1,8]{1,0:T(1,128)S(1)} %copy-done.5, f32[128,4,128]{2,1,0:T(4,128)S(1)} %all_to_all.10.got_ref, f32[3,1,1024]{2,1,0:T(1,128)S(1)} %copy-done.4, f32[1,128,128]{2,1,0:T(8,128)S(1)} %copy-done.3), custom_call_target="tpu_custom_call" | custom-call | tf_op jit(solution)/shard_map/owner/pallas_call | solution.py:552
  62.7 15.3 %all_to_all.11 = f32[128,4,128]{2,1,0:T(4,128)S(1)} all-to-all(f32[128,4,128]{2,1,0:T(4,128)S(1)} %get-tuple-element.16), channel_id=1, replica_groups=mesh['track'=8,'cross'=16] {'track','cross'}, dimensions={0} | all-to-all | bytes 524288 | tf_op jit(solution)/shard_map/all_to_all | solution.py:646
  77.9 0.0 slice-done
  77.9 0.0 slice-done.1
  77.9 0.0 slice-done.2
  78.0 14.0 %adjoint.1 = (f32[3,16,64,256]{3,2,1,0:T(8,128)}, f32[3,64,256]{2,1,0:T(8,128)S(1)}, f32[3,64,256]{2,1,0:T(8,128)S(1)}, f32[3,16,256]{2,1,0:T(8,128)S(1)}, f32[3,16,256]{2,1,0:T(8,128)S(1)}) custom-call(s32[32,256]{1,0:T(8,128)S(1)} %reshape.27.cell_s.cell_ref, f32[64,2,4,128]{3,2,1,0:T(4,128)S(1)} %bitcast.21, s32[32,256]{1,0:T(8,128)S(1)} %reshape.27.cell_s.cell_ref, ...), custom_call_target="tpu_custom_call" | custom-call | tf_op jit(solution)/shard_map/adjoint/pallas_call | solution.py:570
  92.0 0.0 collective-permute-start.4
  92.0 2.9 %collective-permute-start.5 = (f32[3,64,256]{2,1,0:T(8,128)S(1)}, f32[3,64,256]{2,1,0:T(8,128)S(1)}, u32[]{:S(2)}, u32[]{:S(2)}) collective-permute-start(f32[3,64,256]{2,1,0:T(8,128)S(1)} %get-tuple-element.20), channel_id=1, source_target_pairs={{0,112},{16,0},{32,16},{48,32},{64,48},{80,64},{96,80},{112,96},{1... | collective-permute-start | bytes 589832 | tf_op jit(solution)/shard_map/ppermute | solution.py:510
  95.0 0.6 collective-permute-start.6
  95.6 4.7 %collective-permute-start.7 = (f32[3,16,256]{2,1,0:T(8,128)S(1)}, f32[3,16,256]{2,1,0:T(8,128)S(1)}, u32[]{:S(2)}, u32[]{:S(2)}) collective-permute-start(f32[3,16,256]{2,1,0:T(8,128)S(1)} %get-tuple-element.22), channel_id=1, source_target_pairs={{0,15},{1,0},{2,1},{3,2},{4,3},{5,4},{6,5},{7,6},{8,7},{9,8},{10,9... | collective-permute-start | bytes 147464 | tf_op jit(solution)/shard_map/ppermute | solution.py:510
  100.3 2.1 %collective-permute-done.6.ylo_ref = f32[3,16,256]{2,1,0:T(8,128)S(1)} collective-permute-done((f32[3,16,256]{2,1,0:T(8,128)S(1)}, f32[3,16,256]{2,1,0:T(8,128)S(1)}, u32[]{:S(2)}, u32[]{:S(2)}) %collective-permute-start.6) | collective-permute-done | bytes 49184 | tf_op jit(solution)/shard_map/ppermute | solution.py:510
  102.4 0.0 collective-permute-done.7.yhi_ref
  102.4 0.0 collective-permute-done.4.xlo_ref
  102.4 0.0 collective-permute-done.5.xhi_ref
  102.4 2.1 %edges.1 = f32[3,16,64,256]{3,2,1,0:T(8,128)} custom-call(f32[3,16,64,256]{3,2,1,0:T(8,128)} %get-tuple-element.18.given_ref, f32[3,64,256]{2,1,0:T(8,128)S(1)} %collective-permute-done.4.xlo_ref, f32[3,64,256]{2,1,0:T(8,128)S(1)} %collective-permute-done.5.xhi_ref, ...), custom_call_target="tpu_custom_call", output_to_operand_aliasing={{}: (0, {})} | custom-call | tf_op jit(solution)/shard_map/edges/pallas_call | solution.py:598
  (5 shorter events, 0.0 us)
Async XLA Ops:
  1.8 17.8 %collective-permute-start.2 = (f32[3,16,256]{2,1,0:T(8,128)S(1)}, f32[3,16,256]{2,1,0:T(8,128)S(1)}, u32[]{:S(2)}, u32[]{:S(2)}) collective-permute-start(f32[3,16,256]{2,1,0:T(8,128)S(1)} %bitcast.24), channel_id=1, source_target_pairs={{0,1},{1,2},{2,3},{3,4},{4,5},{5,6},{6,7},{7,8},{8,9},{9,10},{10,1... | collective-permute-start | bytes 147464 | tf_op jit(solution)/shard_map/ppermute | solution.py:510
  3.5 16.2 %collective-permute-start.3 = (f32[3,16,256]{2,1,0:T(8,128)S(1)}, f32[3,16,256]{2,1,0:T(8,128)S(1)}, u32[]{:S(2)}, u32[]{:S(2)}) collective-permute-start(f32[3,16,256]{2,1,0:T(8,128)S(1)} %bitcast.25), channel_id=1, source_target_pairs={{0,15},{1,0},{2,1},{3,2},{4,3},{5,4},{6,5},{7,6},{8,7},{9,8},{10,9... | collective-permute-start | bytes 147464 | tf_op jit(solution)/shard_map/ppermute | solution.py:510
  8.3 11.3 %collective-permute-start.1 = (f32[3,64,256]{2,1,0:T(8,128)S(1)}, f32[3,64,256]{2,1,0:T(8,128)S(1)}, u32[]{:S(2)}, u32[]{:S(2)}) collective-permute-start(f32[3,64,256]{2,1,0:T(8,128)S(1)} %get-tuple-element.26), channel_id=1, source_target_pairs={{0,112},{16,0},{32,16},{48,32},{64,48},{80,64},{96,80},{112,96},{1... | collective-permute-start | bytes 589832 | tf_op jit(solution)/shard_map/ppermute | solution.py:510
  11.6 8.1 %collective-permute-start = (f32[3,64,256]{2,1,0:T(8,128)S(1)}, f32[3,64,256]{2,1,0:T(8,128)S(1)}, u32[]{:S(2)}, u32[]{:S(2)}) collective-permute-start(f32[3,64,256]{2,1,0:T(8,128)S(1)} %get-tuple-element.27), channel_id=1, source_target_pairs={{0,16},{16,32},{32,48},{48,64},{64,80},{80,96},{96,112},{112,0},{1... | collective-permute-start | bytes 589832 | tf_op jit(solution)/shard_map/ppermute | solution.py:510
  19.5 37.6 %copy-start.3 = (f32[1,128,128]{2,1,0:T(8,128)S(1)}, f32[1,128,128]{2,1,0:T(8,128)}, u32[]{:S(2)}) copy-start(f32[1,128,128]{2,1,0:T(8,128)} %precision_ref.1) | copy-start | bytes 196612
  19.6 37.6 %copy-start.5 = (s32[1,8]{1,0:T(1,128)S(1)}, s32[1,8]{1,0:T(1,128)}, u32[]{:S(2)}) copy-start(s32[1,8]{1,0:T(1,128)} %counts_s.1) | copy-start | bytes 100
  19.6 58.4 %slice-start = ((s8[9437184]{0:T(1024)(128)(4,1)}), s8[1048576]{0:T(1024)(128)(4,1)S(1)}, s32[]{:S(2)}) async-start(s8[9437184]{0:T(1024)(128)(4,1)} %bitcast.19), calls=%async_computation.2 | async-start | bytes 2097152
  19.6 58.3 %slice-start.1 = ((s8[9437184]{0:T(1024)(128)(4,1)}), s8[4194304]{0:T(1024)(128)(4,1)S(1)}, s32[]{:S(2)}) async-start(s8[9437184]{0:T(1024)(128)(4,1)} %bitcast.19), calls=%async_computation.3 | async-start | bytes 8388608
  19.6 58.3 %slice-start.2 = ((s8[9437184]{0:T(1024)(128)(4,1)}), s8[4194304]{0:T(1024)(128)(4,1)S(1)}, s32[]{:S(2)}) async-start(s8[9437184]{0:T(1024)(128)(4,1)} %bitcast.19), calls=%async_computation.4 | async-start | bytes 8388608
  19.7 2.0 %copy-start = (f32[3,16,64,256]{3,2,1,0:T(8,128)S(1)}, f32[3,16,64,256]{3,2,1,0:T(8,128)}, u32[]{:S(2)}) copy-start(f32[3,16,64,256]{3,2,1,0:T(8,128)} %wind_hbm.3) | copy-start | bytes 9437188
  21.7 2.7 %copy-start.1 = (f32[3,16,64,256]{3,2,1,0:T(8,128)S(1)}, f32[3,16,64,256]{3,2,1,0:T(8,128)}, u32[]{:S(2)}) copy-start(f32[3,16,64,256]{3,2,1,0:T(8,128)} %field_hbm.1) | copy-start | bytes 9437188
  24.4 1.2 %copy-start.2 = (f32[16,64,256]{2,1,0:T(8,128)S(1)}, f32[16,64,256]{2,1,0:T(8,128)}, u32[]{:S(2)}) copy-start(f32[16,64,256]{2,1,0:T(8,128)} %visc_hbm.3) | copy-start | bytes 3145732
  25.6 31.5 %copy-start.4 = (f32[3,1,1024]{2,1,0:T(1,128)S(1)}, f32[3,1,1024]{2,1,0:T(1,128)}, u32[]{:S(2)}) copy-start(f32[3,1,1024]{2,1,0:T(1,128)} %sight_ref.1) | copy-start | bytes 36868
  92.0 10.4 %collective-permute-start.4 = (f32[3,64,256]{2,1,0:T(8,128)S(1)}, f32[3,64,256]{2,1,0:T(8,128)S(1)}, u32[]{:S(2)}, u32[]{:S(2)}) collective-permute-start(f32[3,64,256]{2,1,0:T(8,128)S(1)} %get-tuple-element.19), channel_id=1, source_target_pairs={{0,16},{16,32},{32,48},{48,64},{64,80},{80,96},{96,112},{112,0},{1... | collective-permute-start | bytes 589832 | tf_op jit(solution)/shard_map/ppermute | solution.py:510
  92.0 10.4 %collective-permute-start.5 = (f32[3,64,256]{2,1,0:T(8,128)S(1)}, f32[3,64,256]{2,1,0:T(8,128)S(1)}, u32[]{:S(2)}, u32[]{:S(2)}) collective-permute-start(f32[3,64,256]{2,1,0:T(8,128)S(1)} %get-tuple-element.20), channel_id=1, source_target_pairs={{0,112},{16,0},{32,16},{48,32},{64,48},{80,64},{96,80},{112,96},{1... | collective-permute-start | bytes 589832 | tf_op jit(solution)/shard_map/ppermute | solution.py:510
  95.0 7.4 %collective-permute-start.6 = (f32[3,16,256]{2,1,0:T(8,128)S(1)}, f32[3,16,256]{2,1,0:T(8,128)S(1)}, u32[]{:S(2)}, u32[]{:S(2)}) collective-permute-start(f32[3,16,256]{2,1,0:T(8,128)S(1)} %get-tuple-element.21), channel_id=1, source_target_pairs={{0,1},{1,2},{2,3},{3,4},{4,5},{5,6},{6,7},{7,8},{8,9},{9,10},{10,1... | collective-permute-start | bytes 147464 | tf_op jit(solution)/shard_map/ppermute | solution.py:510
  95.6 6.8 %collective-permute-start.7 = (f32[3,16,256]{2,1,0:T(8,128)S(1)}, f32[3,16,256]{2,1,0:T(8,128)S(1)}, u32[]{:S(2)}, u32[]{:S(2)}) collective-permute-start(f32[3,16,256]{2,1,0:T(8,128)S(1)} %get-tuple-element.22), channel_id=1, source_target_pairs={{0,15},{1,0},{2,1},{3,2},{4,3},{5,4},{6,5},{7,6},{8,7},{9,8},{10,9... | collective-permute-start | bytes 147464 | tf_op jit(solution)/shard_map/ppermute | solution.py:510

commit v3 on v2

--- a/solution.py
+++ b/solution.py
@@ -1,5 +1,3 @@
-import functools
-
 import jax
 import jax.numpy as jnp
 from jax import lax
@@ -13,7 +11,7 @@
 lanes = 128
 span = 64
 strip = 16
-batch = 4
+batch = 2
 row_bits = 8
 f32 = jnp.float32
 bf16 = jnp.bfloat16
@@ -64,7 +62,7 @@
         visit(t, base)
         return jnp.maximum(most, over)
 
-    most = lax.fori_loop(0, tiles, first, i32(0), unroll=8)
+    most = lax.fori_loop(0, tiles, first, i32(0), unroll=16)
 
     @pl.when(most > 0)
     def _():
@@ -97,7 +95,8 @@
     grad_hbm,
     visc_hbm,
     cell_ref,
-    og_ref,
+    owner_ref,
+    gate_ref,
     slots_ref,
     slot_ref,
     field_ref,
@@ -110,8 +109,6 @@
     upper_ref,
     total_ref,
     sems,
-    *,
-    obs,
 ):
     nx, cy, nz = visc_ref.shape
     tiles = cell_ref.shape[0]
@@ -144,7 +141,7 @@
     upper_ref[...] = ones_at(a <= b)
 
     def rank(t, carry):
-        own = og_ref[pl.ds(t, 1), :] // obs
+        own = owner_ref[pl.ds(t, 1), :]
         mask = rows_equal(owners, own)
         counts = dot_nn(ones_at(mask), upper_ref[...])
         offset = offset_ref[...]
@@ -153,7 +150,7 @@
         offset_ref[...] = offset + jnp.broadcast_to(counts[:, tile - 1 : tile], offset.shape)
         return carry
 
-    lax.fori_loop(0, tiles, rank, 0, unroll=8)
+    lax.fori_loop(0, tiles, rank, 0, unroll=16)
 
     y_at = lax.broadcasted_iota(i32, (strip, nz), 0)
     z_at = lax.broadcasted_iota(i32, (strip, nz), 1)
@@ -229,7 +226,7 @@
 
     def add_tile(t, carry):
         line, column = slot_parts(slot_ref[pl.ds(t, 1), :])
-        gate = og_ref[pl.ds(t, 1), :] % obs
+        gate = gate_ref[pl.ds(t, 1), :]
         mask = rows_equal(half, line)
         columns = onehot(2 * lanes, column)
         low = gate % lanes
@@ -248,7 +245,7 @@
         total_ref[...] += dot_nt(left, jnp.concatenate([columns, columns], axis=1))
         return carry
 
-    lax.fori_loop(0, tiles, add_tile, 0, unroll=8)
+    lax.fori_loop(0, tiles, add_tile, 0, unroll=16)
     for c in range(4):
         for h in range(2):
             slots_ref[:, h, c, :] = total_ref[c * half : (c + 1) * half, h * lanes : (h + 1) * lanes]
@@ -269,7 +266,7 @@
     def collect(i, acc):
         rows = gathered(i)
         gate = rows[3:4].astype(i32)
-        gates = ones_at(rows_equal(lanes, gate % lanes))
+        gates = onehot(lanes, gate % lanes)
         gate_ref[i] = gates
         mask = beam_mask(gate)
         parts = []
@@ -280,7 +277,7 @@
         left = jnp.concatenate(parts, axis=0).astype(bf16)
         return acc + dot_nt(left, gates)
 
-    acc = lax.fori_loop(0, sources // group, collect, jnp.zeros((6 * beams, lanes), f32), unroll=4)
+    acc = lax.fori_loop(0, sources // group, collect, jnp.zeros((6 * beams, lanes), f32), unroll=8)
     sights = [
         jnp.concatenate([sight_ref[k, :, b * lanes : (b + 1) * lanes] for b in range(beams)], axis=0)
         for k in range(3)
@@ -300,13 +297,14 @@
         weighted_ref[:, b * lanes : (b + 1) * lanes] = weighted[b : b + 1]
     spread = jnp.concatenate([s * weighted for s in sights], axis=0)
     head = spread.astype(bf16).astype(f32)
-    table = jnp.concatenate([head, spread - head], axis=1).astype(bf16)
+    table = jnp.concatenate([head, spread - head], axis=0).astype(bf16)
 
     def give(i, carry):
         gate = gathered(i)[3:4].astype(i32)
         mask = beam_mask(gate)
         gates = gate_ref[i]
-        found = dot_nn(table, jnp.concatenate([gates, gates], axis=0))
+        found = dot_nn(table, gates)
+        found = found[: 3 * beams] + found[3 * beams :]
         rows = jnp.concatenate(
             [pick(mask, found[k * beams : (k + 1) * beams]) for k in range(3)] + [jnp.zeros((1, wide), f32)], axis=0
         )
@@ -314,7 +312,7 @@
             back_ref[i * group + j] = rows[:, j * lanes : (j + 1) * lanes]
         return carry
 
-    lax.fori_loop(0, sources // group, give, 0, unroll=4)
+    lax.fori_loop(0, sources // group, give, 0, unroll=8)
 
 
 def adjoint_kernel(
@@ -359,19 +357,20 @@
         for h in range(2):
             head, rest = split(back_ref[:, h, c, :])
             table_ref[c * half : (c + 1) * half, h * lanes : (h + 1) * lanes] = head
-            table_ref[c * half : (c + 1) * half, (2 + h) * lanes : (3 + h) * lanes] = rest
+            table_ref[(3 + c) * half : (4 + c) * half, h * lanes : (h + 1) * lanes] = rest
     plane_ref[...] = jnp.zeros_like(plane_ref)
 
     def restore(t, carry):
         line, column = slot_parts(slot_ref[pl.ds(t, 1), :])
         mask = rows_equal(half, line)
         columns = onehot(2 * lanes, column)
-        found = dot_nn(table_ref[...], jnp.concatenate([columns, columns], axis=0))
+        found = dot_nn(table_ref[...], columns)
+        found = found[: 3 * half] + found[3 * half :]
         for c in range(3):
             value_ref[c, pl.ds(t, 1), :] = pick(mask, found[c * half : (c + 1) * half])
         return carry
 
-    lax.fori_loop(0, tiles, restore, 0, unroll=8)
+    lax.fori_loop(0, tiles, restore, 0, unroll=16)
 
     def put(t, begin, least):
         cells = cell_ref[pl.ds(t, 1), :]
@@ -383,8 +382,8 @@
             head, rest = split(value_ref[c, pl.ds(t, 1), :])
             heads.append(jnp.where(mask, head.astype(f32), 0.0).astype(bf16))
             rests.append(jnp.where(mask, rest.astype(f32), 0.0).astype(bf16))
-        left = jnp.concatenate([jnp.concatenate(heads, axis=0), jnp.concatenate(rests, axis=0)], axis=1)
-        added = dot_nt(left, jnp.concatenate([zs, zs], axis=1))
+        added = dot_nt(jnp.concatenate(heads + rests, axis=0), zs)
+        added = added[: 3 * span] + added[3 * span :]
         for c in range(3):
             plane_ref[c, pl.ds(begin, span), :] += added[c * span : (c + 1) * span]
 
@@ -515,17 +514,21 @@
 hbm = pl.BlockSpec(memory_space=pltpu.HBM)
 
 
+def held(value):
+    return pltpu.with_memory_space_constraint(value, pltpu.HBM)
+
+
 def room(mib):
     return pltpu.CompilerParams(vmem_limit_bytes=mib << 20)
 
 
-def call_sample(direction, halo, wind, wind_gradient, viscosity, cells, og, owners, obs):
+def call_sample(direction, halo, wind, wind_gradient, viscosity, cells, owner, gate, owners):
     _, cx, cy, nz = direction.shape
     tiles = cells.shape[0]
     return pl.pallas_call(
-        functools.partial(sample_kernel, obs=obs),
+        sample_kernel,
         name="sample",
-        in_specs=[smem, hbm, vmem, vmem, vmem, vmem, hbm, hbm, hbm, vmem, vmem],
+        in_specs=[smem, hbm, vmem, vmem, vmem, vmem, hbm, hbm, hbm, vmem, vmem, vmem],
         out_specs=[vmem, vmem],
         scratch_shapes=[
             pltpu.VMEM((3, cx + 2, cy, nz), f32),
@@ -544,7 +547,7 @@
             jax.ShapeDtypeStruct((tiles, tile), i32),
         ],
         compiler_params=room(40),
-    )(cells, direction, *halo, wind, wind_gradient, viscosity, cells, og)
+    )(cells, held(direction), *halo, held(wind), held(wind_gradient), held(viscosity), cells, owner, gate)
 
 
 def call_owner(gate_counts, got, sight, precision):
@@ -576,7 +579,7 @@
             pltpu.VMEM((3, cx, cy, nz), f32),
             pltpu.VMEM((9, cx, cy, nz), f32),
             pltpu.VMEM((cx, cy, nz), f32),
-            pltpu.VMEM((3 * half, 4 * lanes), bf16),
+            pltpu.VMEM((6 * half, 2 * lanes), bf16),
             pltpu.VMEM((3, tiles, tile), f32),
             pltpu.VMEM((3, cx * cy, nz), f32),
             pltpu.VMEM((3, cx + 2, cy, nz), f32),
@@ -590,7 +593,7 @@
             jax.ShapeDtypeStruct((3, cx, nz), f32),
         ],
         compiler_params=room(40),
-    )(cells, returned, cells, slot, wind, wind_gradient, viscosity)
+    )(cells, returned, cells, slot, held(wind), held(wind_gradient), held(viscosity))
 
 
 def call_edges(result, halo):
@@ -627,7 +630,6 @@
 ):
     _, cx, cy, nz = direction.shape
     owners = lax.axis_size("track") * lax.axis_size("cross")
-    obs = sight.shape[2]
     names = ("track", "cross")
     halo = (
         shifted(direction[:, cx - 1], "track", 1),
@@ -635,12 +637,13 @@
         shifted(direction[:, :, cy - 1], "cross", 1),
         shifted(direction[:, :, 0], "cross", -1),
     )
-    cells, og = lax.sort(
-        (sample_cell.reshape(-1), sample_owner.reshape(-1) * obs + sample_gate.reshape(-1)), num_keys=1, is_stable=False
-    )
-    cells = cells.reshape(-1, tile)
-    og = og.reshape(-1, tile)
-    slots, slot = call_sample(direction, halo, wind, wind_gradient, viscosity, cells, og, owners, obs)
+    cells, owner, gate = [
+        v.reshape(-1, tile)
+        for v in lax.sort(
+            (sample_cell.reshape(-1), sample_owner.reshape(-1), sample_gate.reshape(-1)), num_keys=1, is_stable=False
+        )
+    ]
+    slots, slot = call_sample(direction, halo, wind, wind_gradient, viscosity, cells, owner, gate, owners)
     got = lax.all_to_all(slots.reshape(owners, 4, lanes), names, split_axis=0, concat_axis=0, tiled=True)
     back, weighted = call_owner(gate_counts, got, sight, precision)
     returned = lax.all_to_all(back, names, split_axis=0, concat_axis=0, tiled=True)

time: 105 us -> 91.4 us (0.87)
  Pallas kernels: 36.1 us -> 29.9 us
  local copies, waits for them, and re-layouts: 8.24 us -> 2.3 us
  other arithmetic: 7.99 us -> 6.52 us
    unnamed x20 -> x8, local copies, waits for them, and re-layouts: 5.98 us -> 0.03 us
    pallas_call x1, Pallas kernels: 14 us -> 11.4 us  [call_adjoint(): pl.pallas_call(adjoint_kernel, name='adjoint', in_specs=[smem, vmem, vmem...]
    pallas_call x1, Pallas kernels: 5.5 us -> 3.56 us  [call_owner(): pl.pallas_call(owner_kernel, name='owner', in_specs=[smem, vmem, vmem, vm...]
    pallas_call x1, Pallas kernels: 14.4 us -> 12.8 us  [call_sample(): pl.pallas_call(sample_kernel, name='sample', in_specs=[smem, hbm, vmem, v...]
where the time goes in v3:
time: 91.4 us; the launch traced here: 91.1 us
  blocking collectives  32 us (35%)
  Pallas kernels  29.9 us (33%)
  starting transfers between devices  17.3 us (19%)
  other arithmetic  6.52 us (7%)
  local copies, waits for them, and re-layouts  2.3 us (3%)
  waiting for transfers between devices  2.08 us (2%)
  between operations  0.94 us (1%)
    ppermute x8, starting transfers between devices, shifted(): lax.ppermute(value, axis, [(i, (i + by) % count) for i in range(count)])  17.3 us
    all_to_all x1, blocking collectives, body(): lax.all_to_all(slots.reshape(owners, 4, lanes), names, split_axis=0, conc...  16.8 us
    all_to_all x1, blocking collectives, body(): lax.all_to_all(back, names, split_axis=0, concat_axis=0, tiled=True)  15.3 us
    pallas_call x1, Pallas kernels, call_sample(): pl.pallas_call(sample_kernel, name='sample', in_specs=[smem, hbm, vmem, v...  12.8 us
    pallas_call x1, Pallas kernels, call_adjoint(): pl.pallas_call(adjoint_kernel, name='adjoint', in_specs=[smem, vmem, vmem...  11.4 us
    sort x1, other arithmetic, body(): lax.sort((sample_cell.reshape(-1), sample_owner.reshape(-1), sample_gate....  6.52 us
    pallas_call x1, Pallas kernels, call_owner(): pl.pallas_call(owner_kernel, name='owner', in_specs=[smem, vmem, vmem, vm...  3.56 us
    pallas_call x1, Pallas kernels, call_edges(): pl.pallas_call(edge_kernel, name='edges', in_specs=[hbm, vmem, vmem, vmem...  2.13 us
  transfers between devices with their start and end apart: 8, of which 1 were waited for; matrix products, arithmetic and copies ran while one was open for 9% of the time, Pallas kernels for 0%

profile of v3, /device:TPU:0, one launch (start us, length us, event | category | flops | bytes accessed | tf_op | source)
XLA Modules:
  0.0 91.1 jit_solution(2240541705450406265)
XLA Ops:
  0.6 1.1 %slice_bitcast_fusion = (f32[3,64,256]{2,1,0:T(8,128)S(1)}, f32[3,64,256]{2,1,0:T(8,128)S(1)}) fusion(f32[3,16,64,256]{3,2,1,0:T(8,128)} %field_hbm.1), kind=kLoop, calls=%fused_computation | loop fusion | bytes 786432 | tf_op jit(solution)/shard_map/squeeze | solution.py:636
  1.7 3.6 %collective-permute-start.1 = (f32[3,64,256]{2,1,0:T(8,128)S(1)}, f32[3,64,256]{2,1,0:T(8,128)S(1)}, u32[]{:S(2)}, u32[]{:S(2)}) collective-permute-start(f32[3,64,256]{2,1,0:T(8,128)S(1)} %get-tuple-element.28), channel_id=1, source_target_pairs={{0,112},{16,0},{32,16},{48,32},{64,48},{80,64},{96,80},{112,96},{1... | collective-permute-start | bytes 589832 | tf_op jit(solution)/shard_map/ppermute | solution.py:509
  5.3 0.0 collective-permute-start
  5.3 1.2 %fusion = (f32[3,16,1,256]{3,2,1,0:T(1,128)S(1)}, f32[3,16,1,256]{3,2,1,0:T(1,128)S(1)}) fusion(f32[3,16,64,256]{3,2,1,0:T(8,128)} %field_hbm.1), kind=kLoop, calls=%fused_computation.4 | loop fusion | bytes 196608 | tf_op jit(solution)/shard_map/slice | solution.py:638
  6.5 1.6 %collective-permute-start.2 = (f32[3,16,256]{2,1,0:T(8,128)S(1)}, f32[3,16,256]{2,1,0:T(8,128)S(1)}, u32[]{:S(2)}, u32[]{:S(2)}) collective-permute-start(f32[3,16,256]{2,1,0:T(8,128)S(1)} %bitcast.21), channel_id=1, source_target_pairs={{0,1},{1,2},{2,3},{3,4},{4,5},{5,6},{6,7},{7,8},{8,9},{9,10},{10,1... | collective-permute-start | bytes 147464 | tf_op jit(solution)/shard_map/ppermute | solution.py:509
  8.0 3.9 %collective-permute-start.3 = (f32[3,16,256]{2,1,0:T(8,128)S(1)}, f32[3,16,256]{2,1,0:T(8,128)S(1)}, u32[]{:S(2)}, u32[]{:S(2)}) collective-permute-start(f32[3,16,256]{2,1,0:T(8,128)S(1)} %bitcast.22), channel_id=1, source_target_pairs={{0,15},{1,0},{2,1},{3,2},{4,3},{5,4},{6,5},{7,6},{8,7},{9,8},{10,9... | collective-permute-start | bytes 147464 | tf_op jit(solution)/shard_map/ppermute | solution.py:509
  11.9 6.5 %sort.21 = (s32[8192]{0:T(1024)S(1)}, s32[8192]{0:T(1024)S(1)}, s32[8192]{0:T(1024)S(1)}) sort(s32[8192]{0:T(1024)} %bitcast.23, s32[8192]{0:T(1024)} %bitcast.24, s32[8192]{0:T(1024)} %bitcast.25), dimensions={0}, to_apply=%region_0.0 | sort | flops 106496 | bytes 196608 | tf_op jit(solution)/shard_map/sort | solution.py:642
  18.5 0.0 copy-start
  18.5 0.0 copy-start.1
  18.5 0.0 copy-start.2
  18.5 0.0 collective-permute-done.2.ylo_ref
  18.5 0.0 collective-permute-done.3.yhi_ref
  18.5 0.0 collective-permute-done.1.xhi_ref
  18.5 0.0 collective-permute-done.xlo_ref
  18.5 12.8 %sample.1 = (f32[64,2,4,128]{3,2,1,0:T(4,128)S(1)}, s32[32,256]{1,0:T(8,128)S(1)}) custom-call(s32[32,256]{1,0:T(8,128)S(1)} %reshape.31.cell_s.cell_ref, f32[3,16,64,256]{3,2,1,0:T(8,128)} %field_hbm.1, f32[3,64,256]{2,1,0:T(8,128)S(1)} %collective-permute-done.xlo_ref, f32[3,64,256]{2,1,0:T(8,128)S(1)} %collective-permute-done.1.xhi_ref, ...), custom_call_target="tpu_custom_call" | custom-call | tf_op jit(solution)/shard_map/sample/pallas_call | solution.py:528
  31.4 16.8 %all_to_all.10.got_ref = f32[128,4,128]{2,1,0:T(4,128)S(1)} all-to-all(f32[128,4,128]{2,1,0:T(4,128)S(1)} %bitcast.20), channel_id=1, replica_groups=mesh['track'=8,'cross'=16] {'track','cross'}, dimensions={0} | all-to-all | bytes 524288 | tf_op jit(solution)/shard_map/all_to_all | solution.py:647
  48.1 0.0 copy-done
  48.2 0.0 copy-done.1
  48.2 0.0 copy-done.2
  48.2 3.6 %owner.1 = (f32[128,4,128]{2,1,0:T(4,128)S(1)}, f32[1,1024]{1,0:T(1,128)}) custom-call(s32[1,8]{1,0:T(1,128)S(1)} %copy-done.2, f32[128,4,128]{2,1,0:T(4,128)S(1)} %all_to_all.10.got_ref, f32[3,1,1024]{2,1,0:T(1,128)S(1)} %copy-done.1, f32[1,128,128]{2,1,0:T(8,128)S(1)} %copy-done), custom_call_target="tpu_custom_call" | custom-call | tf_op jit(solution)/shard_map/owner/pallas_call | solution.py:555
  51.7 15.3 %all_to_all.11 = f32[128,4,128]{2,1,0:T(4,128)S(1)} all-to-all(f32[128,4,128]{2,1,0:T(4,128)S(1)} %get-tuple-element.18), channel_id=1, replica_groups=mesh['track'=8,'cross'=16] {'track','cross'}, dimensions={0} | all-to-all | bytes 524288 | tf_op jit(solution)/shard_map/all_to_all | solution.py:649
  67.0 11.4 %adjoint.1 = (f32[3,16,64,256]{3,2,1,0:T(8,128)}, f32[3,64,256]{2,1,0:T(8,128)S(1)}, f32[3,64,256]{2,1,0:T(8,128)S(1)}, f32[3,16,256]{2,1,0:T(8,128)S(1)}, f32[3,16,256]{2,1,0:T(8,128)S(1)}) custom-call(s32[32,256]{1,0:T(8,128)S(1)} %reshape.31.cell_s.cell_ref, f32[64,2,4,128]{3,2,1,0:T(4,128)S(1)} %bitcast.19, s32[32,256]{1,0:T(8,128)S(1)} %reshape.31.cell_s.cell_ref, ...), custom_call_target="tpu_custom_call" | custom-call | tf_op jit(solution)/shard_map/adjoint/pallas_call | solution.py:573
  78.4 0.0 collective-permute-start.4
  78.5 2.9 %collective-permute-start.5 = (f32[3,64,256]{2,1,0:T(8,128)S(1)}, f32[3,64,256]{2,1,0:T(8,128)S(1)}, u32[]{:S(2)}, u32[]{:S(2)}) collective-permute-start(f32[3,64,256]{2,1,0:T(8,128)S(1)} %get-tuple-element.22), channel_id=1, source_target_pairs={{0,112},{16,0},{32,16},{48,32},{64,48},{80,64},{96,80},{112,96},{1... | collective-permute-start | bytes 589832 | tf_op jit(solution)/shard_map/ppermute | solution.py:509
  81.4 0.6 collective-permute-start.6
  82.0 4.7 %collective-permute-start.7 = (f32[3,16,256]{2,1,0:T(8,128)S(1)}, f32[3,16,256]{2,1,0:T(8,128)S(1)}, u32[]{:S(2)}, u32[]{:S(2)}) collective-permute-start(f32[3,16,256]{2,1,0:T(8,128)S(1)} %get-tuple-element.24), channel_id=1, source_target_pairs={{0,15},{1,0},{2,1},{3,2},{4,3},{5,4},{6,5},{7,6},{8,7},{9,8},{10,9... | collective-permute-start | bytes 147464 | tf_op jit(solution)/shard_map/ppermute | solution.py:509
  86.7 2.1 %collective-permute-done.6.ylo_ref = f32[3,16,256]{2,1,0:T(8,128)S(1)} collective-permute-done((f32[3,16,256]{2,1,0:T(8,128)S(1)}, f32[3,16,256]{2,1,0:T(8,128)S(1)}, u32[]{:S(2)}, u32[]{:S(2)}) %collective-permute-start.6) | collective-permute-done | bytes 49184 | tf_op jit(solution)/shard_map/ppermute | solution.py:509
  88.8 0.0 collective-permute-done.7.yhi_ref
  88.8 0.0 collective-permute-done.4.xlo_ref
  88.8 0.0 collective-permute-done.5.xhi_ref
  88.8 2.1 %edges.1 = f32[3,16,64,256]{3,2,1,0:T(8,128)} custom-call(f32[3,16,64,256]{3,2,1,0:T(8,128)} %get-tuple-element.20.given_ref, f32[3,64,256]{2,1,0:T(8,128)S(1)} %collective-permute-done.4.xlo_ref, f32[3,64,256]{2,1,0:T(8,128)S(1)} %collective-permute-done.5.xhi_ref, ...), custom_call_target="tpu_custom_call", output_to_operand_aliasing={{}: (0, {})} | custom-call | tf_op jit(solution)/shard_map/edges/pallas_call | solution.py:601
  (5 shorter events, 0.0 us)
Async XLA Ops:
  1.7 16.8 %collective-permute-start.1 = (f32[3,64,256]{2,1,0:T(8,128)S(1)}, f32[3,64,256]{2,1,0:T(8,128)S(1)}, u32[]{:S(2)}, u32[]{:S(2)}) collective-permute-start(f32[3,64,256]{2,1,0:T(8,128)S(1)} %get-tuple-element.28), channel_id=1, source_target_pairs={{0,112},{16,0},{32,16},{48,32},{64,48},{80,64},{96,80},{112,96},{1... | collective-permute-start | bytes 589832 | tf_op jit(solution)/shard_map/ppermute | solution.py:509
  5.3 13.3 %collective-permute-start = (f32[3,64,256]{2,1,0:T(8,128)S(1)}, f32[3,64,256]{2,1,0:T(8,128)S(1)}, u32[]{:S(2)}, u32[]{:S(2)}) collective-permute-start(f32[3,64,256]{2,1,0:T(8,128)S(1)} %get-tuple-element.29), channel_id=1, source_target_pairs={{0,16},{16,32},{32,48},{48,64},{64,80},{80,96},{96,112},{112,0},{1... | collective-permute-start | bytes 589832 | tf_op jit(solution)/shard_map/ppermute | solution.py:509
  6.5 12.0 %collective-permute-start.2 = (f32[3,16,256]{2,1,0:T(8,128)S(1)}, f32[3,16,256]{2,1,0:T(8,128)S(1)}, u32[]{:S(2)}, u32[]{:S(2)}) collective-permute-start(f32[3,16,256]{2,1,0:T(8,128)S(1)} %bitcast.21), channel_id=1, source_target_pairs={{0,1},{1,2},{2,3},{3,4},{4,5},{5,6},{6,7},{7,8},{8,9},{9,10},{10,1... | collective-permute-start | bytes 147464 | tf_op jit(solution)/shard_map/ppermute | solution.py:509
  8.0 10.5 %collective-permute-start.3 = (f32[3,16,256]{2,1,0:T(8,128)S(1)}, f32[3,16,256]{2,1,0:T(8,128)S(1)}, u32[]{:S(2)}, u32[]{:S(2)}) collective-permute-start(f32[3,16,256]{2,1,0:T(8,128)S(1)} %bitcast.22), channel_id=1, source_target_pairs={{0,15},{1,0},{2,1},{3,2},{4,3},{5,4},{6,5},{7,6},{8,7},{9,8},{10,9... | collective-permute-start | bytes 147464 | tf_op jit(solution)/shard_map/ppermute | solution.py:509
  18.5 29.7 %copy-start = (f32[1,128,128]{2,1,0:T(8,128)S(1)}, f32[1,128,128]{2,1,0:T(8,128)}, u32[]{:S(2)}) copy-start(f32[1,128,128]{2,1,0:T(8,128)} %precision_ref.1) | copy-start | bytes 196612
  18.5 29.7 %copy-start.1 = (f32[3,1,1024]{2,1,0:T(1,128)S(1)}, f32[3,1,1024]{2,1,0:T(1,128)}, u32[]{:S(2)}) copy-start(f32[3,1,1024]{2,1,0:T(1,128)} %sight_ref.1) | copy-start | bytes 36868
  18.5 29.7 %copy-start.2 = (s32[1,8]{1,0:T(1,128)S(1)}, s32[1,8]{1,0:T(1,128)}, u32[]{:S(2)}) copy-start(s32[1,8]{1,0:T(1,128)} %counts_s.1) | copy-start | bytes 100
  78.4 10.4 %collective-permute-start.4 = (f32[3,64,256]{2,1,0:T(8,128)S(1)}, f32[3,64,256]{2,1,0:T(8,128)S(1)}, u32[]{:S(2)}, u32[]{:S(2)}) collective-permute-start(f32[3,64,256]{2,1,0:T(8,128)S(1)} %get-tuple-element.21), channel_id=1, source_target_pairs={{0,16},{16,32},{32,48},{48,64},{64,80},{80,96},{96,112},{112,0},{1... | collective-permute-start | bytes 589832 | tf_op jit(solution)/shard_map/ppermute | solution.py:509
  78.5 10.4 %collective-permute-start.5 = (f32[3,64,256]{2,1,0:T(8,128)S(1)}, f32[3,64,256]{2,1,0:T(8,128)S(1)}, u32[]{:S(2)}, u32[]{:S(2)}) collective-permute-start(f32[3,64,256]{2,1,0:T(8,128)S(1)} %get-tuple-element.22), channel_id=1, source_target_pairs={{0,112},{16,0},{32,16},{48,32},{64,48},{80,64},{96,80},{112,96},{1... | collective-permute-start | bytes 589832 | tf_op jit(solution)/shard_map/ppermute | solution.py:509
  81.4 7.4 %collective-permute-start.6 = (f32[3,16,256]{2,1,0:T(8,128)S(1)}, f32[3,16,256]{2,1,0:T(8,128)S(1)}, u32[]{:S(2)}, u32[]{:S(2)}) collective-permute-start(f32[3,16,256]{2,1,0:T(8,128)S(1)} %get-tuple-element.23), channel_id=1, source_target_pairs={{0,1},{1,2},{2,3},{3,4},{4,5},{5,6},{6,7},{7,8},{8,9},{9,10},{10,1... | collective-permute-start | bytes 147464 | tf_op jit(solution)/shard_map/ppermute | solution.py:509
  82.0 6.8 %collective-permute-start.7 = (f32[3,16,256]{2,1,0:T(8,128)S(1)}, f32[3,16,256]{2,1,0:T(8,128)S(1)}, u32[]{:S(2)}, u32[]{:S(2)}) collective-permute-start(f32[3,16,256]{2,1,0:T(8,128)S(1)} %get-tuple-element.24), channel_id=1, source_target_pairs={{0,15},{1,0},{2,1},{3,2},{4,3},{5,4},{6,5},{7,6},{8,7},{9,8},{10,9... | collective-permute-start | bytes 147464 | tf_op jit(solution)/shard_map/ppermute | solution.py:509

commit v4 on v3

--- a/solution.py
+++ b/solution.py
@@ -49,6 +49,18 @@
     return jnp.dot(a, b, preferred_element_type=f32)
 
 
+def shift_rows(value, edge, by):
+    count, wide = value.shape
+    row = lax.broadcasted_iota(i32, (8, wide), 0)
+    parts = [value[k : k + 8] for k in range(0, count, 8)]
+    turned = [pltpu.roll(p, by % 8, 0) for p in parts]
+    if by > 0:
+        inner, beside = row == 0, [jnp.broadcast_to(edge, (8, wide))] + turned[:-1]
+    else:
+        inner, beside = row == 7, turned[1:] + [jnp.broadcast_to(edge, (8, wide))]
+    return jnp.concatenate([jnp.where(inner, b, a) for a, b in zip(turned, beside)], axis=0)
+
+
 def window(cell_s, t, rows):
     first = cell_s[t, 0] >> row_bits
     last = cell_s[t, tile - 1] >> row_bits
@@ -84,8 +96,26 @@
     return slot // (2 * lanes), slot % (2 * lanes)
 
 
+def border_kernel(field_hbm, xlo_ref, xhi_ref, ylo_ref, yhi_ref, low_ref, high_ref, sems):
+    nx, cy = field_hbm.shape[1], field_hbm.shape[2]
+    copies = [
+        pltpu.make_async_copy(field_hbm.at[:, :, pl.ds(0, 8)], low_ref, sems.at[0]),
+        pltpu.make_async_copy(field_hbm.at[:, :, pl.ds(cy - 8, 8)], high_ref, sems.at[1]),
+        pltpu.make_async_copy(field_hbm.at[:, 0], xlo_ref, sems.at[2]),
+        pltpu.make_async_copy(field_hbm.at[:, nx - 1], xhi_ref, sems.at[3]),
+    ]
+    for copy in copies:
+        copy.start()
+    for copy, ref, into, at in ((copies[0], low_ref, ylo_ref, 0), (copies[1], high_ref, yhi_ref, 7)):
+        copy.wait()
+        for c in range(3):
+            for x in range(nx):
+                into[c, x : x + 1] = ref[c, x, at : at + 1]
+    copies[2].wait()
+    copies[3].wait()
+
+
 def sample_kernel(
-    cell_s,
     field_hbm,
     xlo_ref,
     xhi_ref,
@@ -108,7 +138,9 @@
     offset_ref,
     upper_ref,
     total_ref,
+    cell_s,
     sems,
+    cell_sem,
 ):
     nx, cy, nz = visc_ref.shape
     tiles = cell_ref.shape[0]
@@ -124,6 +156,8 @@
             pltpu.make_async_copy(visc_hbm.at[part], visc_ref.at[part], sems.at[3, k]),
         ]
 
+    list_cells = pltpu.make_async_copy(cell_ref, cell_s, cell_sem)
+    list_cells.start()
     batches = nx // batch
     for k in range(batches):
         for copy in copies(k):
@@ -152,19 +186,22 @@
 
     lax.fori_loop(0, tiles, rank, 0, unroll=16)
 
-    y_at = lax.broadcasted_iota(i32, (strip, nz), 0)
     z_at = lax.broadcasted_iota(i32, (strip, nz), 1)
 
     def advance(x, carry):
         for y in range(0, cy, strip):
             part = pl.ds(y, strip)
             visc = time_step * visc_ref[x, part]
-            wind = [(-0.5 * time_step) * wind_ref[a, x, part] for a in range(3)]
+            wind = [(0.5 * time_step) * wind_ref[a, x, part] for a in range(3)]
+            from_up, from_right, from_over = [visc - w for w in wind]
+            from_down, from_left, from_under = [visc + w for w in wind]
+            from_over = jnp.where(z_at == nz - 1, 0.0, from_over)
+            from_under = jnp.where(z_at == 0, 0.0, from_under)
+            own = 1.0 - 6.0 * visc
             here = [field_ref[c, x + 1, part] for c in range(3)]
+            scaled = [time_step * f for f in here]
             for c in range(3):
                 f = here[c]
-                down = field_ref[c, x, part]
-                up = field_ref[c, x + 2, part]
                 if y == 0:
                     before = jnp.where(left_edge, 0.0, ylo_ref[c, pl.ds(x, 1), :])
                 else:
@@ -173,19 +210,17 @@
                     after = jnp.where(right_edge, 0.0, yhi_ref[c, pl.ds(x, 1), :])
                 else:
                     after = field_ref[c, x + 1, y + strip : y + strip + 1]
-                left = jnp.where(y_at == 0, before, pltpu.roll(f, 1, 0))
-                right = jnp.where(y_at == strip - 1, after, pltpu.roll(f, strip - 1, 0))
-                under = jnp.where(z_at == 0, 0.0, pltpu.roll(f, 1, 1))
-                over = jnp.where(z_at == nz - 1, 0.0, pltpu.roll(f, nz - 1, 1))
-                near = (up + down) + (right + left) + (over + under)
-                tangent = f + visc * (near - 6.0 * f)
-                tangent += wind[0] * (up - down) + wind[1] * (right - left) + wind[2] * (over - under)
-                gq = (
-                    grad_ref[3 * c, x, part] * here[0]
-                    + grad_ref[3 * c + 1, x, part] * here[1]
-                    + grad_ref[3 * c + 2, x, part] * here[2]
+                tangent = (
+                    (own * f + from_up * field_ref[c, x + 2, part])
+                    + (from_down * field_ref[c, x, part] + from_left * shift_rows(f, before, 1))
+                    + (from_right * shift_rows(f, after, -1) + from_under * pltpu.roll(f, 1, 1))
+                    + from_over * pltpu.roll(f, nz - 1, 1)
+                ) - (
+                    grad_ref[3 * c, x, part] * scaled[0]
+                    + grad_ref[3 * c + 1, x, part] * scaled[1]
+                    + grad_ref[3 * c + 2, x, part] * scaled[2]
                 )
-                head, rest = split(tangent - time_step * gq)
+                head, rest = split(tangent)
                 at = pl.multiple_of(x * cy + y, strip)
                 plane_ref[c, pl.ds(at, strip), :nz] = head
                 plane_ref[c, pl.ds(at, strip), nz:] = rest
@@ -198,6 +233,8 @@
         if k + 1 < batches:
             copies(k + 1)[0].wait()
         lax.fori_loop(k * batch, (k + 1) * batch, advance, 0)
+
+    list_cells.wait()
 
     def find(t, begin, least):
         cells = cell_ref[pl.ds(t, 1), :]
@@ -315,42 +352,38 @@
     lax.fori_loop(0, sources // group, give, 0, unroll=8)
 
 
-def adjoint_kernel(
-    cell_s,
+def scatter_kernel(
     back_ref,
     cell_ref,
     slot_ref,
     wind_hbm,
     grad_hbm,
     visc_hbm,
-    out_hbm,
+    plane_ref,
+    wind_ref,
+    grad_ref,
+    visc_ref,
     xlo_ref,
     xhi_ref,
     ylo_ref,
     yhi_ref,
-    wind_ref,
-    grad_ref,
-    visc_ref,
     table_ref,
     value_ref,
-    plane_ref,
-    out_ref,
+    cell_s,
     sems,
+    cell_sem,
 ):
-    nx, cy, nz = visc_ref.shape
+    nx, cy, nz = visc_hbm.shape
     tiles = cell_ref.shape[0]
     half = back_ref.shape[0]
     rows = nx * cy
-
+    list_cells = pltpu.make_async_copy(cell_ref, cell_s, cell_sem)
+    list_cells.start()
     copies = [
-        pltpu.make_async_copy(wind_hbm, wind_ref, sems.at[0, 0]),
-        pltpu.make_async_copy(grad_hbm, grad_ref, sems.at[1, 0]),
-        pltpu.make_async_copy(visc_hbm, visc_ref, sems.at[2, 0]),
+        pltpu.make_async_copy(visc_hbm, visc_ref, sems.at[0]),
+        pltpu.make_async_copy(wind_hbm, wind_ref, sems.at[1]),
+        pltpu.make_async_copy(grad_hbm, grad_ref, sems.at[2]),
     ]
-
-    def write(x):
-        return pltpu.make_async_copy(out_ref.at[:, x + 1], out_hbm.at[:, x], sems.at[3, x])
-
     for copy in copies:
         copy.start()
     for c in range(3):
@@ -371,6 +404,8 @@
         return carry
 
     lax.fori_loop(0, tiles, restore, 0, unroll=16)
+
+    list_cells.wait()
 
     def put(t, begin, least):
         cells = cell_ref[pl.ds(t, 1), :]
@@ -389,7 +424,28 @@
 
     each_tile(cell_s, tiles, rows, lambda t, base: put(t, base, 0), put)
 
-    y_at = lax.broadcasted_iota(i32, (strip, nz), 0)
+    for copy in copies:
+        copy.wait()
+    for x, ref, sign in ((0, xlo_ref, 1.0), (nx - 1, xhi_ref, -1.0)):
+        passed = time_step * visc_ref[x] + (sign * 0.5 * time_step) * wind_ref[0, x]
+        for c in range(3):
+            ref[c] = passed * plane_ref[c, x * cy : (x + 1) * cy]
+    for y, ref, sign in ((0, ylo_ref, 1.0), (cy - 1, yhi_ref, -1.0)):
+        for x in range(nx):
+            row = slice(y, y + 1)
+            passed = time_step * visc_ref[x, row] + (sign * 0.5 * time_step) * wind_ref[1, x, row]
+            for c in range(3):
+                ref[c, x : x + 1] = passed * plane_ref[c, x * cy + y : x * cy + y + 1]
+
+
+def adjoint_kernel(
+    plane_ref, wind_ref, grad_ref, visc_ref, out_hbm, low_ref, high_ref, left_ref, right_ref, out_ref, sems
+):
+    nx, cy, nz = visc_ref.shape
+
+    def write(x):
+        return pltpu.make_async_copy(out_ref.at[:, x + 1], out_hbm.at[:, x], sems.at[x])
+
     z_at = lax.broadcasted_iota(i32, (strip, nz), 1)
     strips = cy // strip
 
@@ -400,47 +456,38 @@
             pulled = [plane_ref[c, pl.ds(at, strip), :] for c in range(3)]
             visc = time_step * visc_ref[x, part]
             wind = (0.5 * time_step) * wind_ref[1, x, part]
-            mixed = [visc * p for p in pulled]
-            moved = [wind * p for p in pulled]
-            return pulled, mixed, [m + w for m, w in zip(mixed, moved)], [m - w for m, w in zip(mixed, moved)]
+            to_left, to_right = visc + wind, visc - wind
+            return pulled, visc, [to_left * p for p in pulled], [to_right * p for p in pulled]
 
         later = give(0)
-        before = [0.0] * 3
+        before = [jnp.zeros((1, nz), f32)] * 3
         for k in range(strips):
-            pulled, mixed, to_left, to_right = later
+            pulled, visc, to_left, to_right = later
             part = pl.ds(k * strip, strip)
-            after = [0.0] * 3
+            after = [jnp.zeros((1, nz), f32)] * 3
             if k + 1 < strips:
                 later = give(k + 1)
                 after = [v[0:1] for v in later[2]]
             wind_x = (0.5 * time_step) * wind_ref[0, x, part]
             wind_z = (0.5 * time_step) * wind_ref[2, x, part]
+            to_down, to_up = visc + wind_x, visc - wind_x
+            to_under = jnp.where(z_at == 0, 0.0, visc + wind_z)
+            to_over = jnp.where(z_at == nz - 1, 0.0, visc - wind_z)
+            own = 1.0 - 6.0 * visc
+            scaled = [time_step * p for p in pulled]
             for c in range(3):
                 p = pulled[c]
-                sx = wind_x * p
-                sz = wind_z * p
+                around = (shift_rows(to_left[c], after[c], -1) + shift_rows(to_right[c], before[c], 1)) + (
+                    pltpu.roll(to_under * p, nz - 1, 1) + pltpu.roll(to_over * p, 1, 1)
+                )
                 gtr = (
-                    grad_ref[c, x, part] * pulled[0]
-                    + grad_ref[3 + c, x, part] * pulled[1]
-                    + grad_ref[6 + c, x, part] * pulled[2]
+                    grad_ref[c, x, part] * scaled[0]
+                    + grad_ref[3 + c, x, part] * scaled[1]
+                    + grad_ref[6 + c, x, part] * scaled[2]
                 )
-                around = (
-                    jnp.where(y_at == strip - 1, after[c], pltpu.roll(to_left[c], strip - 1, 0))
-                    + jnp.where(y_at == 0, before[c], pltpu.roll(to_right[c], 1, 0))
-                ) + (
-                    jnp.where(z_at == nz - 1, 0.0, pltpu.roll(mixed[c] + sz, nz - 1, 1))
-                    + jnp.where(z_at == 0, 0.0, pltpu.roll(mixed[c] - sz, 1, 1))
-                )
-                own = (p - 6.0 * mixed[c]) + (around - time_step * gtr)
-                out_ref[c, x, part] += mixed[c] + sx
-                out_ref[c, x + 1, part] += own
-                out_ref[c, x + 2, part] = mixed[c] - sx
-            if k == 0:
-                for c in range(3):
-                    ylo_ref[c, pl.ds(x, 1), :] = to_left[c][0:1]
-            if k + 1 == strips:
-                for c in range(3):
-                    yhi_ref[c, pl.ds(x, 1), :] = to_right[c][strip - 1 : strip]
+                out_ref[c, x, part] += to_down * p
+                out_ref[c, x + 1, part] += own * p + (around - gtr)
+                out_ref[c, x + 2, part] = to_up * p
             before = [v[strip - 1 : strip] for v in to_right]
 
         @pl.when(x > 0)
@@ -449,12 +496,12 @@
 
         return carry
 
-    for copy in copies:
-        copy.wait()
     out_ref[:, 0:2] = jnp.zeros((3, 2, cy, nz), f32)
     lax.fori_loop(0, nx, advance, 0)
-    xlo_ref[...] = out_ref[:, 0]
-    xhi_ref[...] = out_ref[:, nx + 1]
+    low_ref[...] = out_ref[:, 1]
+    high_ref[...] = out_ref[:, nx]
+    left_ref[...] = out_ref[:, 2:nx, 0:8]
+    right_ref[...] = out_ref[:, 2:nx, cy - 8 : cy]
     write(nx - 1).start()
 
     def end(x, carry):
@@ -465,41 +512,40 @@
 
 
 def edge_kernel(
-    given_ref, xlo_ref, xhi_ref, ylo_ref, yhi_ref, out_ref, low_ref, high_ref, left_ref, right_ref, sems
+    given_ref, low_ref, high_ref, left_ref, right_ref, xlo_ref, xhi_ref, ylo_ref, yhi_ref, out_ref, *scratch
 ):
     del given_ref
+    *held_refs, sems = scratch
     along, across = lax.axis_index("track"), lax.axis_index("cross")
     last_along, last_across = lax.axis_size("track") - 1, lax.axis_size("cross") - 1
-    ylo = jnp.where(across == 0, 0.0, ylo_ref[...])
-    yhi = jnp.where(across == last_across, 0.0, yhi_ref[...])
     nx, cy = out_ref.shape[1], out_ref.shape[2]
     inner = nx - 2
+    left_edge, right_edge = across == 0, across == last_across
     places = [
-        (out_ref.at[:, 0], low_ref),
-        (out_ref.at[:, nx - 1], high_ref),
-        (out_ref.at[:, pl.ds(1, inner), pl.ds(0, 8)], left_ref),
-        (out_ref.at[:, pl.ds(1, inner), pl.ds(cy - 8, 8)], right_ref),
+        out_ref.at[:, 0],
+        out_ref.at[:, nx - 1],
+        out_ref.at[:, pl.ds(1, inner), pl.ds(0, 8)],
+        out_ref.at[:, pl.ds(1, inner), pl.ds(cy - 8, 8)],
     ]
-    reads = [pltpu.make_async_copy(a, b, sems.at[i]) for i, (a, b) in enumerate(places)]
-    for read in reads:
-        read.start()
-    writes = [pltpu.make_async_copy(b, a, sems.at[4 + i]) for i, (a, b) in enumerate(places)]
-    for i, (x, ref, halo, edge) in enumerate(
-        ((0, low_ref, xlo_ref, along == 0), (nx - 1, high_ref, xhi_ref, along == last_along))
-    ):
-        reads[i].wait()
-        ref[...] += jnp.where(edge, 0.0, halo[...])
-        ref[:, 0:1, :] += ylo[:, x : x + 1, :]
-        ref[:, cy - 1 : cy, :] += yhi[:, x : x + 1, :]
+    writes = [pltpu.make_async_copy(a, b, sems.at[i]) for i, (a, b) in enumerate(zip(held_refs, places))]
+    sides = (
+        (0, held_refs[0], low_ref, xlo_ref, along == 0),
+        (nx - 1, held_refs[1], high_ref, xhi_ref, along == last_along),
+    )
+    for i, (x, ref, own, halo, edge) in enumerate(sides):
+        for c in range(3):
+            ref[c] = own[c] + jnp.where(edge, 0.0, halo[c])
+            ref[c, 0:1] += jnp.where(left_edge, 0.0, ylo_ref[c, x : x + 1])
+            ref[c, cy - 1 : cy] += jnp.where(right_edge, 0.0, yhi_ref[c, x : x + 1])
         writes[i].start()
-    reads[2].wait()
-    for k in range(inner):
-        left_ref[:, k, 0:1, :] += ylo[:, k + 1 : k + 2, :]
-    writes[2].start()
-    reads[3].wait()
-    for k in range(inner):
-        right_ref[:, k, 7:8, :] += yhi[:, k + 1 : k + 2, :]
-    writes[3].start()
+    row_at = lax.broadcasted_iota(i32, (8, out_ref.shape[3]), 0)
+    for i, row, own, halo, edge in ((2, 0, left_ref, ylo_ref, left_edge), (3, 7, right_ref, yhi_ref, right_edge)):
+        ref = held_refs[i]
+        here = (row_at == row) & jnp.logical_not(edge)
+        for c in range(3):
+            for k in range(inner):
+                ref[c, k] = own[c, k] + jnp.where(here, halo[c, k + 1 : k + 2], 0.0)
+        writes[i].start()
     for write in writes:
         write.wait()
 
@@ -520,6 +566,28 @@
 
 def room(mib):
     return pltpu.CompilerParams(vmem_limit_bytes=mib << 20)
+
+
+def call_border(field):
+    _, cx, cy, nz = field.shape
+    return pl.pallas_call(
+        border_kernel,
+        name="border",
+        in_specs=[hbm],
+        out_specs=[vmem] * 4,
+        scratch_shapes=[
+            pltpu.VMEM((3, cx, 8, nz), f32),
+            pltpu.VMEM((3, cx, 8, nz), f32),
+            pltpu.SemaphoreType.DMA((4,)),
+        ],
+        out_shape=[
+            jax.ShapeDtypeStruct((3, cy, nz), f32),
+            jax.ShapeDtypeStruct((3, cy, nz), f32),
+            jax.ShapeDtypeStruct((3, cx, nz), f32),
+            jax.ShapeDtypeStruct((3, cx, nz), f32),
+        ],
+        compiler_params=room(8),
+    )(held(field))
 
 
 def call_sample(direction, halo, wind, wind_gradient, viscosity, cells, owner, gate, owners):
@@ -528,7 +596,7 @@
     return pl.pallas_call(
         sample_kernel,
         name="sample",
-        in_specs=[smem, hbm, vmem, vmem, vmem, vmem, hbm, hbm, hbm, vmem, vmem, vmem],
+        in_specs=[hbm, vmem, vmem, vmem, vmem, hbm, hbm, hbm, vmem, vmem, vmem],
         out_specs=[vmem, vmem],
         scratch_shapes=[
             pltpu.VMEM((3, cx + 2, cy, nz), f32),
@@ -540,14 +608,16 @@
             pltpu.VMEM((owners, lanes), f32),
             pltpu.VMEM((tile, tile), bf16),
             pltpu.VMEM((2 * owners, 2 * lanes), f32),
+            pltpu.SMEM((tiles, tile), i32),
             pltpu.SemaphoreType.DMA((4, cx)),
+            pltpu.SemaphoreType.DMA,
         ],
         out_shape=[
             jax.ShapeDtypeStruct((owners // 2, 2, 4, lanes), f32),
             jax.ShapeDtypeStruct((tiles, tile), i32),
         ],
         compiler_params=room(40),
-    )(cells, held(direction), *halo, held(wind), held(wind_gradient), held(viscosity), cells, owner, gate)
+    )(held(direction), *halo, held(wind), held(wind_gradient), held(viscosity), cells, owner, gate)
 
 
 def call_owner(gate_counts, got, sight, precision):
@@ -566,54 +636,67 @@
     )(gate_counts, got, sight, precision)
 
 
-def call_adjoint(returned, cells, slot, wind, wind_gradient, viscosity):
+def call_scatter(returned, cells, slot, wind, wind_gradient, viscosity):
     _, cx, cy, nz = wind.shape
     tiles = cells.shape[0]
     half = returned.shape[0]
     return pl.pallas_call(
-        adjoint_kernel,
-        name="adjoint",
-        in_specs=[smem, vmem, vmem, vmem, hbm, hbm, hbm],
-        out_specs=[hbm, vmem, vmem, vmem, vmem],
+        scatter_kernel,
+        name="scatter",
+        in_specs=[vmem, vmem, vmem, hbm, hbm, hbm],
+        out_specs=[vmem] * 8,
         scratch_shapes=[
-            pltpu.VMEM((3, cx, cy, nz), f32),
-            pltpu.VMEM((9, cx, cy, nz), f32),
-            pltpu.VMEM((cx, cy, nz), f32),
             pltpu.VMEM((6 * half, 2 * lanes), bf16),
             pltpu.VMEM((3, tiles, tile), f32),
-            pltpu.VMEM((3, cx * cy, nz), f32),
-            pltpu.VMEM((3, cx + 2, cy, nz), f32),
-            pltpu.SemaphoreType.DMA((4, cx)),
+            pltpu.SMEM((tiles, tile), i32),
+            pltpu.SemaphoreType.DMA((3,)),
+            pltpu.SemaphoreType.DMA,
         ],
         out_shape=[
-            jax.ShapeDtypeStruct((3, cx, cy, nz), f32),
+            jax.ShapeDtypeStruct((3, cx * cy, nz), f32),
+            jax.ShapeDtypeStruct(wind.shape, f32),
+            jax.ShapeDtypeStruct(wind_gradient.shape, f32),
+            jax.ShapeDtypeStruct(viscosity.shape, f32),
             jax.ShapeDtypeStruct((3, cy, nz), f32),
             jax.ShapeDtypeStruct((3, cy, nz), f32),
             jax.ShapeDtypeStruct((3, cx, nz), f32),
             jax.ShapeDtypeStruct((3, cx, nz), f32),
         ],
-        compiler_params=room(40),
-    )(cells, returned, cells, slot, held(wind), held(wind_gradient), held(viscosity))
-
-
-def call_edges(result, halo):
+        compiler_params=room(24),
+    )(returned, cells, slot, held(wind), held(wind_gradient), held(viscosity))
+
+
+def border_shapes(cx, cy, nz):
+    return [(3, cy, nz), (3, cy, nz), (3, cx - 2, 8, nz), (3, cx - 2, 8, nz)]
+
+
+def call_adjoint(pulled, wind, wind_gradient, viscosity):
+    _, cx, cy, nz = wind.shape
+    shapes = [(3, cx, cy, nz)] + border_shapes(cx, cy, nz)
+    return pl.pallas_call(
+        adjoint_kernel,
+        name="adjoint",
+        in_specs=[vmem] * 4,
+        out_specs=[hbm] + [vmem] * 4,
+        scratch_shapes=[pltpu.VMEM((3, cx + 2, cy, nz), f32), pltpu.SemaphoreType.DMA((cx,))],
+        out_shape=[jax.ShapeDtypeStruct(shape, f32) for shape in shapes],
+        compiler_params=room(24),
+    )(pulled, wind, wind_gradient, viscosity)
+
+
+def call_edges(result, sides, halo):
     _, cx, cy, nz = result.shape
     return pl.pallas_call(
         edge_kernel,
         name="edges",
-        in_specs=[hbm, vmem, vmem, vmem, vmem],
+        in_specs=[hbm] + [vmem] * 8,
         out_specs=hbm,
-        scratch_shapes=[
-            pltpu.VMEM((3, cy, nz), f32),
-            pltpu.VMEM((3, cy, nz), f32),
-            pltpu.VMEM((3, cx - 2, 8, nz), f32),
-            pltpu.VMEM((3, cx - 2, 8, nz), f32),
-            pltpu.SemaphoreType.DMA((8,)),
-        ],
+        scratch_shapes=[pltpu.VMEM(shape, f32) for shape in border_shapes(cx, cy, nz)]
+        + [pltpu.SemaphoreType.DMA((4,))],
         out_shape=jax.ShapeDtypeStruct(result.shape, f32),
         input_output_aliases={0: 0},
-        compiler_params=room(24),
-    )(result, *halo)
+        compiler_params=room(16),
+    )(result, *sides, *halo)
 
 
 def body(
@@ -628,14 +711,14 @@
     gate_counts,
     precision,
 ):
-    _, cx, cy, nz = direction.shape
     owners = lax.axis_size("track") * lax.axis_size("cross")
     names = ("track", "cross")
+    xlo, xhi, ylo, yhi = call_border(direction)
     halo = (
-        shifted(direction[:, cx - 1], "track", 1),
-        shifted(direction[:, 0], "track", -1),
-        shifted(direction[:, :, cy - 1], "cross", 1),
-        shifted(direction[:, :, 0], "cross", -1),
+        shifted(xhi, "track", 1),
+        shifted(xlo, "track", -1),
+        shifted(yhi, "cross", 1),
+        shifted(ylo, "cross", -1),
     )
     cells, owner, gate = [
         v.reshape(-1, tile)
@@ -648,16 +731,15 @@
     back, weighted = call_owner(gate_counts, got, sight, precision)
     returned = lax.all_to_all(back, names, split_axis=0, concat_axis=0, tiled=True)
     returned = returned.reshape(owners // 2, 2, 4, lanes)
-    result, xlo, xhi, ylo, yhi = call_adjoint(returned, cells, slot, wind, wind_gradient, viscosity)
-    result = call_edges(
-        result,
-        (
-            shifted(xhi, "track", 1),
-            shifted(xlo, "track", -1),
-            shifted(yhi, "cross", 1),
-            shifted(ylo, "cross", -1),
-        ),
+    *taken, xlo, xhi, ylo, yhi = call_scatter(returned, cells, slot, wind, wind_gradient, viscosity)
+    halo = (
+        shifted(xhi, "track", 1),
+        shifted(xlo, "track", -1),
+        shifted(yhi, "cross", 1),
+        shifted(ylo, "cross", -1),
     )
+    result, *sides = call_adjoint(*taken)
+    result = call_edges(result, sides, halo)
     return (result, weighted)
 
 

time: 91.4 us -> 83.8 us (0.917)
  Pallas kernels: 29.9 us -> 27.6 us
  local copies, waits for them, and re-layouts: 2.3 us -> 0.06 us
  waiting for transfers between devices: 2.08 us -> 0.02 us
    pallas_call x3 -> x5, Pallas kernels: 26.4 us -> 24 us  [the longest x1 11.7 us: call_sample(): pl.pallas_call(sample_kernel, name='sample', in_specs=[hbm, vmem, vmem, v...]
    ppermute x8, waiting for transfers between devices: 2.08 us -> 0.02 us  [shifted(): lax.ppermute(value, axis, [(i, (i + by) % count) for i in range(count)])]
    slice x1 -> x0, local copies, waits for them, and re-layouts: 1.19 us -> none  [body(): direction[:, :, 0]]
    squeeze x1 -> x0, local copies, waits for them, and re-layouts: 1.05 us -> none  [body(): direction[:, 0]]
  transfers between devices with their start and end apart: 8 -> 8, of which waited for: 1 -> 0; matrix products, arithmetic and copies ran while one was open for 9% -> 7% of each run, Pallas kernels for 0% -> 6%
where the time goes in v4:
time: 83.8 us; the launch traced here: 83.6 us
  blocking collectives  32 us (38%)
  Pallas kernels  27.6 us (33%)
  starting transfers between devices  17.2 us (21%)
  other arithmetic  5.73 us (7%)
  between operations  1 us (1%)
    ppermute x8, starting transfers between devices, shifted(): lax.ppermute(value, axis, [(i, (i + by) % count) for i in range(count)])  17.2 us
    all_to_all x1, blocking collectives, body(): lax.all_to_all(slots.reshape(owners, 4, lanes), names, split_axis=0, conc...  16.7 us
    all_to_all x1, blocking collectives, body(): lax.all_to_all(back, names, split_axis=0, concat_axis=0, tiled=True)  15.3 us
    pallas_call x1, Pallas kernels, call_sample(): pl.pallas_call(sample_kernel, name='sample', in_specs=[hbm, vmem, vmem, v...  11.7 us
    sort x1, other arithmetic, body(): lax.sort((sample_cell.reshape(-1), sample_owner.reshape(-1), sample_gate....  5.73 us
    pallas_call x1, Pallas kernels, call_scatter(): pl.pallas_call(scatter_kernel, name='scatter', in_specs=[vmem, vmem, vmem...  5.21 us
    pallas_call x1, Pallas kernels, call_adjoint(): pl.pallas_call(adjoint_kernel, name='adjoint', in_specs=[vmem] * 4, out_s...  4.79 us
    pallas_call x1, Pallas kernels, call_owner(): pl.pallas_call(owner_kernel, name='owner', in_specs=[smem, vmem, vmem, vm...  3.56 us
  transfers between devices with their start and end apart: 8, of which 0 were waited for; matrix products, arithmetic and copies ran while one was open for 7% of the time, Pallas kernels for 6%

profile of v4, /device:TPU:0, one launch (start us, length us, event | category | flops | bytes accessed | tf_op | source)
XLA Modules:
  0.0 83.6 jit_solution(4652928391876689804)
XLA Ops:
  0.6 0.0 copy-start.5
  0.6 0.0 copy-start.3
  0.7 0.0 copy-start.4
  0.7 1.3 %border.1 = (f32[3,64,256]{2,1,0:T(8,128)S(1)}, f32[3,64,256]{2,1,0:T(8,128)S(1)}, f32[3,16,256]{2,1,0:T(8,128)S(1)}, f32[3,16,256]{2,1,0:T(8,128)S(1)}) custom-call(f32[3,16,64,256]{3,2,1,0:T(8,128)} %field_hbm.3), custom_call_target="tpu_custom_call" | custom-call | tf_op jit(solution)/shard_map/border/pallas_call | solution.py:573
  1.9 0.0 collective-permute-start
  2.0 3.6 %collective-permute-start.1 = (f32[3,64,256]{2,1,0:T(8,128)S(1)}, f32[3,64,256]{2,1,0:T(8,128)S(1)}, u32[]{:S(2)}, u32[]{:S(2)}) collective-permute-start(f32[3,64,256]{2,1,0:T(8,128)S(1)} %get-tuple-element.27), channel_id=1, source_target_pairs={{0,112},{16,0},{32,16},{48,32},{64,48},{80,64},{96,80},{112,96},{1... | collective-permute-start | bytes 589832 | tf_op jit(solution)/shard_map/ppermute | solution.py:555
  5.5 1.5 %collective-permute-start.2 = (f32[3,16,256]{2,1,0:T(8,128)S(1)}, f32[3,16,256]{2,1,0:T(8,128)S(1)}, u32[]{:S(2)}, u32[]{:S(2)}) collective-permute-start(f32[3,16,256]{2,1,0:T(8,128)S(1)} %get-tuple-element.28), channel_id=1, source_target_pairs={{0,1},{1,2},{2,3},{3,4},{4,5},{5,6},{6,7},{7,8},{8,9},{9,10},{10,1... | collective-permute-start | bytes 147464 | tf_op jit(solution)/shard_map/ppermute | solution.py:555
  7.0 3.9 %collective-permute-start.3 = (f32[3,16,256]{2,1,0:T(8,128)S(1)}, f32[3,16,256]{2,1,0:T(8,128)S(1)}, u32[]{:S(2)}, u32[]{:S(2)}) collective-permute-start(f32[3,16,256]{2,1,0:T(8,128)S(1)} %get-tuple-element.29), channel_id=1, source_target_pairs={{0,15},{1,0},{2,1},{3,2},{4,3},{5,4},{6,5},{7,6},{8,7},{9,8},{10,9... | collective-permute-start | bytes 147464 | tf_op jit(solution)/shard_map/ppermute | solution.py:555
  10.9 0.0 copy-done.5
  10.9 0.0 copy-done.3
  10.9 0.0 copy-done.4
  10.9 5.7 %sort.21 = (s32[8192]{0:T(1024)S(1)}, s32[8192]{0:T(1024)S(1)}, s32[8192]{0:T(1024)S(1)}) sort(s32[8192]{0:T(1024)S(1)} %bitcast.7, s32[8192]{0:T(1024)S(1)} %bitcast.8, s32[8192]{0:T(1024)S(1)} %bitcast.9), dimensions={0}, to_apply=%region_0.0 | sort | flops 106496 | bytes 196608 | tf_op jit(solution)/shard_map/sort | solution.py:725
  16.7 0.0 copy-start
  16.7 0.0 copy-start.1
  16.7 0.0 copy-start.2
  16.7 0.0 collective-permute-done.2.ylo_ref
  16.7 0.0 collective-permute-done.3.yhi_ref
  16.8 0.0 collective-permute-done.xlo_ref
  16.8 0.0 collective-permute-done.1.xhi_ref
  16.8 11.7 %sample.1 = (f32[64,2,4,128]{3,2,1,0:T(4,128)S(1)}, s32[32,256]{1,0:T(8,128)S(1)}) custom-call(f32[3,16,64,256]{3,2,1,0:T(8,128)} %field_hbm.3, f32[3,64,256]{2,1,0:T(8,128)S(1)} %collective-permute-done.xlo_ref, f32[3,64,256]{2,1,0:T(8,128)S(1)} %collective-permute-done.1.xhi_ref, f32[3,16,256]{2,1,0:T(8,128)S(1)} %collective-permute-done.2.ylo_ref, ...), custom_call_target="tpu_custom_call" | custom-call | tf_op jit(solution)/shard_map/sample/pallas_call | solution.py:596
  28.5 16.7 %all_to_all.10.got_ref = f32[128,4,128]{2,1,0:T(4,128)S(1)} all-to-all(f32[128,4,128]{2,1,0:T(4,128)S(1)} %bitcast.6), channel_id=1, replica_groups=mesh['track'=8,'cross'=16] {'track','cross'}, dimensions={0} | all-to-all | bytes 524288 | tf_op jit(solution)/shard_map/all_to_all | solution.py:730
  45.1 0.0 copy-done
  45.1 0.0 copy-done.1
  45.1 0.0 copy-done.2
  45.1 3.6 %owner.1 = (f32[128,4,128]{2,1,0:T(4,128)S(1)}, f32[1,1024]{1,0:T(1,128)}) custom-call(s32[1,8]{1,0:T(1,128)S(1)} %copy-done.2, f32[128,4,128]{2,1,0:T(4,128)S(1)} %all_to_all.10.got_ref, f32[3,1,1024]{2,1,0:T(1,128)S(1)} %copy-done.1, f32[1,128,128]{2,1,0:T(8,128)S(1)} %copy-done), custom_call_target="tpu_custom_call" | custom-call | tf_op jit(solution)/shard_map/owner/pallas_call | solution.py:625
  48.7 15.3 %all_to_all.11 = f32[128,4,128]{2,1,0:T(4,128)S(1)} all-to-all(f32[128,4,128]{2,1,0:T(4,128)S(1)} %get-tuple-element.34), channel_id=1, replica_groups=mesh['track'=8,'cross'=16] {'track','cross'}, dimensions={0} | all-to-all | bytes 524288 | tf_op jit(solution)/shard_map/all_to_all | solution.py:732
  64.0 5.2 %scatter.1 = (f32[3,1024,256]{2,1,0:T(8,128)S(1)}, f32[3,16,64,256]{3,2,1,0:T(8,128)S(1)}, f32[9,16,64,256]{3,2,1,0:T(8,128)S(1)}, f32[16,64,256]{2,1,0:T(8,128)...) custom-call(f32[64,2,4,128]{3,2,1,0:T(4,128)S(1)} %bitcast.5, ...), custom_call_target="tpu_custom_call" | custom-call | tf_op jit(solution)/shard_map/scatter/pallas_call | solution.py:643
  69.2 0.0 collective-permute-start.4
  69.2 2.9 %collective-permute-start.5 = (f32[3,64,256]{2,1,0:T(8,128)S(1)}, f32[3,64,256]{2,1,0:T(8,128)S(1)}, u32[]{:S(2)}, u32[]{:S(2)}) collective-permute-start(f32[3,64,256]{2,1,0:T(8,128)S(1)} %get-tuple-element.46), channel_id=1, source_target_pairs={{0,112},{16,0},{32,16},{48,32},{64,48},{80,64},{96,80},{112,96},{1... | collective-permute-start | bytes 589832 | tf_op jit(solution)/shard_map/ppermute | solution.py:555
  72.2 0.6 collective-permute-start.6
  72.8 4.7 %collective-permute-start.7 = (f32[3,16,256]{2,1,0:T(8,128)S(1)}, f32[3,16,256]{2,1,0:T(8,128)S(1)}, u32[]{:S(2)}, u32[]{:S(2)}) collective-permute-start(f32[3,16,256]{2,1,0:T(8,128)S(1)} %get-tuple-element.48), channel_id=1, source_target_pairs={{0,15},{1,0},{2,1},{3,2},{4,3},{5,4},{6,5},{7,6},{8,7},{9,8},{10,9... | collective-permute-start | bytes 147464 | tf_op jit(solution)/shard_map/ppermute | solution.py:555
  77.5 4.8 %adjoint.1 = (f32[3,16,64,256]{3,2,1,0:T(8,128)}, f32[3,64,256]{2,1,0:T(8,128)S(1)}, f32[3,64,256]{2,1,0:T(8,128)S(1)}, f32[3,14,8,256]{3,2,1,0:T(8,128)S(1)}, f32[3,14,8,256]{3,2,1,0:T(8,128)S(1)}) custom-call(f32[3,1024,256]{2,1,0:T(8,128)S(1)} %get-tuple-element.36.plane_ref, f32[3,16,64,256]{3,2,1,0:T(8,128)S(1)} %get-tuple-element.37.wind_ref, ...), custom_call_target="tpu_custom_call" | custom-call | tf_op jit(solution)/shard_map/adjoint/pallas_call | solution.py:676
  82.3 0.0 collective-permute-done.6.ylo_ref
  82.3 0.0 collective-permute-done.7.yhi_ref
  82.3 0.0 collective-permute-done.4.xlo_ref
  82.4 0.0 collective-permute-done.5.xhi_ref
  82.4 1.1 %edges.1 = f32[3,16,64,256]{3,2,1,0:T(8,128)} custom-call(f32[3,16,64,256]{3,2,1,0:T(8,128)} %get-tuple-element.40.given_ref, f32[3,64,256]{2,1,0:T(8,128)S(1)} %get-tuple-element.41.low_ref, f32[3,64,256]{2,1,0:T(8,128)S(1)} %get-tuple-element.42.high_ref, f32[3,14,8,256]{3,2,1,0:T(8,128)S(1)} %get-tuple-element.43.left_ref, ...), custom_call_target="tpu_custom_call", output_to_operand_aliasing={{}: (0, {})} | custom-call | tf_op jit(solution)/shard_map/edges/pallas_call | solution.py:689
  (3 shorter events, 0.0 us)
Async XLA Ops:
  0.6 10.3 %copy-start.5 = (s32[1,1,8192]{2,1,0:T(1,128)S(1)}, s32[1,1,8192]{2,1,0:T(1,128)}, u32[]{:S(2)}) copy-start(s32[1,1,8192]{2,1,0:T(1,128)} %param.16) | copy-start | bytes 98308
  0.6 10.3 %copy-start.3 = (s32[1,1,8192]{2,1,0:T(1,128)S(1)}, s32[1,1,8192]{2,1,0:T(1,128)}, u32[]{:S(2)}) copy-start(s32[1,1,8192]{2,1,0:T(1,128)} %param.15) | copy-start | bytes 98308
  0.7 10.3 %copy-start.4 = (s32[1,1,8192,1]{2,3,1,0:T(1,128)S(1)}, s32[1,1,8192,1]{2,3,1,0:T(1,128)}, u32[]{:S(2)}) copy-start(s32[1,1,8192,1]{2,3,1,0:T(1,128)} %param.14) | copy-start | bytes 98308
  1.9 14.8 %collective-permute-start = (f32[3,64,256]{2,1,0:T(8,128)S(1)}, f32[3,64,256]{2,1,0:T(8,128)S(1)}, u32[]{:S(2)}, u32[]{:S(2)}) collective-permute-start(f32[3,64,256]{2,1,0:T(8,128)S(1)} %get-tuple-element.26), channel_id=1, source_target_pairs={{0,16},{16,32},{32,48},{48,64},{64,80},{80,96},{96,112},{112,0},{1... | collective-permute-start | bytes 589832 | tf_op jit(solution)/shard_map/ppermute | solution.py:555
  2.0 14.8 %collective-permute-start.1 = (f32[3,64,256]{2,1,0:T(8,128)S(1)}, f32[3,64,256]{2,1,0:T(8,128)S(1)}, u32[]{:S(2)}, u32[]{:S(2)}) collective-permute-start(f32[3,64,256]{2,1,0:T(8,128)S(1)} %get-tuple-element.27), channel_id=1, source_target_pairs={{0,112},{16,0},{32,16},{48,32},{64,48},{80,64},{96,80},{112,96},{1... | collective-permute-start | bytes 589832 | tf_op jit(solution)/shard_map/ppermute | solution.py:555
  5.5 11.2 %collective-permute-start.2 = (f32[3,16,256]{2,1,0:T(8,128)S(1)}, f32[3,16,256]{2,1,0:T(8,128)S(1)}, u32[]{:S(2)}, u32[]{:S(2)}) collective-permute-start(f32[3,16,256]{2,1,0:T(8,128)S(1)} %get-tuple-element.28), channel_id=1, source_target_pairs={{0,1},{1,2},{2,3},{3,4},{4,5},{5,6},{6,7},{7,8},{8,9},{9,10},{10,1... | collective-permute-start | bytes 147464 | tf_op jit(solution)/shard_map/ppermute | solution.py:555
  7.0 9.7 %collective-permute-start.3 = (f32[3,16,256]{2,1,0:T(8,128)S(1)}, f32[3,16,256]{2,1,0:T(8,128)S(1)}, u32[]{:S(2)}, u32[]{:S(2)}) collective-permute-start(f32[3,16,256]{2,1,0:T(8,128)S(1)} %get-tuple-element.29), channel_id=1, source_target_pairs={{0,15},{1,0},{2,1},{3,2},{4,3},{5,4},{6,5},{7,6},{8,7},{9,8},{10,9... | collective-permute-start | bytes 147464 | tf_op jit(solution)/shard_map/ppermute | solution.py:555
  16.7 28.4 %copy-start = (f32[1,128,128]{2,1,0:T(8,128)S(1)}, f32[1,128,128]{2,1,0:T(8,128)}, u32[]{:S(2)}) copy-start(f32[1,128,128]{2,1,0:T(8,128)} %precision_ref.1) | copy-start | bytes 196612
  16.7 28.4 %copy-start.1 = (f32[3,1,1024]{2,1,0:T(1,128)S(1)}, f32[3,1,1024]{2,1,0:T(1,128)}, u32[]{:S(2)}) copy-start(f32[3,1,1024]{2,1,0:T(1,128)} %sight_ref.1) | copy-start | bytes 36868
  16.7 28.4 %copy-start.2 = (s32[1,8]{1,0:T(1,128)S(1)}, s32[1,8]{1,0:T(1,128)}, u32[]{:S(2)}) copy-start(s32[1,8]{1,0:T(1,128)} %counts_s.1) | copy-start | bytes 100
  69.2 13.1 %collective-permute-start.4 = (f32[3,64,256]{2,1,0:T(8,128)S(1)}, f32[3,64,256]{2,1,0:T(8,128)S(1)}, u32[]{:S(2)}, u32[]{:S(2)}) collective-permute-start(f32[3,64,256]{2,1,0:T(8,128)S(1)} %get-tuple-element.45), channel_id=1, source_target_pairs={{0,16},{16,32},{32,48},{48,64},{64,80},{80,96},{96,112},{112,0},{1... | collective-permute-start | bytes 589832 | tf_op jit(solution)/shard_map/ppermute | solution.py:555
  69.2 13.1 %collective-permute-start.5 = (f32[3,64,256]{2,1,0:T(8,128)S(1)}, f32[3,64,256]{2,1,0:T(8,128)S(1)}, u32[]{:S(2)}, u32[]{:S(2)}) collective-permute-start(f32[3,64,256]{2,1,0:T(8,128)S(1)} %get-tuple-element.46), channel_id=1, source_target_pairs={{0,112},{16,0},{32,16},{48,32},{64,48},{80,64},{96,80},{112,96},{1... | collective-permute-start | bytes 589832 | tf_op jit(solution)/shard_map/ppermute | solution.py:555
  72.2 10.1 %collective-permute-start.6 = (f32[3,16,256]{2,1,0:T(8,128)S(1)}, f32[3,16,256]{2,1,0:T(8,128)S(1)}, u32[]{:S(2)}, u32[]{:S(2)}) collective-permute-start(f32[3,16,256]{2,1,0:T(8,128)S(1)} %get-tuple-element.47), channel_id=1, source_target_pairs={{0,1},{1,2},{2,3},{3,4},{4,5},{5,6},{6,7},{7,8},{8,9},{9,10},{10,1... | collective-permute-start | bytes 147464 | tf_op jit(solution)/shard_map/ppermute | solution.py:555
  72.8 9.6 %collective-permute-start.7 = (f32[3,16,256]{2,1,0:T(8,128)S(1)}, f32[3,16,256]{2,1,0:T(8,128)S(1)}, u32[]{:S(2)}, u32[]{:S(2)}) collective-permute-start(f32[3,16,256]{2,1,0:T(8,128)S(1)} %get-tuple-element.48), channel_id=1, source_target_pairs={{0,15},{1,0},{2,1},{3,2},{4,3},{5,4},{6,5},{7,6},{8,7},{9,8},{10,9... | collective-permute-start | bytes 147464 | tf_op jit(solution)/shard_map/ppermute | solution.py:555

commit v5 on v4

--- a/solution.py
+++ b/solution.py
@@ -74,7 +74,7 @@
         visit(t, base)
         return jnp.maximum(most, over)
 
-    most = lax.fori_loop(0, tiles, first, i32(0), unroll=16)
+    most = lax.fori_loop(0, tiles, first, i32(0), unroll=32)
 
     @pl.when(most > 0)
     def _():
@@ -92,8 +92,12 @@
         lax.fori_loop(0, tiles, rest, 0)
 
 
+def divided(value, count):
+    return value >> (count.bit_length() - 1), value & (count - 1)
+
+
 def slot_parts(slot):
-    return slot // (2 * lanes), slot % (2 * lanes)
+    return divided(slot, 2 * lanes)
 
 
 def border_kernel(field_hbm, xlo_ref, xhi_ref, ylo_ref, yhi_ref, low_ref, high_ref, sems):
@@ -184,7 +188,7 @@
         offset_ref[...] = offset + jnp.broadcast_to(counts[:, tile - 1 : tile], offset.shape)
         return carry
 
-    lax.fori_loop(0, tiles, rank, 0, unroll=16)
+    lax.fori_loop(0, tiles, rank, 0, unroll=32)
 
     z_at = lax.broadcasted_iota(i32, (strip, nz), 1)
 
@@ -238,8 +242,8 @@
 
     def find(t, begin, least):
         cells = cell_ref[pl.ds(t, 1), :]
-        zs = onehot(nz, cells % nz)
-        line = cells // nz
+        line, depth = divided(cells, nz)
+        zs = onehot(nz, depth)
         mask = rows_equal(span, jnp.where(line >= least, line - begin, -1))
         block = jnp.concatenate(
             [plane_ref[c, pl.ds(begin, span), h * nz : (h + 1) * nz] for h in range(2) for c in range(3)], axis=0
@@ -266,7 +270,7 @@
         gate = gate_ref[pl.ds(t, 1), :]
         mask = rows_equal(half, line)
         columns = onehot(2 * lanes, column)
-        low = gate % lanes
+        _, low = divided(gate, lanes)
         parts = []
         for c in range(3):
             head, rest = split(value_ref[c, pl.ds(t, 1), :])
@@ -282,7 +286,7 @@
         total_ref[...] += dot_nt(left, jnp.concatenate([columns, columns], axis=1))
         return carry
 
-    lax.fori_loop(0, tiles, add_tile, 0, unroll=16)
+    lax.fori_loop(0, tiles, add_tile, 0, unroll=32)
     for c in range(4):
         for h in range(2):
             slots_ref[:, h, c, :] = total_ref[c * half : (c + 1) * half, h * lanes : (h + 1) * lanes]
@@ -298,12 +302,12 @@
         return jnp.concatenate([got_ref[i * group + j] for j in range(group)], axis=1)
 
     def beam_mask(gate):
-        return rows_equal(beams, gate // lanes)
+        return rows_equal(beams, divided(gate, lanes)[0])
 
     def collect(i, acc):
         rows = gathered(i)
         gate = rows[3:4].astype(i32)
-        gates = onehot(lanes, gate % lanes)
+        gates = onehot(lanes, divided(gate, lanes)[1])
         gate_ref[i] = gates
         mask = beam_mask(gate)
         parts = []
@@ -403,14 +407,14 @@
             value_ref[c, pl.ds(t, 1), :] = pick(mask, found[c * half : (c + 1) * half])
         return carry
 
-    lax.fori_loop(0, tiles, restore, 0, unroll=16)
+    lax.fori_loop(0, tiles, restore, 0, unroll=32)
 
     list_cells.wait()
 
     def put(t, begin, least):
         cells = cell_ref[pl.ds(t, 1), :]
-        zs = onehot(nz, cells % nz)
-        line = cells // nz
+        line, depth = divided(cells, nz)
+        zs = onehot(nz, depth)
         mask = rows_equal(span, jnp.where(line >= least, line - begin, -1))
         heads, rests = [], []
         for c in range(3):

time: 83.8 us -> 83.3 us (level)
  no operation moved by 1% of the time
where the time goes in v5:
time: 83.3 us; the launch traced here: 83.1 us
  blocking collectives  31.9 us (38%)
  Pallas kernels  27.2 us (33%)
  starting transfers between devices  17.2 us (21%)
  other arithmetic  5.73 us (7%)
  between operations  0.99 us (1%)
    ppermute x8, starting transfers between devices, shifted(): lax.ppermute(value, axis, [(i, (i + by) % count) for i in range(count)])  17.2 us
    all_to_all x1, blocking collectives, body(): lax.all_to_all(slots.reshape(owners, 4, lanes), names, split_axis=0, conc...  16.7 us
    all_to_all x1, blocking collectives, body(): lax.all_to_all(back, names, split_axis=0, concat_axis=0, tiled=True)  15.3 us
    pallas_call x1, Pallas kernels, call_sample(): pl.pallas_call(sample_kernel, name='sample', in_specs=[hbm, vmem, vmem, v...  11.3 us
    sort x1, other arithmetic, body(): lax.sort((sample_cell.reshape(-1), sample_owner.reshape(-1), sample_gate....  5.73 us
    pallas_call x1, Pallas kernels, call_scatter(): pl.pallas_call(scatter_kernel, name='scatter', in_specs=[vmem, vmem, vmem...  5.13 us
    pallas_call x1, Pallas kernels, call_adjoint(): pl.pallas_call(adjoint_kernel, name='adjoint', in_specs=[vmem] * 4, out_s...  4.79 us
    pallas_call x1, Pallas kernels, call_owner(): pl.pallas_call(owner_kernel, name='owner', in_specs=[smem, vmem, vmem, vm...  3.59 us
  transfers between devices with their start and end apart: 8, of which 0 were waited for; matrix products, arithmetic and copies ran while one was open for 7% of the time, Pallas kernels for 6%

profile of v5, /device:TPU:0, one launch (start us, length us, event | category | flops | bytes accessed | tf_op | source)
XLA Modules:
  0.0 83.1 jit_solution(7171640562879006268)
XLA Ops:
  0.6 0.0 copy-start.5
  0.6 0.0 copy-start.3
  0.7 0.0 copy-start.4
  0.7 1.3 %border.1 = (f32[3,64,256]{2,1,0:T(8,128)S(1)}, f32[3,64,256]{2,1,0:T(8,128)S(1)}, f32[3,16,256]{2,1,0:T(8,128)S(1)}, f32[3,16,256]{2,1,0:T(8,128)S(1)}) custom-call(f32[3,16,64,256]{3,2,1,0:T(8,128)} %field_hbm.3), custom_call_target="tpu_custom_call" | custom-call | tf_op jit(solution)/shard_map/border/pallas_call | solution.py:577
  1.9 0.0 collective-permute-start
  2.0 3.6 %collective-permute-start.1 = (f32[3,64,256]{2,1,0:T(8,128)S(1)}, f32[3,64,256]{2,1,0:T(8,128)S(1)}, u32[]{:S(2)}, u32[]{:S(2)}) collective-permute-start(f32[3,64,256]{2,1,0:T(8,128)S(1)} %get-tuple-element.27), channel_id=1, source_target_pairs={{0,112},{16,0},{32,16},{48,32},{64,48},{80,64},{96,80},{112,96},{1... | collective-permute-start | bytes 589832 | tf_op jit(solution)/shard_map/ppermute | solution.py:559
  5.5 1.5 %collective-permute-start.2 = (f32[3,16,256]{2,1,0:T(8,128)S(1)}, f32[3,16,256]{2,1,0:T(8,128)S(1)}, u32[]{:S(2)}, u32[]{:S(2)}) collective-permute-start(f32[3,16,256]{2,1,0:T(8,128)S(1)} %get-tuple-element.28), channel_id=1, source_target_pairs={{0,1},{1,2},{2,3},{3,4},{4,5},{5,6},{6,7},{7,8},{8,9},{9,10},{10,1... | collective-permute-start | bytes 147464 | tf_op jit(solution)/shard_map/ppermute | solution.py:559
  7.0 3.9 %collective-permute-start.3 = (f32[3,16,256]{2,1,0:T(8,128)S(1)}, f32[3,16,256]{2,1,0:T(8,128)S(1)}, u32[]{:S(2)}, u32[]{:S(2)}) collective-permute-start(f32[3,16,256]{2,1,0:T(8,128)S(1)} %get-tuple-element.29), channel_id=1, source_target_pairs={{0,15},{1,0},{2,1},{3,2},{4,3},{5,4},{6,5},{7,6},{8,7},{9,8},{10,9... | collective-permute-start | bytes 147464 | tf_op jit(solution)/shard_map/ppermute | solution.py:559
  10.9 0.0 copy-done.5
  10.9 0.0 copy-done.3
  10.9 0.0 copy-done.4
  10.9 5.7 %sort.21 = (s32[8192]{0:T(1024)S(1)}, s32[8192]{0:T(1024)S(1)}, s32[8192]{0:T(1024)S(1)}) sort(s32[8192]{0:T(1024)S(1)} %bitcast.7, s32[8192]{0:T(1024)S(1)} %bitcast.8, s32[8192]{0:T(1024)S(1)} %bitcast.9), dimensions={0}, to_apply=%region_0.0 | sort | flops 106496 | bytes 196608 | tf_op jit(solution)/shard_map/sort | solution.py:729
  16.7 0.0 copy-start
  16.7 0.0 copy-start.1
  16.7 0.0 copy-start.2
  16.7 0.0 collective-permute-done.2.ylo_ref
  16.7 0.0 collective-permute-done.3.yhi_ref
  16.8 0.0 collective-permute-done.xlo_ref
  16.8 0.0 collective-permute-done.1.xhi_ref
  16.8 11.3 %sample.1 = (f32[64,2,4,128]{3,2,1,0:T(4,128)S(1)}, s32[32,256]{1,0:T(8,128)S(1)}) custom-call(f32[3,16,64,256]{3,2,1,0:T(8,128)} %field_hbm.3, f32[3,64,256]{2,1,0:T(8,128)S(1)} %collective-permute-done.xlo_ref, f32[3,64,256]{2,1,0:T(8,128)S(1)} %collective-permute-done.1.xhi_ref, f32[3,16,256]{2,1,0:T(8,128)S(1)} %collective-permute-done.2.ylo_ref, ...), custom_call_target="tpu_custom_call" | custom-call | tf_op jit(solution)/shard_map/sample/pallas_call | solution.py:600
  28.1 16.7 %all_to_all.10.got_ref = f32[128,4,128]{2,1,0:T(4,128)S(1)} all-to-all(f32[128,4,128]{2,1,0:T(4,128)S(1)} %bitcast.6), channel_id=1, replica_groups=mesh['track'=8,'cross'=16] {'track','cross'}, dimensions={0} | all-to-all | bytes 524288 | tf_op jit(solution)/shard_map/all_to_all | solution.py:734
  44.8 0.0 copy-done
  44.8 0.0 copy-done.1
  44.8 0.0 copy-done.2
  44.8 3.6 %owner.1 = (f32[128,4,128]{2,1,0:T(4,128)S(1)}, f32[1,1024]{1,0:T(1,128)}) custom-call(s32[1,8]{1,0:T(1,128)S(1)} %copy-done.2, f32[128,4,128]{2,1,0:T(4,128)S(1)} %all_to_all.10.got_ref, f32[3,1,1024]{2,1,0:T(1,128)S(1)} %copy-done.1, f32[1,128,128]{2,1,0:T(8,128)S(1)} %copy-done), custom_call_target="tpu_custom_call" | custom-call | tf_op jit(solution)/shard_map/owner/pallas_call | solution.py:629
  48.4 15.3 %all_to_all.11 = f32[128,4,128]{2,1,0:T(4,128)S(1)} all-to-all(f32[128,4,128]{2,1,0:T(4,128)S(1)} %get-tuple-element.34), channel_id=1, replica_groups=mesh['track'=8,'cross'=16] {'track','cross'}, dimensions={0} | all-to-all | bytes 524288 | tf_op jit(solution)/shard_map/all_to_all | solution.py:736
  63.6 5.1 %scatter.1 = (f32[3,1024,256]{2,1,0:T(8,128)S(1)}, f32[3,16,64,256]{3,2,1,0:T(8,128)S(1)}, f32[9,16,64,256]{3,2,1,0:T(8,128)S(1)}, f32[16,64,256]{2,1,0:T(8,128)...) custom-call(f32[64,2,4,128]{3,2,1,0:T(4,128)S(1)} %bitcast.5, ...), custom_call_target="tpu_custom_call" | custom-call | tf_op jit(solution)/shard_map/scatter/pallas_call | solution.py:647
  68.8 0.0 collective-permute-start.4
  68.8 2.9 %collective-permute-start.5 = (f32[3,64,256]{2,1,0:T(8,128)S(1)}, f32[3,64,256]{2,1,0:T(8,128)S(1)}, u32[]{:S(2)}, u32[]{:S(2)}) collective-permute-start(f32[3,64,256]{2,1,0:T(8,128)S(1)} %get-tuple-element.46), channel_id=1, source_target_pairs={{0,112},{16,0},{32,16},{48,32},{64,48},{80,64},{96,80},{112,96},{1... | collective-permute-start | bytes 589832 | tf_op jit(solution)/shard_map/ppermute | solution.py:559
  71.7 0.6 collective-permute-start.6
  72.3 4.7 %collective-permute-start.7 = (f32[3,16,256]{2,1,0:T(8,128)S(1)}, f32[3,16,256]{2,1,0:T(8,128)S(1)}, u32[]{:S(2)}, u32[]{:S(2)}) collective-permute-start(f32[3,16,256]{2,1,0:T(8,128)S(1)} %get-tuple-element.48), channel_id=1, source_target_pairs={{0,15},{1,0},{2,1},{3,2},{4,3},{5,4},{6,5},{7,6},{8,7},{9,8},{10,9... | collective-permute-start | bytes 147464 | tf_op jit(solution)/shard_map/ppermute | solution.py:559
  77.1 4.8 %adjoint.1 = (f32[3,16,64,256]{3,2,1,0:T(8,128)}, f32[3,64,256]{2,1,0:T(8,128)S(1)}, f32[3,64,256]{2,1,0:T(8,128)S(1)}, f32[3,14,8,256]{3,2,1,0:T(8,128)S(1)}, f32[3,14,8,256]{3,2,1,0:T(8,128)S(1)}) custom-call(f32[3,1024,256]{2,1,0:T(8,128)S(1)} %get-tuple-element.36.plane_ref, f32[3,16,64,256]{3,2,1,0:T(8,128)S(1)} %get-tuple-element.37.wind_ref, ...), custom_call_target="tpu_custom_call" | custom-call | tf_op jit(solution)/shard_map/adjoint/pallas_call | solution.py:680
  81.9 0.0 collective-permute-done.6.ylo_ref
  81.9 0.0 collective-permute-done.7.yhi_ref
  81.9 0.0 collective-permute-done.4.xlo_ref
  81.9 0.0 collective-permute-done.5.xhi_ref
  81.9 1.1 %edges.1 = f32[3,16,64,256]{3,2,1,0:T(8,128)} custom-call(f32[3,16,64,256]{3,2,1,0:T(8,128)} %get-tuple-element.40.given_ref, f32[3,64,256]{2,1,0:T(8,128)S(1)} %get-tuple-element.41.low_ref, f32[3,64,256]{2,1,0:T(8,128)S(1)} %get-tuple-element.42.high_ref, f32[3,14,8,256]{3,2,1,0:T(8,128)S(1)} %get-tuple-element.43.left_ref, ...), custom_call_target="tpu_custom_call", output_to_operand_aliasing={{}: (0, {})} | custom-call | tf_op jit(solution)/shard_map/edges/pallas_call | solution.py:693
  (3 shorter events, 0.0 us)
Async XLA Ops:
  0.6 10.3 %copy-start.5 = (s32[1,1,8192]{2,1,0:T(1,128)S(1)}, s32[1,1,8192]{2,1,0:T(1,128)}, u32[]{:S(2)}) copy-start(s32[1,1,8192]{2,1,0:T(1,128)} %param.16) | copy-start | bytes 98308
  0.6 10.3 %copy-start.3 = (s32[1,1,8192]{2,1,0:T(1,128)S(1)}, s32[1,1,8192]{2,1,0:T(1,128)}, u32[]{:S(2)}) copy-start(s32[1,1,8192]{2,1,0:T(1,128)} %param.15) | copy-start | bytes 98308
  0.7 10.3 %copy-start.4 = (s32[1,1,8192,1]{2,3,1,0:T(1,128)S(1)}, s32[1,1,8192,1]{2,3,1,0:T(1,128)}, u32[]{:S(2)}) copy-start(s32[1,1,8192,1]{2,3,1,0:T(1,128)} %param.14) | copy-start | bytes 98308
  1.9 14.8 %collective-permute-start = (f32[3,64,256]{2,1,0:T(8,128)S(1)}, f32[3,64,256]{2,1,0:T(8,128)S(1)}, u32[]{:S(2)}, u32[]{:S(2)}) collective-permute-start(f32[3,64,256]{2,1,0:T(8,128)S(1)} %get-tuple-element.26), channel_id=1, source_target_pairs={{0,16},{16,32},{32,48},{48,64},{64,80},{80,96},{96,112},{112,0},{1... | collective-permute-start | bytes 589832 | tf_op jit(solution)/shard_map/ppermute | solution.py:559
  2.0 14.8 %collective-permute-start.1 = (f32[3,64,256]{2,1,0:T(8,128)S(1)}, f32[3,64,256]{2,1,0:T(8,128)S(1)}, u32[]{:S(2)}, u32[]{:S(2)}) collective-permute-start(f32[3,64,256]{2,1,0:T(8,128)S(1)} %get-tuple-element.27), channel_id=1, source_target_pairs={{0,112},{16,0},{32,16},{48,32},{64,48},{80,64},{96,80},{112,96},{1... | collective-permute-start | bytes 589832 | tf_op jit(solution)/shard_map/ppermute | solution.py:559
  5.5 11.2 %collective-permute-start.2 = (f32[3,16,256]{2,1,0:T(8,128)S(1)}, f32[3,16,256]{2,1,0:T(8,128)S(1)}, u32[]{:S(2)}, u32[]{:S(2)}) collective-permute-start(f32[3,16,256]{2,1,0:T(8,128)S(1)} %get-tuple-element.28), channel_id=1, source_target_pairs={{0,1},{1,2},{2,3},{3,4},{4,5},{5,6},{6,7},{7,8},{8,9},{9,10},{10,1... | collective-permute-start | bytes 147464 | tf_op jit(solution)/shard_map/ppermute | solution.py:559
  7.0 9.7 %collective-permute-start.3 = (f32[3,16,256]{2,1,0:T(8,128)S(1)}, f32[3,16,256]{2,1,0:T(8,128)S(1)}, u32[]{:S(2)}, u32[]{:S(2)}) collective-permute-start(f32[3,16,256]{2,1,0:T(8,128)S(1)} %get-tuple-element.29), channel_id=1, source_target_pairs={{0,15},{1,0},{2,1},{3,2},{4,3},{5,4},{6,5},{7,6},{8,7},{9,8},{10,9... | collective-permute-start | bytes 147464 | tf_op jit(solution)/shard_map/ppermute | solution.py:559
  16.7 28.1 %copy-start = (f32[1,128,128]{2,1,0:T(8,128)S(1)}, f32[1,128,128]{2,1,0:T(8,128)}, u32[]{:S(2)}) copy-start(f32[1,128,128]{2,1,0:T(8,128)} %precision_ref.1) | copy-start | bytes 196612
  16.7 28.1 %copy-start.1 = (f32[3,1,1024]{2,1,0:T(1,128)S(1)}, f32[3,1,1024]{2,1,0:T(1,128)}, u32[]{:S(2)}) copy-start(f32[3,1,1024]{2,1,0:T(1,128)} %sight_ref.1) | copy-start | bytes 36868
  16.7 28.1 %copy-start.2 = (s32[1,8]{1,0:T(1,128)S(1)}, s32[1,8]{1,0:T(1,128)}, u32[]{:S(2)}) copy-start(s32[1,8]{1,0:T(1,128)} %counts_s.1) | copy-start | bytes 100
  68.8 13.1 %collective-permute-start.4 = (f32[3,64,256]{2,1,0:T(8,128)S(1)}, f32[3,64,256]{2,1,0:T(8,128)S(1)}, u32[]{:S(2)}, u32[]{:S(2)}) collective-permute-start(f32[3,64,256]{2,1,0:T(8,128)S(1)} %get-tuple-element.45), channel_id=1, source_target_pairs={{0,16},{16,32},{32,48},{48,64},{64,80},{80,96},{96,112},{112,0},{1... | collective-permute-start | bytes 589832 | tf_op jit(solution)/shard_map/ppermute | solution.py:559
  68.8 13.1 %collective-permute-start.5 = (f32[3,64,256]{2,1,0:T(8,128)S(1)}, f32[3,64,256]{2,1,0:T(8,128)S(1)}, u32[]{:S(2)}, u32[]{:S(2)}) collective-permute-start(f32[3,64,256]{2,1,0:T(8,128)S(1)} %get-tuple-element.46), channel_id=1, source_target_pairs={{0,112},{16,0},{32,16},{48,32},{64,48},{80,64},{96,80},{112,96},{1... | collective-permute-start | bytes 589832 | tf_op jit(solution)/shard_map/ppermute | solution.py:559
  71.7 10.1 %collective-permute-start.6 = (f32[3,16,256]{2,1,0:T(8,128)S(1)}, f32[3,16,256]{2,1,0:T(8,128)S(1)}, u32[]{:S(2)}, u32[]{:S(2)}) collective-permute-start(f32[3,16,256]{2,1,0:T(8,128)S(1)} %get-tuple-element.47), channel_id=1, source_target_pairs={{0,1},{1,2},{2,3},{3,4},{4,5},{5,6},{6,7},{7,8},{8,9},{9,10},{10,1... | collective-permute-start | bytes 147464 | tf_op jit(solution)/shard_map/ppermute | solution.py:559
  72.3 9.6 %collective-permute-start.7 = (f32[3,16,256]{2,1,0:T(8,128)S(1)}, f32[3,16,256]{2,1,0:T(8,128)S(1)}, u32[]{:S(2)}, u32[]{:S(2)}) collective-permute-start(f32[3,16,256]{2,1,0:T(8,128)S(1)} %get-tuple-element.48), channel_id=1, source_target_pairs={{0,15},{1,0},{2,1},{3,2},{4,3},{5,4},{6,5},{7,6},{8,7},{9,8},{10,9... | collective-permute-start | bytes 147464 | tf_op jit(solution)/shard_map/ppermute | solution.py:559

commit v6 on v5

--- a/solution.py
+++ b/solution.py
@@ -148,7 +148,7 @@
 ):
     nx, cy, nz = visc_ref.shape
     tiles = cell_ref.shape[0]
-    owners = 2 * slots_ref.shape[0]
+    owners = 2 * slots_ref.shape[1]
     rows = nx * cy
 
     def copies(k):
@@ -184,7 +184,8 @@
         counts = dot_nn(ones_at(mask), upper_ref[...])
         offset = offset_ref[...]
         ranks = pick(mask, counts + jnp.concatenate([offset] * (tile // lanes), axis=1))
-        slot_ref[pl.ds(t, 1), :] = own * lanes + ranks.astype(i32) - 1
+        high, line = divided(own, owners // 2)
+        slot_ref[pl.ds(t, 1), :] = (2 * line + high) * lanes + ranks.astype(i32) - 1
         offset_ref[...] = offset + jnp.broadcast_to(counts[:, tile - 1 : tile], offset.shape)
         return carry
 
@@ -289,7 +290,7 @@
     lax.fori_loop(0, tiles, add_tile, 0, unroll=32)
     for c in range(4):
         for h in range(2):
-            slots_ref[:, h, c, :] = total_ref[c * half : (c + 1) * half, h * lanes : (h + 1) * lanes]
+            slots_ref[h, :, c, :] = total_ref[c * half : (c + 1) * half, h * lanes : (h + 1) * lanes]
 
 
 def owner_kernel(counts_s, got_ref, sight_ref, precision_ref, back_ref, weighted_ref, gate_ref):
@@ -346,11 +347,10 @@
         gates = gate_ref[i]
         found = dot_nn(table, gates)
         found = found[: 3 * beams] + found[3 * beams :]
-        rows = jnp.concatenate(
-            [pick(mask, found[k * beams : (k + 1) * beams]) for k in range(3)] + [jnp.zeros((1, wide), f32)], axis=0
-        )
-        for j in range(group):
-            back_ref[i * group + j] = rows[:, j * lanes : (j + 1) * lanes]
+        for k in range(3):
+            row = pick(mask, found[k * beams : (k + 1) * beams])
+            for j in range(group):
+                back_ref[i * group + j, :, k * lanes : (k + 1) * lanes] = row[:, j * lanes : (j + 1) * lanes]
         return carry
 
     lax.fori_loop(0, sources // group, give, 0, unroll=8)
@@ -379,7 +379,7 @@
 ):
     nx, cy, nz = visc_hbm.shape
     tiles = cell_ref.shape[0]
-    half = back_ref.shape[0]
+    half = back_ref.shape[0] // 2
     rows = nx * cy
     list_cells = pltpu.make_async_copy(cell_ref, cell_s, cell_sem)
     list_cells.start()
@@ -392,7 +392,7 @@
         copy.start()
     for c in range(3):
         for h in range(2):
-            head, rest = split(back_ref[:, h, c, :])
+            head, rest = split(back_ref[h * half : (h + 1) * half, 0, c * lanes : (c + 1) * lanes])
             table_ref[c * half : (c + 1) * half, h * lanes : (h + 1) * lanes] = head
             table_ref[(3 + c) * half : (4 + c) * half, h * lanes : (h + 1) * lanes] = rest
     plane_ref[...] = jnp.zeros_like(plane_ref)
@@ -617,7 +617,7 @@
             pltpu.SemaphoreType.DMA,
         ],
         out_shape=[
-            jax.ShapeDtypeStruct((owners // 2, 2, 4, lanes), f32),
+            jax.ShapeDtypeStruct((2, owners // 2, 4, lanes), f32),
             jax.ShapeDtypeStruct((tiles, tile), i32),
         ],
         compiler_params=room(40),
@@ -633,7 +633,7 @@
         out_specs=[vmem, vmem],
         scratch_shapes=[pltpu.VMEM((owners // 8, lanes, 8 * lanes), bf16)],
         out_shape=[
-            jax.ShapeDtypeStruct((owners, 4, lanes), f32),
+            jax.ShapeDtypeStruct((owners, 1, 3 * lanes), f32),
             jax.ShapeDtypeStruct((1, sight.shape[2]), f32),
         ],
         compiler_params=room(24),
@@ -643,7 +643,7 @@
 def call_scatter(returned, cells, slot, wind, wind_gradient, viscosity):
     _, cx, cy, nz = wind.shape
     tiles = cells.shape[0]
-    half = returned.shape[0]
+    half = returned.shape[0] // 2
     return pl.pallas_call(
         scatter_kernel,
         name="scatter",
@@ -734,7 +734,6 @@
     got = lax.all_to_all(slots.reshape(owners, 4, lanes), names, split_axis=0, concat_axis=0, tiled=True)
     back, weighted = call_owner(gate_counts, got, sight, precision)
     returned = lax.all_to_all(back, names, split_axis=0, concat_axis=0, tiled=True)
-    returned = returned.reshape(owners // 2, 2, 4, lanes)
     *taken, xlo, xhi, ylo, yhi = call_scatter(returned, cells, slot, wind, wind_gradient, viscosity)
     halo = (
         shifted(xhi, "track", 1),

time: 83.3 us -> 82.6 us (level)
  no operation moved by 1% of the time
where the time goes in v6:
time: 82.6 us; the launch traced here: 82.5 us
  blocking collectives  31.2 us (38%)
  Pallas kernels  27.2 us (33%)
  starting transfers between devices  17.2 us (21%)
  other arithmetic  5.73 us (7%)
  between operations  0.99 us (1%)
    ppermute x8, starting transfers between devices, shifted(): lax.ppermute(value, axis, [(i, (i + by) % count) for i in range(count)])  17.2 us
    all_to_all x1, blocking collectives, body(): lax.all_to_all(slots.reshape(owners, 4, lanes), names, split_axis=0, conc...  16.7 us
    all_to_all x1, blocking collectives, body(): lax.all_to_all(back, names, split_axis=0, concat_axis=0, tiled=True)  14.6 us
    pallas_call x1, Pallas kernels, call_sample(): pl.pallas_call(sample_kernel, name='sample', in_specs=[hbm, vmem, vmem, v...  11.3 us
    sort x1, other arithmetic, body(): lax.sort((sample_cell.reshape(-1), sample_owner.reshape(-1), sample_gate....  5.73 us
    pallas_call x1, Pallas kernels, call_scatter(): pl.pallas_call(scatter_kernel, name='scatter', in_specs=[vmem, vmem, vmem...  5.13 us
    pallas_call x1, Pallas kernels, call_adjoint(): pl.pallas_call(adjoint_kernel, name='adjoint', in_specs=[vmem] * 4, out_s...  4.79 us
    pallas_call x1, Pallas kernels, call_owner(): pl.pallas_call(owner_kernel, name='owner', in_specs=[smem, vmem, vmem, vm...  3.58 us
  transfers between devices with their start and end apart: 8, of which 0 were waited for; matrix products, arithmetic and copies ran while one was open for 7% of the time, Pallas kernels for 6%

profile of v6, /device:TPU:0, one launch (start us, length us, event | category | flops | bytes accessed | tf_op | source)
XLA Modules:
  0.0 82.5 jit_solution(392851073340397144)
XLA Ops:
  0.6 0.0 copy-start.5
  0.6 0.0 copy-start.3
  0.7 0.0 copy-start.4
  0.7 1.3 %border.1 = (f32[3,64,256]{2,1,0:T(8,128)S(1)}, f32[3,64,256]{2,1,0:T(8,128)S(1)}, f32[3,16,256]{2,1,0:T(8,128)S(1)}, f32[3,16,256]{2,1,0:T(8,128)S(1)}) custom-call(f32[3,16,64,256]{3,2,1,0:T(8,128)} %field_hbm.3), custom_call_target="tpu_custom_call" | custom-call | tf_op jit(solution)/shard_map/border/pallas_call | solution.py:577
  1.9 0.0 collective-permute-start
  2.0 3.6 %collective-permute-start.1 = (f32[3,64,256]{2,1,0:T(8,128)S(1)}, f32[3,64,256]{2,1,0:T(8,128)S(1)}, u32[]{:S(2)}, u32[]{:S(2)}) collective-permute-start(f32[3,64,256]{2,1,0:T(8,128)S(1)} %get-tuple-element.27), channel_id=1, source_target_pairs={{0,112},{16,0},{32,16},{48,32},{64,48},{80,64},{96,80},{112,96},{1... | collective-permute-start | bytes 589832 | tf_op jit(solution)/shard_map/ppermute | solution.py:559
  5.5 1.5 %collective-permute-start.2 = (f32[3,16,256]{2,1,0:T(8,128)S(1)}, f32[3,16,256]{2,1,0:T(8,128)S(1)}, u32[]{:S(2)}, u32[]{:S(2)}) collective-permute-start(f32[3,16,256]{2,1,0:T(8,128)S(1)} %get-tuple-element.28), channel_id=1, source_target_pairs={{0,1},{1,2},{2,3},{3,4},{4,5},{5,6},{6,7},{7,8},{8,9},{9,10},{10,1... | collective-permute-start | bytes 147464 | tf_op jit(solution)/shard_map/ppermute | solution.py:559
  7.0 3.9 %collective-permute-start.3 = (f32[3,16,256]{2,1,0:T(8,128)S(1)}, f32[3,16,256]{2,1,0:T(8,128)S(1)}, u32[]{:S(2)}, u32[]{:S(2)}) collective-permute-start(f32[3,16,256]{2,1,0:T(8,128)S(1)} %get-tuple-element.29), channel_id=1, source_target_pairs={{0,15},{1,0},{2,1},{3,2},{4,3},{5,4},{6,5},{7,6},{8,7},{9,8},{10,9... | collective-permute-start | bytes 147464 | tf_op jit(solution)/shard_map/ppermute | solution.py:559
  10.9 0.0 copy-done.5
  10.9 0.0 copy-done.3
  10.9 0.0 copy-done.4
  10.9 5.7 %sort.21 = (s32[8192]{0:T(1024)S(1)}, s32[8192]{0:T(1024)S(1)}, s32[8192]{0:T(1024)S(1)}) sort(s32[8192]{0:T(1024)S(1)} %bitcast.5, s32[8192]{0:T(1024)S(1)} %bitcast.6, s32[8192]{0:T(1024)S(1)} %bitcast.7), dimensions={0}, to_apply=%region_0.0 | sort | flops 106496 | bytes 196608 | tf_op jit(solution)/shard_map/sort | solution.py:729
  16.7 0.0 copy-start
  16.7 0.0 copy-start.1
  16.7 0.0 copy-start.2
  16.7 0.0 collective-permute-done.2.ylo_ref
  16.7 0.0 collective-permute-done.3.yhi_ref
  16.8 0.0 collective-permute-done.xlo_ref
  16.8 0.0 collective-permute-done.1.xhi_ref
  16.8 11.3 %sample.1 = (f32[2,64,4,128]{3,2,1,0:T(4,128)S(1)}, s32[32,256]{1,0:T(8,128)S(1)}) custom-call(f32[3,16,64,256]{3,2,1,0:T(8,128)} %field_hbm.3, f32[3,64,256]{2,1,0:T(8,128)S(1)} %collective-permute-done.xlo_ref, f32[3,64,256]{2,1,0:T(8,128)S(1)} %collective-permute-done.1.xhi_ref, f32[3,16,256]{2,1,0:T(8,128)S(1)} %collective-permute-done.2.ylo_ref, ...), custom_call_target="tpu_custom_call" | custom-call | tf_op jit(solution)/shard_map/sample/pallas_call | solution.py:600
  28.1 16.7 %all_to_all.10.got_ref = f32[128,4,128]{2,1,0:T(4,128)S(1)} all-to-all(f32[128,4,128]{2,1,0:T(4,128)S(1)} %bitcast.4), channel_id=1, replica_groups=mesh['track'=8,'cross'=16] {'track','cross'}, dimensions={0} | all-to-all | bytes 524288 | tf_op jit(solution)/shard_map/all_to_all | solution.py:734
  44.8 0.0 copy-done
  44.8 0.0 copy-done.1
  44.8 0.0 copy-done.2
  44.8 3.6 %owner.1 = (f32[128,1,384]{2,1,0:T(1,128)S(1)}, f32[1,1024]{1,0:T(1,128)}) custom-call(s32[1,8]{1,0:T(1,128)S(1)} %copy-done.2, f32[128,4,128]{2,1,0:T(4,128)S(1)} %all_to_all.10.got_ref, f32[3,1,1024]{2,1,0:T(1,128)S(1)} %copy-done.1, f32[1,128,128]{2,1,0:T(8,128)S(1)} %copy-done), custom_call_target="tpu_custom_call" | custom-call | tf_op jit(solution)/shard_map/owner/pallas_call | solution.py:629
  48.4 14.6 %all_to_all.11.back_ref = f32[128,1,384]{2,1,0:T(1,128)S(1)} all-to-all(f32[128,1,384]{2,1,0:T(1,128)S(1)} %get-tuple-element.34), channel_id=1, replica_groups=mesh['track'=8,'cross'=16] {'track','cross'}, dimensions={0} | all-to-all | bytes 393216 | tf_op jit(solution)/shard_map/all_to_all | solution.py:736
  63.0 5.1 %scatter.1 = (f32[3,1024,256]{2,1,0:T(8,128)S(1)}, f32[3,16,64,256]{3,2,1,0:T(8,128)S(1)}, f32[9,16,64,256]{3,2,1,0:T(8,128)S(1)}, f32[16,64,256]{2,1,0:T(8,128)...) custom-call(f32[128,1,384]{2,1,0:T(1,128)S(1)} %all_to_all.11.back_r, ...), custom_call_target="tpu_custom_call" | custom-call | tf_op jit(solution)/shard_map/scatter/pallas_call | solution.py:647
  68.1 0.0 collective-permute-start.4
  68.1 2.9 %collective-permute-start.5 = (f32[3,64,256]{2,1,0:T(8,128)S(1)}, f32[3,64,256]{2,1,0:T(8,128)S(1)}, u32[]{:S(2)}, u32[]{:S(2)}) collective-permute-start(f32[3,64,256]{2,1,0:T(8,128)S(1)} %get-tuple-element.46), channel_id=1, source_target_pairs={{0,112},{16,0},{32,16},{48,32},{64,48},{80,64},{96,80},{112,96},{1... | collective-permute-start | bytes 589832 | tf_op jit(solution)/shard_map/ppermute | solution.py:559
  71.1 0.6 collective-permute-start.6
  71.7 4.7 %collective-permute-start.7 = (f32[3,16,256]{2,1,0:T(8,128)S(1)}, f32[3,16,256]{2,1,0:T(8,128)S(1)}, u32[]{:S(2)}, u32[]{:S(2)}) collective-permute-start(f32[3,16,256]{2,1,0:T(8,128)S(1)} %get-tuple-element.48), channel_id=1, source_target_pairs={{0,15},{1,0},{2,1},{3,2},{4,3},{5,4},{6,5},{7,6},{8,7},{9,8},{10,9... | collective-permute-start | bytes 147464 | tf_op jit(solution)/shard_map/ppermute | solution.py:559
  76.4 4.8 %adjoint.1 = (f32[3,16,64,256]{3,2,1,0:T(8,128)}, f32[3,64,256]{2,1,0:T(8,128)S(1)}, f32[3,64,256]{2,1,0:T(8,128)S(1)}, f32[3,14,8,256]{3,2,1,0:T(8,128)S(1)}, f32[3,14,8,256]{3,2,1,0:T(8,128)S(1)}) custom-call(f32[3,1024,256]{2,1,0:T(8,128)S(1)} %get-tuple-element.36.plane_ref, f32[3,16,64,256]{3,2,1,0:T(8,128)S(1)} %get-tuple-element.37.wind_ref, ...), custom_call_target="tpu_custom_call" | custom-call | tf_op jit(solution)/shard_map/adjoint/pallas_call | solution.py:680
  81.2 0.0 collective-permute-done.6.ylo_ref
  81.2 0.0 collective-permute-done.7.yhi_ref
  81.2 0.0 collective-permute-done.4.xlo_ref
  81.2 0.0 collective-permute-done.5.xhi_ref
  81.2 1.1 %edges.1 = f32[3,16,64,256]{3,2,1,0:T(8,128)} custom-call(f32[3,16,64,256]{3,2,1,0:T(8,128)} %get-tuple-element.40.given_ref, f32[3,64,256]{2,1,0:T(8,128)S(1)} %get-tuple-element.41.low_ref, f32[3,64,256]{2,1,0:T(8,128)S(1)} %get-tuple-element.42.high_ref, f32[3,14,8,256]{3,2,1,0:T(8,128)S(1)} %get-tuple-element.43.left_ref, ...), custom_call_target="tpu_custom_call", output_to_operand_aliasing={{}: (0, {})} | custom-call | tf_op jit(solution)/shard_map/edges/pallas_call | solution.py:693
  (3 shorter events, 0.0 us)
Async XLA Ops:
  0.6 10.3 %copy-start.5 = (s32[1,1,8192]{2,1,0:T(1,128)S(1)}, s32[1,1,8192]{2,1,0:T(1,128)}, u32[]{:S(2)}) copy-start(s32[1,1,8192]{2,1,0:T(1,128)} %param.16) | copy-start | bytes 98308
  0.6 10.3 %copy-start.3 = (s32[1,1,8192]{2,1,0:T(1,128)S(1)}, s32[1,1,8192]{2,1,0:T(1,128)}, u32[]{:S(2)}) copy-start(s32[1,1,8192]{2,1,0:T(1,128)} %param.15) | copy-start | bytes 98308
  0.7 10.3 %copy-start.4 = (s32[1,1,8192,1]{2,3,1,0:T(1,128)S(1)}, s32[1,1,8192,1]{2,3,1,0:T(1,128)}, u32[]{:S(2)}) copy-start(s32[1,1,8192,1]{2,3,1,0:T(1,128)} %param.14) | copy-start | bytes 98308
  1.9 14.8 %collective-permute-start = (f32[3,64,256]{2,1,0:T(8,128)S(1)}, f32[3,64,256]{2,1,0:T(8,128)S(1)}, u32[]{:S(2)}, u32[]{:S(2)}) collective-permute-start(f32[3,64,256]{2,1,0:T(8,128)S(1)} %get-tuple-element.26), channel_id=1, source_target_pairs={{0,16},{16,32},{32,48},{48,64},{64,80},{80,96},{96,112},{112,0},{1... | collective-permute-start | bytes 589832 | tf_op jit(solution)/shard_map/ppermute | solution.py:559
  2.0 14.8 %collective-permute-start.1 = (f32[3,64,256]{2,1,0:T(8,128)S(1)}, f32[3,64,256]{2,1,0:T(8,128)S(1)}, u32[]{:S(2)}, u32[]{:S(2)}) collective-permute-start(f32[3,64,256]{2,1,0:T(8,128)S(1)} %get-tuple-element.27), channel_id=1, source_target_pairs={{0,112},{16,0},{32,16},{48,32},{64,48},{80,64},{96,80},{112,96},{1... | collective-permute-start | bytes 589832 | tf_op jit(solution)/shard_map/ppermute | solution.py:559
  5.5 11.2 %collective-permute-start.2 = (f32[3,16,256]{2,1,0:T(8,128)S(1)}, f32[3,16,256]{2,1,0:T(8,128)S(1)}, u32[]{:S(2)}, u32[]{:S(2)}) collective-permute-start(f32[3,16,256]{2,1,0:T(8,128)S(1)} %get-tuple-element.28), channel_id=1, source_target_pairs={{0,1},{1,2},{2,3},{3,4},{4,5},{5,6},{6,7},{7,8},{8,9},{9,10},{10,1... | collective-permute-start | bytes 147464 | tf_op jit(solution)/shard_map/ppermute | solution.py:559
  7.0 9.7 %collective-permute-start.3 = (f32[3,16,256]{2,1,0:T(8,128)S(1)}, f32[3,16,256]{2,1,0:T(8,128)S(1)}, u32[]{:S(2)}, u32[]{:S(2)}) collective-permute-start(f32[3,16,256]{2,1,0:T(8,128)S(1)} %get-tuple-element.29), channel_id=1, source_target_pairs={{0,15},{1,0},{2,1},{3,2},{4,3},{5,4},{6,5},{7,6},{8,7},{9,8},{10,9... | collective-permute-start | bytes 147464 | tf_op jit(solution)/shard_map/ppermute | solution.py:559
  16.7 28.1 %copy-start = (f32[1,128,128]{2,1,0:T(8,128)S(1)}, f32[1,128,128]{2,1,0:T(8,128)}, u32[]{:S(2)}) copy-start(f32[1,128,128]{2,1,0:T(8,128)} %precision_ref.1) | copy-start | bytes 196612
  16.7 28.1 %copy-start.1 = (f32[3,1,1024]{2,1,0:T(1,128)S(1)}, f32[3,1,1024]{2,1,0:T(1,128)}, u32[]{:S(2)}) copy-start(f32[3,1,1024]{2,1,0:T(1,128)} %sight_ref.1) | copy-start | bytes 36868
  16.7 28.1 %copy-start.2 = (s32[1,8]{1,0:T(1,128)S(1)}, s32[1,8]{1,0:T(1,128)}, u32[]{:S(2)}) copy-start(s32[1,8]{1,0:T(1,128)} %counts_s.1) | copy-start | bytes 100
  68.1 13.1 %collective-permute-start.4 = (f32[3,64,256]{2,1,0:T(8,128)S(1)}, f32[3,64,256]{2,1,0:T(8,128)S(1)}, u32[]{:S(2)}, u32[]{:S(2)}) collective-permute-start(f32[3,64,256]{2,1,0:T(8,128)S(1)} %get-tuple-element.45), channel_id=1, source_target_pairs={{0,16},{16,32},{32,48},{48,64},{64,80},{80,96},{96,112},{112,0},{1... | collective-permute-start | bytes 589832 | tf_op jit(solution)/shard_map/ppermute | solution.py:559
  68.1 13.1 %collective-permute-start.5 = (f32[3,64,256]{2,1,0:T(8,128)S(1)}, f32[3,64,256]{2,1,0:T(8,128)S(1)}, u32[]{:S(2)}, u32[]{:S(2)}) collective-permute-start(f32[3,64,256]{2,1,0:T(8,128)S(1)} %get-tuple-element.46), channel_id=1, source_target_pairs={{0,112},{16,0},{32,16},{48,32},{64,48},{80,64},{96,80},{112,96},{1... | collective-permute-start | bytes 589832 | tf_op jit(solution)/shard_map/ppermute | solution.py:559
  71.1 10.1 %collective-permute-start.6 = (f32[3,16,256]{2,1,0:T(8,128)S(1)}, f32[3,16,256]{2,1,0:T(8,128)S(1)}, u32[]{:S(2)}, u32[]{:S(2)}) collective-permute-start(f32[3,16,256]{2,1,0:T(8,128)S(1)} %get-tuple-element.47), channel_id=1, source_target_pairs={{0,1},{1,2},{2,3},{3,4},{4,5},{5,6},{6,7},{7,8},{8,9},{9,10},{10,1... | collective-permute-start | bytes 147464 | tf_op jit(solution)/shard_map/ppermute | solution.py:559
  71.7 9.6 %collective-permute-start.7 = (f32[3,16,256]{2,1,0:T(8,128)S(1)}, f32[3,16,256]{2,1,0:T(8,128)S(1)}, u32[]{:S(2)}, u32[]{:S(2)}) collective-permute-start(f32[3,16,256]{2,1,0:T(8,128)S(1)} %get-tuple-element.48), channel_id=1, source_target_pairs={{0,15},{1,0},{2,1},{3,2},{4,3},{5,4},{6,5},{7,6},{8,7},{9,8},{10,9... | collective-permute-start | bytes 147464 | tf_op jit(solution)/shard_map/ppermute | solution.py:559
